TPU v7x, 512 devices: a whole 4x8x8 slice. The times are simulated.
512 devices in a mesh: team: 16 (over y, core), tm: 32 (over x, z).
Axes of the slice: x: 4, y: 8, z: 8, core: 2. Of those that a mesh axis runs over, the one named last changes fastest.
Arguments:
- transitions: float32 [16, 32, 512, 512], P('team', 'tm'), may hold values from -0.25 to 1.25
- states: float32 [16, 32, 64, 512], P('team', 'tm'), may hold values from -1 to 1
- cotangent: float32 [16, 32, 64, 512], P('team', 'tm'), may hold values from -2.4 to 2.4
- terminal: float32 [16, 64, 512], P('team'), may hold values from -6 to 6
- incidence: int32 [16, 32, 32, 2048], P('team', 'tm'), may hold values 0 or 1
- measured: float32 [16, 32, 64, 32], P('team', 'tm'), may hold values from -0.12 to 0.12
- obs_gain: float32 [16, 512], P('team'), may hold values from -6 to 6
Outputs:
- adjoint: float32 [16, 32, 64, 512], P('team', 'tm')
- grad_transitions: bfloat16 [16, 32, 512, 512], P('team', 'tm')
All inputs are finite; a program needn't handle non-finite values. No bound on the sum of `incidence` on one device may be relied on, other than what follows from the above.
Results may differ from a plain program's by a relative error of at most 0.001.
Values sent between devices are 32-bit elements; how exact they have to be, the bound alone decides.
No kernel may reach another device: no remote copies, remote signals or barrier semaphores. Data moves between devices by JAX's collectives and lax.ppermute only.
A program may use at most 64 MiB of HBM per device.

v0:
```python
import jax
import jax.numpy as jnp
from jax import lax
from jax.sharding import PartitionSpec as P

STATES = 16
TEAM_STATES = 512
COLS = 64
ROBOTS = 32
LMK = 2048
TEAMS = 16
STEPS = 32
RING = 8
BOTH = ("team", "tm")

HIGH = lax.Precision.HIGH


def matmul(left, right):
    return jnp.dot(left, right, precision=HIGH)


def route(pairs_of):
    out = []
    for team in range(TEAMS):
        for ring in range(STEPS // RING):
            for src, dst in pairs_of(team % 2):
                base = team * STEPS + ring * RING
                out.append((base + src, base + dst))
    return out


def holder(pair, odd):
    return 2 * pair + odd


def partner(pair, odd):
    return 2 * pair + 1 - odd


def own_pair(odd):
    return 2 if odd else 1


def near_pair(odd):
    return 3 if odd else 0


def far_pair(odd):
    return 1 if odd else 2


def last_pair(odd):
    return 0 if odd else 3


TO_HOLDER = route(lambda odd: [(partner(p, odd), holder(p, odd)) for p in range(4)])
TO_PARTNER = [(dst, src) for src, dst in TO_HOLDER]


def between(source, target):
    return route(lambda odd: [(holder(source(odd), odd), holder(target(odd), odd))])


NEAR_IN = between(near_pair, own_pair)
FAR_IN = between(far_pair, own_pair)
LAST_STEP = between(last_pair, far_pair)
FIRST_IN = between(lambda odd: 0, own_pair)
FINAL_IN = between(lambda odd: 3, own_pair)
FIRST_OUT = between(own_pair, lambda odd: 0)
FINAL_OUT = between(own_pair, lambda odd: 3)
FAR_OUT = between(own_pair, far_pair)


def ring_hop(ring):
    out = []
    for team in range(TEAMS):
        z = holder(own_pair(team % 2), team % 2)
        out.append((team * STEPS + ring * RING + z, team * STEPS + (ring - 1) * RING + z))
    return out


def send(value, pairs):
    return lax.ppermute(value, BOTH, pairs)


def fold(rows):
    return jnp.concatenate([rows[..., :16, :], rows[..., 16:, :]], axis=-1)


def unfold(packed):
    return jnp.concatenate([packed[..., :64], packed[..., 64:]], axis=-2)


def shards(transitions, states, cotangent, terminal, incidence, measured, obs_gain):
    matrix = transitions[0, 0]
    state = states[0, 0]
    cot = cotangent[0, 0]
    team = lax.axis_index("team")
    step = lax.axis_index("tm")
    even = team % 2 == 0
    ring = step // RING

    def pick(a, b):
        return jnp.where(even, a, b)

    other_matrix = send(matrix, TO_HOLDER)
    other_cot = send(cot, TO_HOLDER)

    incident = incidence[0, 0].astype(jnp.float32)
    slices = incident.reshape(ROBOTS, TEAMS, LMK // TEAMS).transpose(1, 0, 2)
    packed = fold(measured[0, 0].T)
    packed = jnp.broadcast_to(packed[None], (TEAMS,) + packed.shape)
    got = lax.all_to_all(jnp.concatenate([slices, packed], axis=1), "team", 0, 0, tiled=True)
    rows = got[:, :ROBOTS].reshape(TEAMS * ROBOTS, LMK // TEAMS)
    seen = unfold(got[:, ROBOTS:]).reshape(TEAMS * ROBOTS, COLS)
    landmark = jnp.einsum("rc,rl->cl", seen, rows, precision=HIGH)
    part = jnp.einsum("rl,cl->rc", rows, landmark, precision=HIGH)
    part = fold(part.reshape(TEAMS, ROBOTS, COLS))
    parts = lax.all_to_all(part, "team", 0, 0, tiled=True)
    injected = jnp.sum(parts, axis=0)

    high = pick(other_matrix, matrix)
    low = pick(matrix, other_matrix)
    two = jnp.dot(high, low, precision=lax.Precision.HIGHEST)
    two_passed = send(two, LAST_STEP)
    two_near = send(two, NEAR_IN)
    two_far = send(two, FAR_IN)
    two_last = send(two_passed, FAR_IN)

    other_injected = send(injected, TO_HOLDER)
    owner = jnp.arange(TEAM_STATES)[None, :] // STATES == jnp.arange(ROBOTS)[:, None]
    spread = jnp.where(owner, obs_gain[0][None, :], 0.0)

    def drive(direct, packed_rows):
        return direct + jnp.einsum("rc,rn->cn", unfold(packed_rows), spread, precision=HIGH)

    driven = drive(cot, injected)
    other_driven = drive(other_cot, other_injected)
    driven_high = pick(other_driven, driven)
    driven_low = pick(driven, other_driven)
    offset = matmul(driven_high, low) + driven_low
    off0 = send(offset, FIRST_IN)
    off3 = send(offset, FINAL_IN)
    off_far = send(offset, FAR_IN)
    off1 = pick(offset, off_far)
    off2 = pick(off_far, offset)

    map3, map2, map1, map0 = pick(two_last, two_near), pick(two_far, two), pick(two, two_far), pick(two_near, two_last)
    enter1 = matmul(map3, map2)
    enter0 = matmul(enter1, map1)
    eight = matmul(enter0, map0)
    shift1 = matmul(off3, map2) + off2
    shift0 = matmul(shift1, map1) + off1
    total = matmul(shift0, map0) + off0
    enter_far, shift_far = pick(map3, enter1), pick(off3, shift1)
    enter_own, shift_own = pick(enter1, map3), pick(shift1, off3)

    incoming = terminal[0]
    before = jnp.where(ring == STEPS // RING - 1, incoming, 0.0)
    for source in range(STEPS // RING - 1, 0, -1):
        leaving = matmul(incoming, eight) + total
        incoming = send(leaving, ring_hop(source))
        if source > 1:
            before = jnp.where(ring == source - 1, incoming, before)
    incoming = jnp.where(ring == 0, incoming, before)

    to_final = send(incoming, FINAL_OUT)
    to_first = send(matmul(incoming, enter0) + shift0, FIRST_OUT)
    to_far = send(matmul(incoming, enter_far) + shift_far, FAR_OUT)
    at_own = matmul(incoming, enter_own) + shift_own
    pair = (step % RING) // 2
    is_own = pair == pick(own_pair(0), own_pair(1))
    enter = jnp.where(is_own, at_own, jnp.where(pair == 0, to_first, jnp.where(pair == 3, to_final, to_far)))
    middle = matmul(enter, high) + driven_high
    passed = send(pick(enter, middle), TO_PARTNER)
    holds = step % 2 == team % 2
    running = jnp.where(holds, pick(middle, enter), passed)
    grad = jnp.einsum("cn,cm->nm", running, state, precision=HIGH).astype(jnp.bfloat16)
    adjoint = matmul(running, matrix) + driven
    return adjoint[None, None], grad[None, None]


def solution(mesh):
    placed = (
        P("team", "tm", None, None),
        P("team", "tm", None, None),
        P("team", "tm", None, None),
        P("team", None, None),
        P("team", "tm", None, None),
        P("team", "tm", None, None),
        P("team", None),
    )
    return jax.shard_map(
        shards,
        mesh=mesh,
        in_specs=placed,
        out_specs=(P("team", "tm", None, None), P("team", "tm", None, None)),
        check_vma=False,
    )
```

profile of v0, /device:TPU:1, one launch (start us, length us, event | category | flops | bytes accessed | tf_op | source)
XLA Modules:
  0.0 131.8 jit_solution(11847673820517765693)
XLA Ops:
  0.6 0.8 fusion.52
  1.4 1.0 convert_bitcast_fusion
  2.6 0.8 pad_maximum_fusion
  3.4 10.2 %all-to-all-start = ((f32[16,48,128]{2,1,0:T(8,128)}), f32[16,48,128]{2,1,0:T(8,128)S(1)}, u32[]{:S(2)}, u32[]{:S(2)}) async-start(f32[16,48,128]{2,1,0:T(8,128)} %pad_maximum_fusion), calls=%async_computation | async-start | bytes 786432 | tf_op jit(solution)/shard_map/all_to_all | solution.py:114
  13.6 2.5 %collective-permute-start = (f32[512,512]{1,0:T(8,128)S(1)}, f32[512,512]{1,0:T(8,128)S(1)}, u32[]{:S(2)}, u32[]{:S(2)}) collective-permute-start(f32[512,512]{1,0:T(8,128)S(1)} %bitcast.73), channel_id=1, source_target_pairs={{1,0},{3,2},{5,4},{7,6},{9,8},{11,10},{13,12},{15,14},{17,16},{19,... | collective-permute-start | bytes 3145736 | tf_op jit(solution)/shard_map/ppermute | solution.py:84
  16.1 12.0 %all-to-all-done = f32[16,48,128]{2,1,0:T(8,128)S(1)} async-done(((f32[16,48,128]{2,1,0:T(8,128)}), f32[16,48,128]{2,1,0:T(8,128)S(1)}, u32[]{:S(2)}, u32[]{:S(2)}) %all-to-all-start) | async-done | bytes 393248 | tf_op jit(solution)/shard_map/all_to_all | solution.py:114
  28.9 1.9 %fusion.8 = f32[512,512]{1,0:T(8,128)S(1)} fusion(f32[512,512]{1,0:T(8,128)S(1)} %collective-permute-done, pred[]{:T(512)S(6)} %eq.46, f32[1,1,512,512]{3,2,1,0:T(8,128)S(1)} %copy-done.1), kind=kOutput, calls=%fused_computation.29 | convolution fusion | flops 1611137024 | bytes 3145729 | tf_op jit(solution)/shard_map/dot_general | solution.py:125
  30.8 1.6 %collective-permute-start.1 = (f32[512,512]{1,0:T(8,128)S(1)}, f32[512,512]{1,0:T(8,128)}, u32[]{:S(2)}, u32[]{:S(2)}) collective-permute-start(f32[512,512]{1,0:T(8,128)S(1)} %fusion.8), channel_id=1, source_target_pairs={{6,4},{14,12},{22,20},{30,28},{33,35},{41,43},{49,51},{57,59},{70,... | collective-permute-start | bytes 3145736 | tf_op jit(solution)/shard_map/ppermute | solution.py:84
  32.4 0.8 pad_maximum_fusion.1
  33.2 8.8 %all-to-all-start.1 = ((f32[16,16,128]{2,1,0:T(8,128)}), f32[16,16,128]{2,1,0:T(8,128)S(1)}, u32[]{:S(2)}, u32[]{:S(2)}) async-start(f32[16,16,128]{2,1,0:T(8,128)} %pad_maximum_fusion.1), calls=%async_computation.1 | async-start | bytes 262144 | tf_op jit(solution)/shard_map/all_to_all | solution.py:120
  42.0 6.8 %collective-permute-start.5 = (f32[64,512]{1,0:T(8,128)S(1)}, f32[64,512]{1,0:T(8,128)}, u32[]{:S(2)}, u32[]{:S(2)}) collective-permute-start(f32[64,512]{1,0:T(8,128)S(1)} %bitcast.76), channel_id=1, source_target_pairs={{1,0},{3,2},{5,4},{7,6},{9,8},{11,10},{13,12},{15,14},{17,16},{19,... | collective-permute-start | bytes 393224 | tf_op jit(solution)/shard_map/ppermute | solution.py:84
  48.8 2.1 %all-to-all-done.1 = f32[16,16,128]{2,1,0:T(8,128)S(1)} async-done(((f32[16,16,128]{2,1,0:T(8,128)}), f32[16,16,128]{2,1,0:T(8,128)S(1)}, u32[]{:S(2)}, u32[]{:S(2)}) %all-to-all-start.1) | async-done | bytes 131104 | tf_op jit(solution)/shard_map/all_to_all | solution.py:120
  50.9 6.1 %collective-permute-start.6 = (f32[16,128]{1,0:T(8,128)S(1)}, f32[16,128]{1,0:T(8,128)S(1)}, u32[]{:S(2)}, u32[]{:S(2)}) collective-permute-start(f32[16,128]{1,0:T(8,128)S(1)} %reduce_sum.9), channel_id=1, source_target_pairs={{1,0},{3,2},{5,4},{7,6},{9,8},{11,10},{13,12},{15,14},{17,16},{19,... | collective-permute-start | bytes 24584 | tf_op jit(solution)/shard_map/ppermute | solution.py:84
  57.1 0.7 collective-permute-start.4
  57.8 0.7 copy-done.18
  58.9 0.7 collective-permute-start.3
  59.6 0.7 collective-permute-start.2
  60.3 1.2 convolution_add_fusion.12
  61.5 1.7 %convolution_add_fusion.10 = f32[64,512]{1,0:T(8,128)S(1)} fusion(f32[512,512]{1,0:T(8,128)} %copy-done.4, pred[]{:T(512)S(6)} %eq.46, f32[64,512]{1,0:T(8,128)S(1)} %convolution_add_fusion.11, f32[64,512]{1,0:T(8,128)S(1)} %convolution_add_fusion.12, f32[1,1,512,512]{3,2,1,0:T(8,128)S(1)} %copy-done.1), kind=kOutput, calls=%fused_computation.13 | convolution fusion | flops 101023744 | bytes 2490369 | tf_op jit(solution)/shard_map/dot_general | solution.py:20
  63.2 0.7 collective-permute-start.7
  63.9 0.7 collective-permute-start.8
  64.6 0.7 collective-permute-start.9
  65.3 0.5 convolution_add_fusion.9
  65.8 0.5 convolution_add_fusion.8
  66.3 1.1 fusion.9
  67.4 1.0 fusion.10
  68.5 1.0 fusion.11
  69.6 0.5 convolution_add_fusion.7
  70.1 0.4 copy-done.14
  70.5 0.4 fusion.2
  70.9 0.7 collective-permute-start.10
  71.6 0.4 convolution_add_fusion.6
  72.2 0.7 collective-permute-start.11
  72.9 1.1 convolution_add_fusion.5
  74.0 1.3 collective-permute-start.12
  75.3 1.8 %fusion.23 = f32[64,512]{1,0:T(8,128)} fusion(f32[64,512]{1,0:T(8,128)} %collective-permute-done.12, f32[64,512]{1,0:T(8,128)} %copy-done.16, f32[64,512]{1,0:T(8,128)} %copy-done.15, f32[1,64,512]{2,1,0:T(8,128)} %param.10, pred[]{:T(512)S(6)} %eq.54, pred[]{:T(512)S(6)} %eq.53, pred[]{:T(512)S(6)} %eq.52, pred[]{:T(512)S(6)} %eq.48), kind=kLoop, calls=%fused_computation.49 | loop fusion | flops 131072 | bytes 655364 | tf_op jit(solution)/shard_map/jit(_where)/select_n | solution.py:166
  77.1 2.3 %convolution_add_fusion.3 = f32[64,512]{1,0:T(8,128)} fusion(f32[64,512]{1,0:T(8,128)} %copy-done.13, f32[64,512]{1,0:T(8,128)} %fusion.23, f32[512,512]{1,0:T(8,128)} %copy-done.8), kind=kOutput, calls=%fused_computation.6 | convolution fusion | flops 100696064 | bytes 1441792 | tf_op jit(solution)/shard_map/dot_general | solution.py:20
  79.5 1.3 collective-permute-start.14
  80.8 1.3 collective-permute-start.13
  82.1 2.0 %convolution_add_fusion.2 = f32[64,512]{1,0:T(8,128)} fusion(f32[64,512]{1,0:T(8,128)} %fusion.23, f32[512,512]{1,0:T(8,128)S(1)} %copy-done.7, pred[]{:T(512)S(6)} %eq.46, f32[64,512]{1,0:T(8,128)} %copy-done.9, f32[64,512]{1,0:T(8,128)S(1)} %convolution_add_fusion.9, f32[512,512]{1,0:T(8,128)S(1)} %copy-done.3, f32[512,512]{1,0:T(8,128)S(1)} %collective-permute-done.3), kind=kOutput, calls=%fused_computation.5 | convolution fusion | flops 101253120 | bytes 3670017 | tf_op jit(solution)/shard_map/dot_general | solution.py:20
  84.1 1.3 collective-permute-start.15
  85.5 1.7 %fusion.3 = f32[64,512]{1,0:T(8,128)S(1)} fusion(f32[64,512]{1,0:T(8,128)} %fusion.23, f32[512,512]{1,0:T(8,128)} %copy-done.6, pred[]{:T(512)S(6)} %eq.46, f32[64,512]{1,0:T(8,128)} %collective-permute-done.13, f32[64,512]{1,0:T(8,128)} %collective-permute-done.14, f32[64,512]{1,0:T(8,128)} %collective-permute-done.15, ...), kind=kOutput, calls=%fused_computation.16 | convolution fusion | flops 101351424 | bytes 4063236 | tf_op jit(solution)/shard_map/dot_general | solution.py:20
  87.2 0.4 broadcast_select_fusion.16
  87.8 1.3 collective-permute-start.16
  89.1 39.2 %collective-permute-done.16 = f32[64,512]{1,0:T(8,128)S(1)} collective-permute-done((f32[64,512]{1,0:T(8,128)S(1)}, f32[64,512]{1,0:T(8,128)S(1)}, u32[]{:S(2)}, u32[]{:S(2)}) %collective-permute-start.16) | collective-permute-done | bytes 131104 | tf_op jit(solution)/shard_map/ppermute | solution.py:84
  128.3 0.9 select_select_fusion
  129.3 1.1 fusion.1
  130.4 1.4 %fusion = bf16[1,1,512,512]{3,2,1,0:T(8,128)(2,1)} fusion(f32[64,512]{1,0:T(8,128)S(1)} %select_select_fusion, f32[1,1,64,512]{3,2,1,0:T(8,128)S(1)} %copy-done), kind=kOutput, calls=%fused_computation.1 | convolution fusion | flops 100925440 | bytes 786432 | tf_op jit(solution)/shard_map/cn,cm->nm/dot_general | solution.py:179
  (65 shorter events, 1.9 us)
Async XLA Ops:
  0.6 129.7 %copy-start = (f32[1,1,64,512]{3,2,1,0:T(8,128)S(1)}, f32[1,1,64,512]{3,2,1,0:T(8,128)}, u32[]{:S(2)}) copy-start(f32[1,1,64,512]{3,2,1,0:T(8,128)} %param.8) | copy-start | bytes 393220
  2.4 11.2 %copy-start.1 = (f32[1,1,512,512]{3,2,1,0:T(8,128)S(1)}, f32[1,1,512,512]{3,2,1,0:T(8,128)}, u32[]{:S(2)}) copy-start(f32[1,1,512,512]{3,2,1,0:T(8,128)} %param.7) | copy-start | bytes 3145732
  3.4 24.7 %all-to-all-start = ((f32[16,48,128]{2,1,0:T(8,128)}), f32[16,48,128]{2,1,0:T(8,128)S(1)}, u32[]{:S(2)}, u32[]{:S(2)}) async-start(f32[16,48,128]{2,1,0:T(8,128)} %pad_maximum_fusion), calls=%async_computation | async-start | bytes 786432 | tf_op jit(solution)/shard_map/all_to_all | solution.py:114
  13.6 15.3 %collective-permute-start = (f32[512,512]{1,0:T(8,128)S(1)}, f32[512,512]{1,0:T(8,128)S(1)}, u32[]{:S(2)}, u32[]{:S(2)}) collective-permute-start(f32[512,512]{1,0:T(8,128)S(1)} %bitcast.73), channel_id=1, source_target_pairs={{1,0},{3,2},{5,4},{7,6},{9,8},{11,10},{13,12},{15,14},{17,16},{19,... | collective-permute-start | bytes 3145736 | tf_op jit(solution)/shard_map/ppermute | solution.py:84
  28.9 1.9 %copy-start.4 = (f32[512,512]{1,0:T(8,128)}, f32[512,512]{1,0:T(8,128)S(1)}, u32[]{:S(2)}) copy-start(f32[512,512]{1,0:T(8,128)S(1)} %collective-permute-done) | copy-start | bytes 3145732
  30.8 28.8 %collective-permute-start.1 = (f32[512,512]{1,0:T(8,128)S(1)}, f32[512,512]{1,0:T(8,128)}, u32[]{:S(2)}, u32[]{:S(2)}) collective-permute-start(f32[512,512]{1,0:T(8,128)S(1)} %fusion.8), channel_id=1, source_target_pairs={{6,4},{14,12},{22,20},{30,28},{33,35},{41,43},{49,51},{57,59},{70,... | collective-permute-start | bytes 3145736 | tf_op jit(solution)/shard_map/ppermute | solution.py:84
  33.2 8.8 %copy-start.17 = (f32[1,1,64,512]{3,2,1,0:T(8,128)S(1)}, f32[1,1,64,512]{3,2,1,0:T(8,128)}, u32[]{:S(2)}) copy-start(f32[1,1,64,512]{3,2,1,0:T(8,128)} %param.9) | copy-start | bytes 393220
  33.2 17.7 %all-to-all-start.1 = ((f32[16,16,128]{2,1,0:T(8,128)}), f32[16,16,128]{2,1,0:T(8,128)S(1)}, u32[]{:S(2)}, u32[]{:S(2)}) async-start(f32[16,16,128]{2,1,0:T(8,128)} %pad_maximum_fusion.1), calls=%async_computation.1 | async-start | bytes 262144 | tf_op jit(solution)/shard_map/all_to_all | solution.py:120
  42.0 18.3 %collective-permute-start.5 = (f32[64,512]{1,0:T(8,128)S(1)}, f32[64,512]{1,0:T(8,128)}, u32[]{:S(2)}, u32[]{:S(2)}) collective-permute-start(f32[64,512]{1,0:T(8,128)S(1)} %bitcast.76), channel_id=1, source_target_pairs={{1,0},{3,2},{5,4},{7,6},{9,8},{11,10},{13,12},{15,14},{17,16},{19,... | collective-permute-start | bytes 393224 | tf_op jit(solution)/shard_map/ppermute | solution.py:84
  50.9 7.8 %collective-permute-start.6 = (f32[16,128]{1,0:T(8,128)S(1)}, f32[16,128]{1,0:T(8,128)S(1)}, u32[]{:S(2)}, u32[]{:S(2)}) collective-permute-start(f32[16,128]{1,0:T(8,128)S(1)} %reduce_sum.9), channel_id=1, source_target_pairs={{1,0},{3,2},{5,4},{7,6},{9,8},{11,10},{13,12},{15,14},{17,16},{19,... | collective-permute-start | bytes 24584 | tf_op jit(solution)/shard_map/ppermute | solution.py:84
  57.1 8.2 %collective-permute-start.4 = (f32[512,512]{1,0:T(8,128)S(1)}, f32[512,512]{1,0:T(8,128)S(1)}, u32[]{:S(2)}, u32[]{:S(2)}) collective-permute-start(f32[512,512]{1,0:T(8,128)S(1)} %fusion.8), channel_id=1, source_target_pairs={{4,2},{12,10},{20,18},{28,26},{35,37},{43,45},{51,53},{59,61},{68,... | collective-permute-start | bytes 3145736 | tf_op jit(solution)/shard_map/ppermute | solution.py:84
  57.8 0.7 copy-start.18
  58.9 7.4 %collective-permute-start.3 = (f32[512,512]{1,0:T(8,128)S(1)}, f32[512,512]{1,0:T(8,128)S(1)}, u32[]{:S(2)}, u32[]{:S(2)}) collective-permute-start(f32[512,512]{1,0:T(8,128)S(1)} %fusion.8), channel_id=1, source_target_pairs={{0,2},{8,10},{16,18},{24,26},{39,37},{47,45},{55,53},{63,61},{64,6... | collective-permute-start | bytes 3145736 | tf_op jit(solution)/shard_map/ppermute | solution.py:84
  59.6 6.7 %collective-permute-start.2 = (f32[512,512]{1,0:T(8,128)}, f32[512,512]{1,0:T(8,128)S(1)}, u32[]{:S(2)}, u32[]{:S(2)}) collective-permute-start(f32[512,512]{1,0:T(8,128)} %collective-permute-done.1), channel_id=1, source_target_pairs={{4,2},{12,10},{20,18},{28,26},{35,37},{43,45},{51,53},{59,61},{68,... | collective-permute-start | bytes 3145736 | tf_op jit(solution)/shard_map/ppermute | solution.py:84
  61.5 1.7 %copy-start.10 = (f32[64,512]{1,0:T(8,128)}, f32[64,512]{1,0:T(8,128)S(1)}, u32[]{:S(2)}) copy-start(f32[64,512]{1,0:T(8,128)S(1)} %convolution_add_fusion.12) | copy-start | bytes 393220
  63.2 1.4 %collective-permute-start.7 = (f32[64,512]{1,0:T(8,128)S(1)}, f32[64,512]{1,0:T(8,128)S(1)}, u32[]{:S(2)}, u32[]{:S(2)}) collective-permute-start(f32[64,512]{1,0:T(8,128)S(1)} %convolution_add_fusion.10), channel_id=1, source_target_pairs={{6,2},{14,10},{22,18},{30,26},{39,37},{47,45},{55,53},{63,61},{70,... | collective-permute-start | bytes 393224 | tf_op jit(solution)/shard_map/ppermute | solution.py:84
  63.9 1.4 %collective-permute-start.8 = (f32[64,512]{1,0:T(8,128)S(1)}, f32[64,512]{1,0:T(8,128)S(1)}, u32[]{:S(2)}, u32[]{:S(2)}) collective-permute-start(f32[64,512]{1,0:T(8,128)S(1)} %convolution_add_fusion.10), channel_id=1, source_target_pairs={{4,2},{12,10},{20,18},{28,26},{35,37},{43,45},{51,53},{59,61},{68,... | collective-permute-start | bytes 393224 | tf_op jit(solution)/shard_map/ppermute | solution.py:84
  64.6 1.2 copy-start.9
  64.6 4.9 %collective-permute-start.9 = (f32[64,512]{1,0:T(8,128)S(1)}, f32[64,512]{1,0:T(8,128)S(1)}, u32[]{:S(2)}, u32[]{:S(2)}) collective-permute-start(f32[64,512]{1,0:T(8,128)S(1)} %convolution_add_fusion.10), channel_id=1, source_target_pairs={{0,2},{8,10},{16,18},{24,26},{33,37},{41,45},{49,53},{57,61},{64,6... | collective-permute-start | bytes 393224 | tf_op jit(solution)/shard_map/ppermute | solution.py:84
  66.3 3.3 %copy-start.13 = (f32[64,512]{1,0:T(8,128)}, f32[64,512]{1,0:T(8,128)S(1)}, u32[]{:S(2)}) copy-start(f32[64,512]{1,0:T(8,128)S(1)} %convolution_add_fusion.8) | copy-start | bytes 393220
  66.3 3.3 %copy-start.2 = (f32[512,512]{1,0:T(8,128)}, f32[512,512]{1,0:T(8,128)S(1)}, u32[]{:S(2)}) copy-start(f32[512,512]{1,0:T(8,128)S(1)} %collective-permute-done.2) | copy-start | bytes 3145732
  67.4 1.1 copy-start.6
  68.5 1.1 copy-start.8
  69.5 0.9 copy-start.14
  70.9 0.7 collective-permute-start.10
  71.6 0.6 copy-start.15
  72.2 0.7 collective-permute-start.11
  72.9 1.1 copy-start.16
  74.0 1.3 collective-permute-start.12
  75.3 6.8 %copy-start.3 = (f32[512,512]{1,0:T(8,128)S(1)}, f32[512,512]{1,0:T(8,128)}, u32[]{:S(2)}) copy-start(f32[512,512]{1,0:T(8,128)} %copy-done.2) | copy-start | bytes 3145732
  75.3 6.8 %copy-start.7 = (f32[512,512]{1,0:T(8,128)S(1)}, f32[512,512]{1,0:T(8,128)}, u32[]{:S(2)}) copy-start(f32[512,512]{1,0:T(8,128)} %copy-done.6) | copy-start | bytes 3145732
  79.5 6.0 %collective-permute-start.14 = (f32[64,512]{1,0:T(8,128)}, f32[64,512]{1,0:T(8,128)}, u32[]{:S(2)}, u32[]{:S(2)}) collective-permute-start(f32[64,512]{1,0:T(8,128)} %fusion.23), channel_id=1, source_target_pairs={{2,6},{10,14},{18,22},{26,30},{37,39},{45,47},{53,55},{61,63},{66,... | collective-permute-start | bytes 393224 | tf_op jit(solution)/shard_map/ppermute | solution.py:84
  80.8 4.7 %collective-permute-start.13 = (f32[64,512]{1,0:T(8,128)}, f32[64,512]{1,0:T(8,128)}, u32[]{:S(2)}, u32[]{:S(2)}) collective-permute-start(f32[64,512]{1,0:T(8,128)} %convolution_add_fusion.3), channel_id=1, source_target_pairs={{2,0},{10,8},{18,16},{26,24},{37,33},{45,41},{53,49},{61,57},{66,6... | collective-permute-start | bytes 393224 | tf_op jit(solution)/shard_map/ppermute | solution.py:84
  84.1 1.3 %collective-permute-start.15 = (f32[64,512]{1,0:T(8,128)}, f32[64,512]{1,0:T(8,128)}, u32[]{:S(2)}, u32[]{:S(2)}) collective-permute-start(f32[64,512]{1,0:T(8,128)} %convolution_add_fusion.2), channel_id=1, source_target_pairs={{2,4},{10,12},{18,20},{26,28},{37,35},{45,43},{53,51},{61,59},{66,... | collective-permute-start | bytes 393224 | tf_op jit(solution)/shard_map/ppermute | solution.py:84
  85.4 1.7 %copy-start.5 = (f32[512,512]{1,0:T(8,128)S(1)}, f32[512,512]{1,0:T(8,128)}, u32[]{:S(2)}) copy-start(f32[512,512]{1,0:T(8,128)} %copy-done.4) | copy-start | bytes 3145732
  85.4 1.7 %copy-start.11 = (f32[64,512]{1,0:T(8,128)S(1)}, f32[64,512]{1,0:T(8,128)}, u32[]{:S(2)}) copy-start(f32[64,512]{1,0:T(8,128)} %copy-done.10) | copy-start | bytes 393220
  87.2 0.7 copy-start.12
  87.8 40.5 %collective-permute-start.16 = (f32[64,512]{1,0:T(8,128)S(1)}, f32[64,512]{1,0:T(8,128)S(1)}, u32[]{:S(2)}, u32[]{:S(2)}) collective-permute-start(f32[64,512]{1,0:T(8,128)S(1)} %get-tuple-element.12), channel_id=1, source_target_pairs={{0,1},{2,3},{4,5},{6,7},{8,9},{10,11},{12,13},{14,15},{16,17},{18,... | collective-permute-start | bytes 393224 | tf_op jit(solution)/shard_map/ppermute | solution.py:84
where the time goes:
time: 133 us; the launch traced here: 132 us
  waiting for transfers between devices  53.4 us (40%)
  starting transfers between devices  48 us (36%)
  matrix products  21.2 us (16%)
  other arithmetic  5.34 us (4%)
  local copies, waits for them, and re-layouts  2.69 us (2%)
    ppermute x17, waiting for transfers between devices, send(): return lax.ppermute(value, BOTH, pairs)  39.3 us
    ppermute x17, starting transfers between devices, send(): return lax.ppermute(value, BOTH, pairs)  29 us
    dot_general x15, matrix products, matmul(): return jnp.dot(left, right, precision=HIGH)  15.9 us
    all_to_all x1, waiting for transfers between devices, shards(): lax.all_to_all(jnp.concatenate([slices, packed], axis=1), 'team', 0, 0, t...  12 us
    all_to_all x1, starting transfers between devices, shards(): lax.all_to_all(jnp.concatenate([slices, packed], axis=1), 'team', 0, 0, t...  10.2 us
    all_to_all x1, starting transfers between devices, shards(): parts = lax.all_to_all(part, 'team', 0, 0, tiled=True)  8.81 us
  transfers between devices with their start and end apart: 19, of which 3 were waited for; matrix products, arithmetic and copies ran while one was open for 8% of the time, Pallas kernels for 0%

commit v1 on v0

--- a/solution.py
+++ b/solution.py
@@ -62,14 +62,27 @@
     return route(lambda odd: [(holder(source(odd), odd), holder(target(odd), odd))])
 
 
-NEAR_IN = between(near_pair, own_pair)
+INWARD = route(
+    lambda odd: [
+        (holder(near_pair(odd), odd), holder(own_pair(odd), odd)),
+        (holder(last_pair(odd), odd), holder(far_pair(odd), odd)),
+    ]
+)
 FAR_IN = between(far_pair, own_pair)
-LAST_STEP = between(last_pair, far_pair)
 FIRST_IN = between(lambda odd: 0, own_pair)
 FINAL_IN = between(lambda odd: 3, own_pair)
 FIRST_OUT = between(own_pair, lambda odd: 0)
-FINAL_OUT = between(own_pair, lambda odd: 3)
 FAR_OUT = between(own_pair, far_pair)
+
+
+def down(target):
+    out = []
+    for team in range(TEAMS):
+        odd = team % 2
+        for ring in range(1, STEPS // RING):
+            base = team * STEPS + ring * RING
+            out.append((base + holder(own_pair(odd), odd), base - RING + holder(target(odd), odd)))
+    return out
 
 
 def ring_hop(ring):
@@ -105,7 +118,6 @@
         return jnp.where(even, a, b)
 
     other_matrix = send(matrix, TO_HOLDER)
-    other_cot = send(cot, TO_HOLDER)
 
     incident = incidence[0, 0].astype(jnp.float32)
     slices = incident.reshape(ROBOTS, TEAMS, LMK // TEAMS).transpose(1, 0, 2)
@@ -123,59 +135,72 @@
     high = pick(other_matrix, matrix)
     low = pick(matrix, other_matrix)
     two = jnp.dot(high, low, precision=lax.Precision.HIGHEST)
-    two_passed = send(two, LAST_STEP)
-    two_near = send(two, NEAR_IN)
+    inward = send(two, INWARD)
     two_far = send(two, FAR_IN)
-    two_last = send(two_passed, FAR_IN)
-
-    other_injected = send(injected, TO_HOLDER)
+    two_last = send(inward, FAR_IN)
+
     owner = jnp.arange(TEAM_STATES)[None, :] // STATES == jnp.arange(ROBOTS)[:, None]
     spread = jnp.where(owner, obs_gain[0][None, :], 0.0)
-
-    def drive(direct, packed_rows):
-        return direct + jnp.einsum("rc,rn->cn", unfold(packed_rows), spread, precision=HIGH)
-
-    driven = drive(cot, injected)
-    other_driven = drive(other_cot, other_injected)
+    driven = cot + jnp.einsum("rc,rn->cn", unfold(injected), spread, precision=HIGH)
+    other_driven = send(driven, TO_HOLDER)
     driven_high = pick(other_driven, driven)
     driven_low = pick(driven, other_driven)
     offset = matmul(driven_high, low) + driven_low
-    off0 = send(offset, FIRST_IN)
     off3 = send(offset, FINAL_IN)
     off_far = send(offset, FAR_IN)
-    off1 = pick(offset, off_far)
-    off2 = pick(off_far, offset)
-
-    map3, map2, map1, map0 = pick(two_last, two_near), pick(two_far, two), pick(two, two_far), pick(two_near, two_last)
+    off0 = send(offset, FIRST_IN)
+
+    map3, map2, map1, map0 = pick(two_last, inward), pick(two_far, two), pick(two, two_far), pick(inward, two_last)
+    map3, map2, map1, map0 = lax.optimization_barrier((map3, map2, map1, map0))
     enter1 = matmul(map3, map2)
     enter0 = matmul(enter1, map1)
     eight = matmul(enter0, map0)
+    enter_far = pick(map3, enter1)
+    enter_own = pick(enter1, map3)
+    eight, enter0, enter_far, enter_own, off3, off_far, off0 = lax.optimization_barrier(
+        (eight, enter0, enter_far, enter_own, off3, off_far, off0)
+    )
+    off1 = pick(offset, off_far)
+    off2 = pick(off_far, offset)
     shift1 = matmul(off3, map2) + off2
     shift0 = matmul(shift1, map1) + off1
     total = matmul(shift0, map0) + off0
-    enter_far, shift_far = pick(map3, enter1), pick(off3, shift1)
-    enter_own, shift_own = pick(enter1, map3), pick(shift1, off3)
-
-    incoming = terminal[0]
-    before = jnp.where(ring == STEPS // RING - 1, incoming, 0.0)
-    for source in range(STEPS // RING - 1, 0, -1):
-        leaving = matmul(incoming, eight) + total
-        incoming = send(leaving, ring_hop(source))
-        if source > 1:
-            before = jnp.where(ring == source - 1, incoming, before)
-    incoming = jnp.where(ring == 0, incoming, before)
-
-    to_final = send(incoming, FINAL_OUT)
-    to_first = send(matmul(incoming, enter0) + shift0, FIRST_OUT)
-    to_far = send(matmul(incoming, enter_far) + shift_far, FAR_OUT)
-    at_own = matmul(incoming, enter_own) + shift_own
+    shift_far = pick(off3, shift1)
+    shift_own = pick(shift1, off3)
+
     pair = (step % RING) // 2
     is_own = pair == pick(own_pair(0), own_pair(1))
-    enter = jnp.where(is_own, at_own, jnp.where(pair == 0, to_first, jnp.where(pair == 3, to_final, to_far)))
+    last_ring = STEPS // RING - 1
+    leaving = matmul(terminal[0], eight) + total
+    incoming = send(leaving, ring_hop(last_ring))
+    map_first = send(enter0, FIRST_OUT)
+    map_far = send(enter_far, FAR_OUT)
+    shift_first = send(shift0, FIRST_OUT)
+    shift_far = send(shift_far, FAR_OUT)
+    out = leaving
+    for source in range(last_ring - 1, 0, -1):
+        leaving = matmul(incoming, eight) + total
+        out = jnp.where(ring == source, leaving, out)
+        if source > 1:
+            incoming = send(leaving, ring_hop(source))
+    parts = [
+        send(out, down(lambda odd: 3)),
+        send(out, down(lambda odd: 0)),
+        send(out, down(far_pair)),
+        send(out, down(own_pair)),
+    ]
+    enter_map = jnp.where(is_own, enter_own, jnp.where(pair == 0, map_first, map_far))
+    enter_shift = jnp.where(is_own, shift_own, jnp.where(pair == 0, shift_first, shift_far))
+    enter_map, enter_shift = lax.optimization_barrier((enter_map, enter_shift))
+    entry = (parts[0] + parts[1]) + (parts[2] + parts[3]) + jnp.where(ring == last_ring, terminal[0], 0.0)
+    entry = lax.optimization_barrier(entry)
+    enter = jnp.where(pair == 3, entry, matmul(entry, enter_map) + enter_shift)
+    enter = lax.optimization_barrier(enter)
     middle = matmul(enter, high) + driven_high
     passed = send(pick(enter, middle), TO_PARTNER)
     holds = step % 2 == team % 2
     running = jnp.where(holds, pick(middle, enter), passed)
+    running = lax.optimization_barrier(running)
     grad = jnp.einsum("cn,cm->nm", running, state, precision=HIGH).astype(jnp.bfloat16)
     adjoint = matmul(running, matrix) + driven
     return adjoint[None, None], grad[None, None]

time: 133 us -> 150 us (1.13)
  the two profiles are of different devices: /device:TPU:1 before, /device:TPU:37 now
where the time goes in v1:
time: 150 us; the launch traced here: 149 us
  waiting for transfers between devices  63.6 us (42%)
  starting transfers between devices  52.5 us (35%)
  matrix products  19.1 us (13%)
  other arithmetic  9.15 us (6%)
  local copies, waits for them, and re-layouts  3.73 us (2%)
    ppermute x19, waiting for transfers between devices, send(): return lax.ppermute(value, BOTH, pairs)  50.7 us
    ppermute x19, starting transfers between devices, send(): return lax.ppermute(value, BOTH, pairs)  32.9 us
    dot_general x13, matrix products, matmul(): return jnp.dot(left, right, precision=HIGH)  14.9 us
    all_to_all x1, starting transfers between devices, shards(): parts = lax.all_to_all(part, 'team', 0, 0, tiled=True)  12.7 us
    all_to_all x1, waiting for transfers between devices, shards(): lax.all_to_all(jnp.concatenate([slices, packed], axis=1), 'team', 0, 0, t...  10.2 us
    all_to_all x1, starting transfers between devices, shards(): lax.all_to_all(jnp.concatenate([slices, packed], axis=1), 'team', 0, 0, t...  6.95 us
  transfers between devices with their start and end apart: 21, of which 4 were waited for; matrix products, arithmetic and copies ran while one was open for 13% of the time, Pallas kernels for 0%

profile of v1, /device:TPU:37, one launch (start us, length us, event | category | flops | bytes accessed | tf_op | source)
XLA Modules:
  0.0 149.2 jit_solution(15588884353698063321)
XLA Ops:
  0.6 4.2 %collective-permute-start = (f32[512,512]{1,0:T(8,128)}, f32[512,512]{1,0:T(8,128)S(1)}, u32[]{:S(2)}, u32[]{:S(2)}) collective-permute-start(f32[512,512]{1,0:T(8,128)} %bitcast.74), channel_id=1, source_target_pairs={{1,0},{3,2},{5,4},{7,6},{9,8},{11,10},{13,12},{15,14},{17,16},{19,... | collective-permute-start | bytes 3145736 | tf_op jit(solution)/shard_map/ppermute | solution.py:97
  4.8 0.7 fusion.35
  5.6 1.0 convert_bitcast_fusion
  6.8 0.8 pad_maximum_fusion
  7.6 6.9 %all-to-all-start = ((f32[16,48,128]{2,1,0:T(8,128)}), f32[16,48,128]{2,1,0:T(8,128)S(1)}, u32[]{:S(2)}, u32[]{:S(2)}) async-start(f32[16,48,128]{2,1,0:T(8,128)} %pad_maximum_fusion), calls=%async_computation | async-start | bytes 786432 | tf_op jit(solution)/shard_map/all_to_all | solution.py:126
  14.5 10.2 %all-to-all-done = f32[16,48,128]{2,1,0:T(8,128)S(1)} async-done(((f32[16,48,128]{2,1,0:T(8,128)}), f32[16,48,128]{2,1,0:T(8,128)S(1)}, u32[]{:S(2)}, u32[]{:S(2)}) %all-to-all-start) | async-done | bytes 393248 | tf_op jit(solution)/shard_map/all_to_all | solution.py:126
  24.8 0.6 copy-done.3
  25.4 1.9 %fusion.5 = f32[512,512]{1,0:T(8,128)S(1)} fusion(f32[512,512]{1,0:T(8,128)S(1)} %collective-permute-done, pred[]{:T(512)S(6)} %eq.44, f32[1,1,512,512]{3,2,1,0:T(8,128)S(1)} %copy-done.1), kind=kOutput, calls=%fused_computation.26 | convolution fusion | flops 1611137024 | bytes 3145729 | tf_op jit(solution)/shard_map/dot_general | solution.py:137
  27.3 1.7 %collective-permute-start.1 = (f32[512,512]{1,0:T(8,128)S(1)}, f32[512,512]{1,0:T(8,128)}, u32[]{:S(2)}, u32[]{:S(2)}) collective-permute-start(f32[512,512]{1,0:T(8,128)S(1)} %fusion.5), channel_id=1, source_target_pairs={{0,2},{6,4},{8,10},{14,12},{16,18},{22,20},{24,26},{30,28},{39,37}... | collective-permute-start | bytes 3145736 | tf_op jit(solution)/shard_map/ppermute | solution.py:97
  29.7 0.8 pad_maximum_fusion.1
  30.4 12.7 %all-to-all-start.1 = ((f32[16,16,128]{2,1,0:T(8,128)}), f32[16,16,128]{2,1,0:T(8,128)S(1)}, u32[]{:S(2)}, u32[]{:S(2)}) async-start(f32[16,16,128]{2,1,0:T(8,128)} %pad_maximum_fusion.1), calls=%async_computation.1 | async-start | bytes 262144 | tf_op jit(solution)/shard_map/all_to_all | solution.py:132
  43.1 1.8 %collective-permute-start.3 = (f32[512,512]{1,0:T(8,128)S(1)}, f32[512,512]{1,0:T(8,128)}, u32[]{:S(2)}, u32[]{:S(2)}) collective-permute-start(f32[512,512]{1,0:T(8,128)S(1)} %fusion.5), channel_id=1, source_target_pairs={{4,2},{12,10},{20,18},{28,26},{35,37},{43,45},{51,53},{59,61},{68,... | collective-permute-start | bytes 3145736 | tf_op jit(solution)/shard_map/ppermute | solution.py:97
  44.9 2.8 %all-to-all-done.1 = f32[16,16,128]{2,1,0:T(8,128)S(1)} async-done(((f32[16,16,128]{2,1,0:T(8,128)}), f32[16,16,128]{2,1,0:T(8,128)S(1)}, u32[]{:S(2)}, u32[]{:S(2)}) %all-to-all-start.1) | async-done | bytes 131104 | tf_op jit(solution)/shard_map/all_to_all | solution.py:132
  47.6 0.7 collective-permute-start.2
  48.5 0.7 copy-done.13
  49.4 10.6 %collective-permute-start.4 = (f32[64,512]{1,0:T(8,128)S(1)}, f32[64,512]{1,0:T(8,128)S(1)}, u32[]{:S(2)}, u32[]{:S(2)}) collective-permute-start(f32[64,512]{1,0:T(8,128)S(1)} %convolution_add_fusion.9), channel_id=1, source_target_pairs={{1,0},{3,2},{5,4},{7,6},{9,8},{11,10},{13,12},{15,14},{17,16},{19,... | collective-permute-start | bytes 393224 | tf_op jit(solution)/shard_map/ppermute | solution.py:97
  60.0 1.9 %collective-permute-done.4 = f32[64,512]{1,0:T(8,128)S(1)} collective-permute-done((f32[64,512]{1,0:T(8,128)S(1)}, f32[64,512]{1,0:T(8,128)S(1)}, u32[]{:S(2)}, u32[]{:S(2)}) %collective-permute-start.4) | collective-permute-done | bytes 131104 | tf_op jit(solution)/shard_map/ppermute | solution.py:97
  62.6 0.7 collective-permute-start.5
  63.2 0.7 collective-permute-start.6
  63.9 0.7 collective-permute-start.7
  64.6 1.5 broadcast_select_fusion.3
  66.1 1.5 %broadcast_select_fusion.2 = (f32[512,512]{1,0:T(8,128)S(1)}, f32[512,512]{1,0:T(8,128)S(1)}) fusion(f32[512,512]{1,0:T(8,128)} %collective-permute-done.1, f32[512,512]{1,0:T(8,128)S(1)} %collective-permute-done.2, pred[]{:T(512)S(6)} %eq.44), kind=kLoop, calls=%fused_computation.20 | loop fusion | flops 524288 | bytes 4194305 | tf_op jit(solution)/shard_map/jit(_where)/select_n | solution.py:118
  67.6 2.5 %broadcast_select_fusion = (f32[512,512]{1,0:T(8,128)}, f32[512,512]{1,0:T(8,128)}, f32[512,512]{1,0:T(8,128)S(1)}) fusion(f32[512,512]{1,0:T(8,128)S(1)} %get-tuple-element.15, pred[]{:T(512)S(6)} %eq.44, f32[512,512]{1,0:T(8,128)S(1)} %get-tuple-element.16), kind=kOutput, calls=%fused_computation.18 | convolution fusion | flops 805830656 | bytes 5242881 | tf_op jit(solution)/shard_map/dot_general | solution.py:20
  70.1 2.0 %fusion.37 = f32[512,512]{1,0:T(8,128)} fusion(f32[512,512]{1,0:T(8,128)S(1)} %get-tuple-element.42, f32[512,512]{1,0:T(8,128)S(1)} %get-tuple-element.17), kind=kOutput, calls=%fused_computation.74 | convolution fusion | flops 805306368 | bytes 3145728 | tf_op jit(solution)/shard_map/dot_general | solution.py:20
  72.1 2.3 %fusion.38 = f32[512,512]{1,0:T(8,128)S(1)} fusion(f32[512,512]{1,0:T(8,128)} %fusion.37, f32[512,512]{1,0:T(8,128)S(1)} %get-tuple-element.18), kind=kOutput, calls=%fused_computation.75 | convolution fusion | flops 805306368 | bytes 3145728 | tf_op jit(solution)/shard_map/dot_general | solution.py:20
  74.4 1.1 broadcast_select_fusion.13
  75.6 0.5 convolution_add_fusion.6
  76.2 0.5 convolution_add_fusion.5
  77.6 0.7 collective-permute-start.8
  78.3 1.7 %collective-permute-start.14 = (f32[512,512]{1,0:T(8,128)}, f32[512,512]{1,0:T(8,128)}, u32[]{:S(2)}, u32[]{:S(2)}) collective-permute-start(f32[512,512]{1,0:T(8,128)} %fusion.37), channel_id=1, source_target_pairs={{2,0},{10,8},{18,16},{26,24},{37,33},{45,41},{53,49},{61,57},{66,6... | collective-permute-start | bytes 3145736 | tf_op jit(solution)/shard_map/ppermute | solution.py:97
  80.0 1.7 %collective-permute-start.15 = (f32[512,512]{1,0:T(8,128)}, f32[512,512]{1,0:T(8,128)}, u32[]{:S(2)}, u32[]{:S(2)}) collective-permute-start(f32[512,512]{1,0:T(8,128)} %get-tuple-element.25), channel_id=1, source_target_pairs={{2,4},{10,12},{18,20},{26,28},{37,35},{45,43},{53,51},{61,59},{66,... | collective-permute-start | bytes 3145736 | tf_op jit(solution)/shard_map/ppermute | solution.py:97
  81.6 1.1 convolution_add_fusion.4
  82.7 1.3 collective-permute-start.9
  84.0 1.3 collective-permute-start.16
  85.3 1.3 collective-permute-start.17
  86.6 2.1 %fusion.4 = f32[64,512]{1,0:T(8,128)} fusion(f32[64,512]{1,0:T(8,128)S(1)} %convolution_add_fusion.5, f32[64,512]{1,0:T(8,128)} %collective-permute-done.9, f32[512,512]{1,0:T(8,128)S(1)} %fusion.38, f32[64,512]{1,0:T(8,128)} %convolution_add_fusion.4, f32[64,512]{1,0:T(8,128)} %copy-done.10, pred[]{:T(512)S(6)} %eq.50, pred[]{:T(512)S(6)} %eq.46), kind=kOutput, calls=%fused_computation.15 | convolution fusion | flops 100761600 | bytes 1703938 | tf_op jit(solution)/shard_map/dot_general | solution.py:20
  88.7 0.8 collective-permute-start.10
  89.6 0.7 collective-permute-start.11
  90.2 0.7 collective-permute-start.12
  90.9 0.7 collective-permute-start.13
  91.6 1.0 select_select_fusion.2
  92.7 1.0 fusion.15
  93.7 1.6 %select_select_fusion = f32[512,512]{1,0:T(8,128)S(1)} fusion(f32[512,512]{1,0:T(8,128)S(1)} %copy-done.2, f32[512,512]{1,0:T(8,128)} %collective-permute-done.14, f32[512,512]{1,0:T(8,128)} %collective-permute-done.15, pred[]{:T(512)S(6)} %eq.53, pred[]{:T(512)S(6)} %eq.52), kind=kLoop, calls=%fused_computation.17 | loop fusion | flops 524288 | bytes 4194306 | tf_op jit(solution)/shard_map/jit(_where)/select_n | solution.py:192
  95.3 0.5 fusion.2
  96.6 1.3 collective-permute-start.18
  97.9 48.7 %collective-permute-done.18 = f32[64,512]{1,0:T(8,128)S(1)} collective-permute-done((f32[64,512]{1,0:T(8,128)S(1)}, f32[64,512]{1,0:T(8,128)S(1)}, u32[]{:S(2)}, u32[]{:S(2)}) %collective-permute-start.18) | collective-permute-done | bytes 131104 | tf_op jit(solution)/shard_map/ppermute | solution.py:97
  146.7 1.1 fusion.1
  147.7 1.4 fusion
  (59 shorter events, 4.0 us)
Async XLA Ops:
  0.6 147.1 %copy-start = (f32[1,1,64,512]{3,2,1,0:T(8,128)S(1)}, f32[1,1,64,512]{3,2,1,0:T(8,128)}, u32[]{:S(2)}) copy-start(f32[1,1,64,512]{3,2,1,0:T(8,128)} %param.8) | copy-start | bytes 393220
  0.6 24.8 %collective-permute-start = (f32[512,512]{1,0:T(8,128)}, f32[512,512]{1,0:T(8,128)S(1)}, u32[]{:S(2)}, u32[]{:S(2)}) collective-permute-start(f32[512,512]{1,0:T(8,128)} %bitcast.74), channel_id=1, source_target_pairs={{1,0},{3,2},{5,4},{7,6},{9,8},{11,10},{13,12},{15,14},{17,16},{19,... | collective-permute-start | bytes 3145736 | tf_op jit(solution)/shard_map/ppermute | solution.py:97
  6.8 18.6 %copy-start.1 = (f32[1,1,512,512]{3,2,1,0:T(8,128)S(1)}, f32[1,1,512,512]{3,2,1,0:T(8,128)}, u32[]{:S(2)}) copy-start(f32[1,1,512,512]{3,2,1,0:T(8,128)} %param.7) | copy-start | bytes 3145732
  7.6 17.1 %all-to-all-start = ((f32[16,48,128]{2,1,0:T(8,128)}), f32[16,48,128]{2,1,0:T(8,128)S(1)}, u32[]{:S(2)}, u32[]{:S(2)}) async-start(f32[16,48,128]{2,1,0:T(8,128)} %pad_maximum_fusion), calls=%async_computation | async-start | bytes 786432 | tf_op jit(solution)/shard_map/all_to_all | solution.py:126
  24.7 0.7 copy-start.3
  25.4 3.6 %copy-start.4 = (f32[16,48,128]{2,1,0:T(8,128)S(1)}, f32[16,48,128]{2,1,0:T(8,128)}, u32[]{:S(2)}) copy-start(f32[16,48,128]{2,1,0:T(8,128)} %copy-done.3) | copy-start | bytes 1179652
  27.3 20.3 %collective-permute-start.1 = (f32[512,512]{1,0:T(8,128)S(1)}, f32[512,512]{1,0:T(8,128)}, u32[]{:S(2)}, u32[]{:S(2)}) collective-permute-start(f32[512,512]{1,0:T(8,128)S(1)} %fusion.5), channel_id=1, source_target_pairs={{0,2},{6,4},{8,10},{14,12},{16,18},{22,20},{24,26},{30,28},{39,37}... | collective-permute-start | bytes 3145736 | tf_op jit(solution)/shard_map/ppermute | solution.py:97
  30.4 17.2 %all-to-all-start.1 = ((f32[16,16,128]{2,1,0:T(8,128)}), f32[16,16,128]{2,1,0:T(8,128)S(1)}, u32[]{:S(2)}, u32[]{:S(2)}) async-start(f32[16,16,128]{2,1,0:T(8,128)} %pad_maximum_fusion.1), calls=%async_computation.1 | async-start | bytes 262144 | tf_op jit(solution)/shard_map/all_to_all | solution.py:132
  43.1 5.4 %copy-start.12 = (f32[1,1,64,512]{3,2,1,0:T(8,128)S(1)}, f32[1,1,64,512]{3,2,1,0:T(8,128)}, u32[]{:S(2)}) copy-start(f32[1,1,64,512]{3,2,1,0:T(8,128)} %param.9) | copy-start | bytes 393220
  43.1 21.5 %collective-permute-start.3 = (f32[512,512]{1,0:T(8,128)S(1)}, f32[512,512]{1,0:T(8,128)}, u32[]{:S(2)}, u32[]{:S(2)}) collective-permute-start(f32[512,512]{1,0:T(8,128)S(1)} %fusion.5), channel_id=1, source_target_pairs={{4,2},{12,10},{20,18},{28,26},{35,37},{43,45},{51,53},{59,61},{68,... | collective-permute-start | bytes 3145736 | tf_op jit(solution)/shard_map/ppermute | solution.py:97
  47.6 18.4 %collective-permute-start.2 = (f32[512,512]{1,0:T(8,128)}, f32[512,512]{1,0:T(8,128)S(1)}, u32[]{:S(2)}, u32[]{:S(2)}) collective-permute-start(f32[512,512]{1,0:T(8,128)} %collective-permute-done.1), channel_id=1, source_target_pairs={{4,2},{12,10},{20,18},{28,26},{35,37},{43,45},{51,53},{59,61},{68,... | collective-permute-start | bytes 3145736 | tf_op jit(solution)/shard_map/ppermute | solution.py:97
  48.4 0.7 copy-start.13
  49.4 12.5 %collective-permute-start.4 = (f32[64,512]{1,0:T(8,128)S(1)}, f32[64,512]{1,0:T(8,128)S(1)}, u32[]{:S(2)}, u32[]{:S(2)}) collective-permute-start(f32[64,512]{1,0:T(8,128)S(1)} %convolution_add_fusion.9), channel_id=1, source_target_pairs={{1,0},{3,2},{5,4},{7,6},{9,8},{11,10},{13,12},{15,14},{17,16},{19,... | collective-permute-start | bytes 393224 | tf_op jit(solution)/shard_map/ppermute | solution.py:97
  61.9 0.7 copy-start.6
  62.6 11.9 %collective-permute-start.5 = (f32[64,512]{1,0:T(8,128)S(1)}, f32[64,512]{1,0:T(8,128)S(1)}, u32[]{:S(2)}, u32[]{:S(2)}) collective-permute-start(f32[64,512]{1,0:T(8,128)S(1)} %convolution_add_fusion.8), channel_id=1, source_target_pairs={{6,2},{14,10},{22,18},{30,26},{39,37},{47,45},{55,53},{63,61},{70,... | collective-permute-start | bytes 393224 | tf_op jit(solution)/shard_map/ppermute | solution.py:97
  63.2 11.2 %collective-permute-start.6 = (f32[64,512]{1,0:T(8,128)S(1)}, f32[64,512]{1,0:T(8,128)S(1)}, u32[]{:S(2)}, u32[]{:S(2)}) collective-permute-start(f32[64,512]{1,0:T(8,128)S(1)} %convolution_add_fusion.8), channel_id=1, source_target_pairs={{4,2},{12,10},{20,18},{28,26},{35,37},{43,45},{51,53},{59,61},{68,... | collective-permute-start | bytes 393224 | tf_op jit(solution)/shard_map/ppermute | solution.py:97
  63.9 10.5 %collective-permute-start.7 = (f32[64,512]{1,0:T(8,128)S(1)}, f32[64,512]{1,0:T(8,128)S(1)}, u32[]{:S(2)}, u32[]{:S(2)}) collective-permute-start(f32[64,512]{1,0:T(8,128)S(1)} %convolution_add_fusion.8), channel_id=1, source_target_pairs={{0,2},{8,10},{16,18},{24,26},{33,37},{41,45},{49,53},{57,61},{64,6... | collective-permute-start | bytes 393224 | tf_op jit(solution)/shard_map/ppermute | solution.py:97
  74.4 1.2 copy-start.8
  75.6 0.7 copy-start.5
  76.2 0.7 copy-start.9
  76.2 1.0 copy-start.11
  77.6 5.1 %copy-start.10 = (f32[64,512]{1,0:T(8,128)}, f32[64,512]{1,0:T(8,128)S(1)}, u32[]{:S(2)}) copy-start(f32[64,512]{1,0:T(8,128)S(1)} %fusion.3) | copy-start | bytes 393220
  77.6 4.0 %collective-permute-start.8 = (f32[64,512]{1,0:T(8,128)S(1)}, f32[64,512]{1,0:T(8,128)S(1)}, u32[]{:S(2)}, u32[]{:S(2)}) collective-permute-start(f32[64,512]{1,0:T(8,128)S(1)} %fusion.3), channel_id=1, source_target_pairs={{26,18},{61,53},{90,82},{125,117},{154,146},{189,181},{218,210},{2... | collective-permute-start | bytes 393224 | tf_op jit(solution)/shard_map/ppermute | solution.py:97
  78.3 15.3 %collective-permute-start.14 = (f32[512,512]{1,0:T(8,128)}, f32[512,512]{1,0:T(8,128)}, u32[]{:S(2)}, u32[]{:S(2)}) collective-permute-start(f32[512,512]{1,0:T(8,128)} %fusion.37), channel_id=1, source_target_pairs={{2,0},{10,8},{18,16},{26,24},{37,33},{45,41},{53,49},{61,57},{66,6... | collective-permute-start | bytes 3145736 | tf_op jit(solution)/shard_map/ppermute | solution.py:97
  80.0 13.7 %collective-permute-start.15 = (f32[512,512]{1,0:T(8,128)}, f32[512,512]{1,0:T(8,128)}, u32[]{:S(2)}, u32[]{:S(2)}) collective-permute-start(f32[512,512]{1,0:T(8,128)} %get-tuple-element.25), channel_id=1, source_target_pairs={{2,4},{10,12},{18,20},{26,28},{37,35},{45,43},{53,51},{61,59},{66,... | collective-permute-start | bytes 3145736 | tf_op jit(solution)/shard_map/ppermute | solution.py:97
  82.7 3.9 %collective-permute-start.9 = (f32[64,512]{1,0:T(8,128)}, f32[64,512]{1,0:T(8,128)}, u32[]{:S(2)}, u32[]{:S(2)}) collective-permute-start(f32[64,512]{1,0:T(8,128)} %convolution_add_fusion.4), channel_id=1, source_target_pairs={{18,10},{53,45},{82,74},{117,109},{146,138},{181,173},{210,202},{2... | collective-permute-start | bytes 393224 | tf_op jit(solution)/shard_map/ppermute | solution.py:97
  84.0 5.5 %collective-permute-start.16 = (f32[64,512]{1,0:T(8,128)}, f32[64,512]{1,0:T(8,128)}, u32[]{:S(2)}, u32[]{:S(2)}) collective-permute-start(f32[64,512]{1,0:T(8,128)} %copy-done.9), channel_id=1, source_target_pairs={{2,0},{10,8},{18,16},{26,24},{37,33},{45,41},{53,49},{61,57},{66,6... | collective-permute-start | bytes 393224 | tf_op jit(solution)/shard_map/ppermute | solution.py:97
  85.3 4.9 %collective-permute-start.17 = (f32[64,512]{1,0:T(8,128)}, f32[64,512]{1,0:T(8,128)}, u32[]{:S(2)}, u32[]{:S(2)}) collective-permute-start(f32[64,512]{1,0:T(8,128)} %get-tuple-element.43), channel_id=1, source_target_pairs={{2,4},{10,12},{18,20},{26,28},{37,35},{45,43},{53,51},{61,59},{66,... | collective-permute-start | bytes 393224 | tf_op jit(solution)/shard_map/ppermute | solution.py:97
  88.7 5.0 %copy-start.2 = (f32[512,512]{1,0:T(8,128)S(1)}, f32[512,512]{1,0:T(8,128)}, u32[]{:S(2)}) copy-start(f32[512,512]{1,0:T(8,128)} %get-tuple-element.23) | copy-start | bytes 3145732
  88.7 2.2 %collective-permute-start.10 = (f32[64,512]{1,0:T(8,128)}, f32[64,512]{1,0:T(8,128)S(1)}, u32[]{:S(2)}, u32[]{:S(2)}) collective-permute-start(f32[64,512]{1,0:T(8,128)} %fusion.4), channel_id=1, source_target_pairs={{10,6},{18,14},{26,22},{45,39},{53,47},{61,55},{74,70},{82,78},{90... | collective-permute-start | bytes 393224 | tf_op jit(solution)/shard_map/ppermute | solution.py:97
  89.6 3.1 %collective-permute-start.11 = (f32[64,512]{1,0:T(8,128)}, f32[64,512]{1,0:T(8,128)S(1)}, u32[]{:S(2)}, u32[]{:S(2)}) collective-permute-start(f32[64,512]{1,0:T(8,128)} %fusion.4), channel_id=1, source_target_pairs={{10,0},{18,8},{26,16},{45,33},{53,41},{61,49},{74,64},{82,72},{90,... | collective-permute-start | bytes 393224 | tf_op jit(solution)/shard_map/ppermute | solution.py:97
  90.2 2.4 %collective-permute-start.12 = (f32[64,512]{1,0:T(8,128)}, f32[64,512]{1,0:T(8,128)S(1)}, u32[]{:S(2)}, u32[]{:S(2)}) collective-permute-start(f32[64,512]{1,0:T(8,128)} %fusion.4), channel_id=1, source_target_pairs={{10,4},{18,12},{26,20},{45,35},{53,43},{61,51},{74,68},{82,76},{90... | collective-permute-start | bytes 393224 | tf_op jit(solution)/shard_map/ppermute | solution.py:97
  90.9 1.7 %collective-permute-start.13 = (f32[64,512]{1,0:T(8,128)}, f32[64,512]{1,0:T(8,128)S(1)}, u32[]{:S(2)}, u32[]{:S(2)}) collective-permute-start(f32[64,512]{1,0:T(8,128)} %fusion.4), channel_id=1, source_target_pairs={{10,2},{18,10},{26,18},{45,37},{53,45},{61,53},{74,66},{82,74},{90... | collective-permute-start | bytes 393224 | tf_op jit(solution)/shard_map/ppermute | solution.py:97
  95.2 0.9 copy-start.7
  96.6 50.0 %collective-permute-start.18 = (f32[64,512]{1,0:T(8,128)S(1)}, f32[64,512]{1,0:T(8,128)S(1)}, u32[]{:S(2)}, u32[]{:S(2)}) collective-permute-start(f32[64,512]{1,0:T(8,128)S(1)} %get-tuple-element.45), channel_id=1, source_target_pairs={{0,1},{2,3},{4,5},{6,7},{8,9},{10,11},{12,13},{14,15},{16,17},{18,... | collective-permute-start | bytes 393224 | tf_op jit(solution)/shard_map/ppermute | solution.py:97

commit v2 on v1

v2 whole, which is shorter than its diff:
```python
import jax
import jax.numpy as jnp
from jax import lax
from jax.experimental import pallas as pl
from jax.experimental.pallas import tpu as pltpu
from jax.sharding import PartitionSpec as P

STATES = 16
TEAM_STATES = 512
COLS = 64
ROBOTS = 32
LMK = 2048
TEAMS = 16
STEPS = 32
RING = 8
BOTH = ("team", "tm")

HIGH = lax.Precision.HIGH


def matmul(left, right):
    return jnp.dot(left, right, precision=HIGH)


def route(pairs_of):
    out = []
    for team in range(TEAMS):
        for ring in range(STEPS // RING):
            for src, dst in pairs_of(team % 2):
                base = team * STEPS + ring * RING
                out.append((base + src, base + dst))
    return out


def holder(pair, odd):
    return 2 * pair + odd


def partner(pair, odd):
    return 2 * pair + 1 - odd


NEAR = 0
FAR = 2


def own_pair(odd):
    return 3 if odd else 1


def last_pair(odd):
    return 1 if odd else 3


WORKER_PAIR = route(lambda odd: [(partner(own_pair(odd), odd), holder(own_pair(odd), odd))])
OTHER_PAIRS = route(
    lambda odd: [(partner(p, odd), holder(p, odd)) for p in range(4) if p != own_pair(odd)]
)
TO_HOLDER = route(lambda odd: [(partner(p, odd), holder(p, odd)) for p in range(4)])
TO_PARTNER = [(dst, src) for src, dst in TO_HOLDER]


def between(source, target, only_odd=False):
    def pairs_of(odd):
        if only_odd and not odd:
            return []
        return [(holder(source(odd), odd), holder(target(odd), odd))]

    return route(pairs_of)


def near_pair(odd):
    return NEAR


def far_pair(odd):
    return FAR


LAST_STEP = between(last_pair, far_pair)
FAR_IN = between(far_pair, own_pair)
NEAR_IN = between(near_pair, own_pair)
LAST_IN = between(last_pair, own_pair)
NEAR_OUT = between(own_pair, near_pair)
FAR_OUT = between(own_pair, far_pair)
FAR_OUT_ODD = between(own_pair, far_pair, True)
LAST_OUT_ODD = between(own_pair, last_pair, True)


def down(target):
    out = []
    for team in range(TEAMS):
        odd = team % 2
        for ring in range(1, STEPS // RING):
            base = team * STEPS + ring * RING
            out.append((base + holder(own_pair(odd), odd), base - RING + holder(target(odd), odd)))
    return out


def ring_hop(ring):
    out = []
    for team in range(TEAMS):
        z = holder(own_pair(team % 2), team % 2)
        out.append((team * STEPS + ring * RING + z, team * STEPS + (ring - 1) * RING + z))
    return out


def send(value, pairs):
    return lax.ppermute(value, BOTH, pairs)


def fold(rows):
    return jnp.concatenate([rows[..., :16, :], rows[..., 16:, :]], axis=-1)


def unfold(packed):
    return jnp.concatenate([packed[..., :64], packed[..., 64:]], axis=-2)


def split(value):
    high = value.astype(jnp.bfloat16)
    return high, (value - high.astype(jnp.float32)).astype(jnp.bfloat16)


def product(left, right, dims=(((1,), (0,)), ((), ()))):
    def one(a, b):
        return lax.dot_general(a, b, dims, preferred_element_type=jnp.float32)

    return one(left[0], right[0]) + (one(left[0], right[1]) + one(left[1], right[0]))


def compose_kernel(flag, two, last, far, near, enter1, enter0, eight, m3, m2, m1, m0, r1, r0, r8, sems, out_sems):
    def load(src, dst, k):
        return pltpu.make_async_copy(src, dst, sems.at[k])

    def store(src, dst, k):
        return pltpu.make_async_copy(src, dst, out_sems.at[k])

    @pl.when(flag[0] == 1)
    def _():
        load(last, m3, 0).start()
        load(two, m1, 2).start()

    @pl.when(flag[0] == 0)
    def _():
        load(two, m3, 0).start()
        load(last, m1, 2).start()

    load(far, m2, 1).start()
    load(near, m0, 3).start()
    load(last, m3, 0).wait()
    load(far, m2, 1).wait()
    r1[...] = product(split(m3[...]), split(m2[...]))
    store(r1, enter1, 0).start()
    load(last, m1, 2).wait()
    r0[...] = product(split(r1[...]), split(m1[...]))
    store(r0, enter0, 1).start()
    load(near, m0, 3).wait()
    r8[...] = product(split(r0[...]), split(m0[...]))
    store(r8, eight, 2).start()
    store(r1, enter1, 0).wait()
    store(r0, enter0, 1).wait()
    store(r8, eight, 2).wait()


def compose(even, two, last, far, near):
    shape = (TEAM_STATES, TEAM_STATES)
    return pl.pallas_call(
        compose_kernel,
        out_shape=[jax.ShapeDtypeStruct(shape, jnp.float32)] * 3,
        in_specs=[pl.BlockSpec(memory_space=pltpu.SMEM)] + [pl.BlockSpec(memory_space=pl.ANY)] * 4,
        out_specs=[pl.BlockSpec(memory_space=pl.ANY)] * 3,
        scratch_shapes=[pltpu.VMEM(shape, jnp.float32)] * 7
        + [pltpu.SemaphoreType.DMA((4,)), pltpu.SemaphoreType.DMA((3,))],
        name="compose",
    )(even.astype(jnp.int32)[None], two, last, far, near)


def landmark_kernel(got, part):
    rows = got[:, :ROBOTS, :].reshape(TEAMS * ROBOTS, LMK // TEAMS).astype(jnp.bfloat16)
    packed = got[:, ROBOTS:, :]
    seen = jnp.concatenate([packed[..., :COLS], packed[..., COLS:]], axis=1).reshape(TEAMS * ROBOTS, COLS)

    def one(a, b, left, right):
        return lax.dot_general(a, b, (((left,), (right,)), ((), ())), preferred_element_type=jnp.float32)

    first, second = split(seen)
    landmark = one(first, rows, 0, 0) + one(second, rows, 0, 0)
    first, second = split(landmark)
    back = (one(rows, first, 1, 1) + one(rows, second, 1, 1)).reshape(TEAMS, ROBOTS, COLS)
    part[..., :COLS] = back[:, : ROBOTS // 2, :]
    part[..., COLS:] = back[:, ROBOTS // 2 :, :]


def shards(transitions, states, cotangent, terminal, incidence, measured, obs_gain):
    matrix = transitions[0, 0]
    state = states[0, 0]
    cot = cotangent[0, 0]
    team = lax.axis_index("team")
    step = lax.axis_index("tm")
    even = team % 2 == 0
    ring = step // RING

    def pick(a, b):
        return jnp.where(even, a, b)

    other_matrix = send(matrix, TO_HOLDER)

    incident = incidence[0, 0].astype(jnp.float32)
    slices = incident.reshape(ROBOTS, TEAMS, LMK // TEAMS).transpose(1, 0, 2)
    packed = fold(measured[0, 0].T)
    packed = jnp.broadcast_to(packed[None], (TEAMS,) + packed.shape)
    got = lax.all_to_all(jnp.concatenate([slices, packed], axis=1), "team", 0, 0, tiled=True)
    part = pl.pallas_call(
        landmark_kernel,
        out_shape=jax.ShapeDtypeStruct((TEAMS, ROBOTS // 2, 2 * COLS), jnp.float32),
        name="landmark",
    )(got)
    parts = lax.all_to_all(part, "team", 0, 0, tiled=True)
    injected = jnp.sum(parts, axis=0)

    high = pick(other_matrix, matrix)
    low = pick(matrix, other_matrix)
    two = jnp.dot(high, low, precision=lax.Precision.HIGHEST)
    passing = send(two, LAST_STEP)
    two_far = send(two, FAR_IN)
    two_near = send(two, NEAR_IN)
    two_last = send(passing, FAR_IN)

    owner = jnp.arange(TEAM_STATES)[None, :] // STATES == jnp.arange(ROBOTS)[:, None]
    spread = jnp.where(owner, obs_gain[0][None, :], 0.0)
    driven = cot + jnp.einsum("rc,rn->cn", unfold(injected), spread, precision=HIGH)
    other_driven = send(driven, OTHER_PAIRS)
    own_driven = send(driven, WORKER_PAIR)

    def compose_driven(other):
        later, sooner = pick(other, driven), pick(driven, other)
        return later, matmul(later, low) + sooner

    later, offset = compose_driven(other_driven)
    off_last = send(offset, LAST_IN)
    off_far = send(offset, FAR_IN)
    off_near = send(offset, NEAR_IN)

    map1 = pick(two, two_last)
    enter1, enter0, eight = compose(even, two, two_last, two_far, two_near)
    eight, enter0, enter1, off_last, off_far, off_near = lax.optimization_barrier(
        (eight, enter0, enter1, off_last, off_far, off_near)
    )
    own_later, own_offset = compose_driven(own_driven)
    off3 = pick(off_last, own_offset)
    off1 = pick(own_offset, off_last)
    shift1 = matmul(off3, two_far) + off_far
    shift0 = matmul(shift1, map1) + off1
    total = matmul(shift0, two_near) + off_near

    last_ring = STEPS // RING - 1
    leaving = matmul(terminal[0], eight) + total
    incoming = send(leaving, ring_hop(last_ring))
    map_near = send(enter0, NEAR_OUT)
    map_far = send(two, FAR_OUT_ODD)
    map_last = send(enter1, LAST_OUT_ODD)
    shift_near = send(shift0, NEAR_OUT)
    shift_far = send(off3, FAR_OUT)
    shift_last = send(shift1, LAST_OUT_ODD)
    out = leaving
    for source in range(last_ring - 1, 0, -1):
        leaving = matmul(incoming, eight) + total
        out = jnp.where(ring == source, leaving, out)
        if source > 1:
            incoming = send(leaving, ring_hop(source))
    arrived = [
        send(out, down(last_pair)), send(out, down(near_pair)), send(out, down(far_pair)), send(out, down(own_pair))
    ]
    pair = (step % RING) // 2
    enter_map = jnp.where(pair == NEAR, map_near, jnp.where(pair == FAR, pick(passing, map_far), pick(enter1, map_last)))
    enter_shift = jnp.where(pair == NEAR, shift_near, jnp.where(pair == FAR, shift_far, pick(shift1, shift_last)))
    enter_map, enter_shift = lax.optimization_barrier((enter_map, enter_shift))
    entry = (arrived[0] + arrived[1]) + (arrived[2] + arrived[3]) + jnp.where(ring == last_ring, terminal[0], 0.0)
    entry = lax.optimization_barrier(entry)
    enter = jnp.where(pair == 3, entry, matmul(entry, enter_map) + enter_shift)
    enter = lax.optimization_barrier(enter)
    driven_high = jnp.where(pair == pick(own_pair(0), own_pair(1)), own_later, later)
    middle = matmul(enter, high) + driven_high
    passed = send(pick(enter, middle), TO_PARTNER)
    holds = step % 2 == team % 2
    running = jnp.where(holds, pick(middle, enter), passed)
    running = lax.optimization_barrier(running)
    grad = jnp.einsum("cn,cm->nm", running, state, precision=HIGH).astype(jnp.bfloat16)
    adjoint = matmul(running, matrix) + driven
    return adjoint[None, None], grad[None, None]


def solution(mesh):
    placed = (
        P("team", "tm", None, None),
        P("team", "tm", None, None),
        P("team", "tm", None, None),
        P("team", None, None),
        P("team", "tm", None, None),
        P("team", "tm", None, None),
        P("team", None),
    )
    return jax.shard_map(
        shards,
        mesh=mesh,
        in_specs=placed,
        out_specs=(P("team", "tm", None, None), P("team", "tm", None, None)),
        check_vma=False,
    )
```

time: 150 us -> 155 us (1.033)
  the two profiles are of different devices: /device:TPU:37 before, /device:TPU:1 now
where the time goes in v2:
time: 155 us; the launch traced here: 154 us
  waiting for transfers between devices  52.4 us (34%)
  starting transfers between devices  41.1 us (27%)
  blocking collectives  24.6 us (16%)
  matrix products  18.5 us (12%)
  Pallas kernels  8.11 us (5%)
  other arithmetic  5.6 us (4%)
  local copies, waits for them, and re-layouts  2.1 us (1%)
    ppermute x23, waiting for transfers between devices, send(): return lax.ppermute(value, BOTH, pairs)  49.2 us
    ppermute x23, starting transfers between devices, send(): return lax.ppermute(value, BOTH, pairs)  37.7 us
    all_to_all x1, blocking collectives, shards(): lax.all_to_all(jnp.concatenate([slices, packed], axis=1), 'team', 0, 0, t...  24.6 us
    dot_general x11, matrix products, matmul(): return jnp.dot(left, right, precision=HIGH)  13.3 us
    pallas_call x1, Pallas kernels, compose(): pl.pallas_call(compose_kernel, out_shape=[jax.ShapeDtypeStruct(shape, jnp...  5.86 us
    dot_general x1, matrix products, shards(): two = jnp.dot(high, low, precision=lax.Precision.HIGHEST)  3.47 us
    all_to_all x1, starting transfers between devices, shards(): parts = lax.all_to_all(part, 'team', 0, 0, tiled=True)  3.41 us
    all_to_all x1, waiting for transfers between devices, shards(): parts = lax.all_to_all(part, 'team', 0, 0, tiled=True)  3.21 us
  transfers between devices with their start and end apart: 24, of which 4 were waited for; matrix products, arithmetic and copies ran while one was open for 5% of the time, Pallas kernels for 5%

profile of v2, /device:TPU:1, one launch (start us, length us, event | category | flops | bytes accessed | tf_op | source)
XLA Modules:
  0.0 153.5 jit_solution(3175569765280154674)
XLA Ops:
  0.7 5.0 %collective-permute-start = (f32[512,512]{1,0:T(8,128)}, f32[512,512]{1,0:T(8,128)S(1)}, u32[]{:S(2)}, u32[]{:S(2)}) collective-permute-start(f32[512,512]{1,0:T(8,128)} %bitcast.66), channel_id=1, source_target_pairs={{1,0},{3,2},{5,4},{7,6},{9,8},{11,10},{13,12},{15,14},{17,16},{19,... | collective-permute-start | bytes 3145736 | tf_op jit(solution)/shard_map/ppermute | solution.py:109
  5.7 1.0 convert_bitcast_fusion
  6.7 11.0 %collective-permute-done = f32[512,512]{1,0:T(8,128)S(1)} collective-permute-done((f32[512,512]{1,0:T(8,128)}, f32[512,512]{1,0:T(8,128)S(1)}, u32[]{:S(2)}, u32[]{:S(2)}) %collective-permute-start) | collective-permute-done | bytes 1048608 | tf_op jit(solution)/shard_map/ppermute | solution.py:109
  17.7 3.5 %fusion.7.two = f32[512,512]{1,0:T(8,128)S(1)} fusion(f32[512,512]{1,0:T(8,128)S(1)} %collective-permute-done, pred[]{:T(512)S(6)} %eq.48, f32[1,1,512,512]{3,2,1,0:T(8,128)} %param.7), kind=kOutput, calls=%fused_computation.23 | convolution fusion | flops 1611137024 | bytes 3145729 | tf_op jit(solution)/shard_map/dot_general | solution.py:224
  21.1 1.7 %collective-permute-start.1 = (f32[512,512]{1,0:T(8,128)S(1)}, f32[512,512]{1,0:T(8,128)}, u32[]{:S(2)}, u32[]{:S(2)}) collective-permute-start(f32[512,512]{1,0:T(8,128)S(1)} %fusion.7.two), channel_id=1, source_target_pairs={{6,4},{14,12},{22,20},{30,28},{35,37},{43,45},{51,53},{59,61},{70,... | collective-permute-start | bytes 3145736 | tf_op jit(solution)/shard_map/ppermute | solution.py:109
  23.1 24.6 %all_to_all.10.got = f32[16,48,128]{2,1,0:T(8,128)} all-to-all(f32[16,48,128]{2,1,0:T(8,128)S(1)} %pad_maximum_fusion), channel_id=1, replica_groups=mesh['team'=16,'tm'=32] {'team'}, dimensions={0} | all-to-all | bytes 786432 | tf_op jit(solution)/shard_map/all_to_all | solution.py:213
  47.7 2.2 %landmark.1 = f32[16,16,128]{2,1,0:T(8,128)} custom-call(f32[16,48,128]{2,1,0:T(8,128)} %all_to_all.10.got), custom_call_target="tpu_custom_call" | custom-call | tf_op jit(solution)/shard_map/landmark/pallas_call | solution.py:214
  50.0 3.4 %all-to-all-start.1 = ((f32[16,16,128]{2,1,0:T(8,128)}), f32[16,16,128]{2,1,0:T(8,128)S(1)}, u32[]{:S(2)}, u32[]{:S(2)}) async-start(f32[16,16,128]{2,1,0:T(8,128)} %landmark.1), calls=%async_computation.1 | async-start | bytes 262144 | tf_op jit(solution)/shard_map/all_to_all | solution.py:219
  53.4 1.9 %collective-permute-start.3 = (f32[512,512]{1,0:T(8,128)S(1)}, f32[512,512]{1,0:T(8,128)}, u32[]{:S(2)}, u32[]{:S(2)}) collective-permute-start(f32[512,512]{1,0:T(8,128)S(1)} %fusion.7.two), channel_id=1, source_target_pairs={{4,2},{12,10},{20,18},{28,26},{37,39},{45,47},{53,55},{61,63},{68,... | collective-permute-start | bytes 3145736 | tf_op jit(solution)/shard_map/ppermute | solution.py:109
  55.3 1.7 %collective-permute-start.4 = (f32[512,512]{1,0:T(8,128)S(1)}, f32[512,512]{1,0:T(8,128)}, u32[]{:S(2)}, u32[]{:S(2)}) collective-permute-start(f32[512,512]{1,0:T(8,128)S(1)} %fusion.7.two), channel_id=1, source_target_pairs={{0,2},{8,10},{16,18},{24,26},{33,39},{41,47},{49,55},{57,63},{64,6... | collective-permute-start | bytes 3145736 | tf_op jit(solution)/shard_map/ppermute | solution.py:109
  56.9 1.6 %collective-permute-start.2 = (f32[512,512]{1,0:T(8,128)}, f32[512,512]{1,0:T(8,128)}, u32[]{:S(2)}, u32[]{:S(2)}) collective-permute-start(f32[512,512]{1,0:T(8,128)} %collective-permute-done.1), channel_id=1, source_target_pairs={{4,2},{12,10},{20,18},{28,26},{37,39},{45,47},{53,55},{61,63},{68,... | collective-permute-start | bytes 3145736 | tf_op jit(solution)/shard_map/ppermute | solution.py:109
  58.6 3.2 %all-to-all-done.1 = f32[16,16,128]{2,1,0:T(8,128)S(1)} async-done(((f32[16,16,128]{2,1,0:T(8,128)}), f32[16,16,128]{2,1,0:T(8,128)S(1)}, u32[]{:S(2)}, u32[]{:S(2)}) %all-to-all-start.1) | async-done | bytes 131104 | tf_op jit(solution)/shard_map/all_to_all | solution.py:219
  61.9 0.7 copy-done.16
  62.8 6.3 %collective-permute-start.5 = (f32[64,512]{1,0:T(8,128)S(1)}, f32[64,512]{1,0:T(8,128)S(1)}, u32[]{:S(2)}, u32[]{:S(2)}) collective-permute-start(f32[64,512]{1,0:T(8,128)S(1)} %convolution_add_fusion.10), channel_id=1, source_target_pairs={{1,0},{5,4},{7,6},{9,8},{13,12},{15,14},{17,16},{21,20},{23,22},{2... | collective-permute-start | bytes 393224 | tf_op jit(solution)/shard_map/ppermute | solution.py:109
  69.1 3.3 %collective-permute-done.5 = f32[64,512]{1,0:T(8,128)S(1)} collective-permute-done((f32[64,512]{1,0:T(8,128)S(1)}, f32[64,512]{1,0:T(8,128)S(1)}, u32[]{:S(2)}, u32[]{:S(2)}) %collective-permute-start.5) | collective-permute-done | bytes 131104 | tf_op jit(solution)/shard_map/ppermute | solution.py:109
  72.4 1.1 convolution_add_fusion.9
  73.5 0.7 collective-permute-start.6
  74.2 1.3 collective-permute-start.7
  75.5 1.3 collective-permute-start.8
  76.8 0.7 collective-permute-start.9
  77.5 5.9 %compose.1 = (f32[512,512]{1,0:T(8,128)}, f32[512,512]{1,0:T(8,128)}, f32[512,512]{1,0:T(8,128)}) custom-call(s32[1]{0:T(128)} %bitcast.flag, f32[512,512]{1,0:T(8,128)} %copy-done.2, f32[512,512]{1,0:T(8,128)} %collective-permute-done.2.last, f32[512,512]{1,0:T(8,128)} %collective-permute-done.3.far, f32[512,512]{1,0:T(8,128)} %collective-permute-done.4.near), custom_call_target="tpu_custom_call" | custom-call | tf_op jit(solution)/shard_map/compose/pallas_call | solution.py:168
  83.4 0.6 copy-done.8
  84.5 1.7 %convolution_add_fusion.7 = f32[64,512]{1,0:T(8,128)S(1)} fusion(f32[64,512]{1,0:T(8,128)} %collective-permute-done.7, f32[64,512]{1,0:T(8,128)S(1)} %get-tuple-element.28, f32[512,512]{1,0:T(8,128)} %collective-permute-done.3.far), kind=kOutput, calls=%fused_computation.11 | convolution fusion | flops 100696064 | bytes 1441792 | tf_op jit(solution)/shard_map/dot_general | solution.py:22
  86.3 2.4 %convolution_add_fusion.6 = f32[64,512]{1,0:T(8,128)} fusion(f32[64,512]{1,0:T(8,128)S(1)} %convolution_add_fusion.7, f32[512,512]{1,0:T(8,128)S(1)} %copy-done.3, f32[512,512]{1,0:T(8,128)} %collective-permute-done.2.last, pred[]{:T(512)S(6)} %eq.48, f32[64,512]{1,0:T(8,128)S(1)} %get-tuple-element.29, f32[64,512]{1,0:T(8,128)S(1)} %collective-permute-done.6), kind=kOutput, calls=%fused_computation.10 | convolution fusion | flops 100990976 | bytes 2621441 | tf_op jit(solution)/shard_map/dot_general | solution.py:22
  88.7 1.8 %convolution_add_fusion.5 = f32[64,512]{1,0:T(8,128)S(1)} fusion(f32[64,512]{1,0:T(8,128)} %collective-permute-done.8, f32[64,512]{1,0:T(8,128)} %convolution_add_fusion.6, f32[512,512]{1,0:T(8,128)} %collective-permute-done.4.near), kind=kOutput, calls=%fused_computation.9 | convolution fusion | flops 100696064 | bytes 1441792 | tf_op jit(solution)/shard_map/dot_general | solution.py:22
  90.9 0.7 collective-permute-start.10
  91.6 1.7 %collective-permute-start.17 = (f32[512,512]{1,0:T(8,128)S(1)}, f32[512,512]{1,0:T(8,128)}, u32[]{:S(2)}, u32[]{:S(2)}) collective-permute-start(f32[512,512]{1,0:T(8,128)S(1)} %copy-done.3), channel_id=1, source_target_pairs={{39,37},{47,45},{55,53},{63,61},{103,101},{111,109},{119,117},{127... | collective-permute-start | bytes 3145736 | tf_op jit(solution)/shard_map/ppermute | solution.py:109
  93.3 1.3 collective-permute-start.19
  94.6 1.7 %collective-permute-start.16 = (f32[512,512]{1,0:T(8,128)}, f32[512,512]{1,0:T(8,128)}, u32[]{:S(2)}, u32[]{:S(2)}) collective-permute-start(f32[512,512]{1,0:T(8,128)} %get-tuple-element.20), channel_id=1, source_target_pairs={{2,0},{10,8},{18,16},{26,24},{39,33},{47,41},{55,49},{63,57},{66,6... | collective-permute-start | bytes 3145736 | tf_op jit(solution)/shard_map/ppermute | solution.py:109
  96.3 1.6 %collective-permute-start.18 = (f32[512,512]{1,0:T(8,128)}, f32[512,512]{1,0:T(8,128)}, u32[]{:S(2)}, u32[]{:S(2)}) collective-permute-start(f32[512,512]{1,0:T(8,128)} %get-tuple-element.21), channel_id=1, source_target_pairs={{39,35},{47,43},{55,51},{63,59},{103,99},{111,107},{119,115},{127,... | collective-permute-start | bytes 3145736 | tf_op jit(solution)/shard_map/ppermute | solution.py:109
  97.9 1.1 convolution_add_fusion.4
  99.0 1.3 collective-permute-start.11
  100.4 1.3 collective-permute-start.21
  101.7 1.3 collective-permute-start.20
  103.0 2.4 %fusion.4 = f32[64,512]{1,0:T(8,128)} fusion(f32[64,512]{1,0:T(8,128)S(1)} %convolution_add_fusion.5, f32[64,512]{1,0:T(8,128)} %collective-permute-done.11, f32[512,512]{1,0:T(8,128)} %get-tuple-element.16, f32[64,512]{1,0:T(8,128)} %convolution_add_fusion.4, f32[64,512]{1,0:T(8,128)} %copy-done.11, pred[]{:T(512)S(6)} %eq.54, pred[]{:T(512)S(6)} %eq.50), kind=kOutput, calls=%fused_computation.16 | convolution fusion | flops 100761600 | bytes 1703938 | tf_op jit(solution)/shard_map/dot_general | solution.py:22
  105.4 0.7 collective-permute-start.12
  106.0 1.3 collective-permute-start.13
  107.4 0.8 collective-permute-start.14
  108.2 0.7 collective-permute-start.15
  108.9 1.0 select_select_fusion.2
  109.9 1.0 fusion.10
  110.9 2.5 %select_select_fusion = f32[512,512]{1,0:T(8,128)S(1)} fusion(f32[512,512]{1,0:T(8,128)} %collective-permute-done.16, f32[512,512]{1,0:T(8,128)} %get-tuple-element.21, f32[512,512]{1,0:T(8,128)} %collective-permute-done.18, f32[512,512]{1,0:T(8,128)} %collective-permute-done.1, f32[512,512]{1,0:T(8,128)} %collective-permute-done.17, pred[]{:T(512)S(6)} %eq.57, ...), kind=kLoop, calls=%fused_computation.18 | loop fusion | flops 1048576 | bytes 6291459 | tf_op jit(solution)/shard_map/jit(_where)/select_n | solution.py:276
  113.4 0.5 fusion.2
  114.4 0.4 broadcast_select_fusion.4
  114.8 1.3 collective-permute-start.22
  116.1 34.9 %collective-permute-done.22 = f32[64,512]{1,0:T(8,128)S(1)} collective-permute-done((f32[64,512]{1,0:T(8,128)S(1)}, f32[64,512]{1,0:T(8,128)S(1)}, u32[]{:S(2)}, u32[]{:S(2)}) %collective-permute-start.22) | collective-permute-done | bytes 131104 | tf_op jit(solution)/shard_map/ppermute | solution.py:109
  151.0 1.1 fusion.1
  152.1 1.4 fusion
  (65 shorter events, 2.1 us)
Async XLA Ops:
  0.6 151.5 %copy-start = (f32[1,1,64,512]{3,2,1,0:T(8,128)S(1)}, f32[1,1,64,512]{3,2,1,0:T(8,128)}, u32[]{:S(2)}) copy-start(f32[1,1,64,512]{3,2,1,0:T(8,128)} %param.8) | copy-start | bytes 393220
  0.6 5.0 %copy-start.15 = (f32[1,1,64,32]{2,3,1,0:T(8,128)S(1)}, f32[1,1,64,32]{2,3,1,0:T(8,128)}, u32[]{:S(2)}) copy-start(f32[1,1,64,32]{2,3,1,0:T(8,128)} %param.12) | copy-start | bytes 24580
  0.7 17.0 %collective-permute-start = (f32[512,512]{1,0:T(8,128)}, f32[512,512]{1,0:T(8,128)S(1)}, u32[]{:S(2)}, u32[]{:S(2)}) collective-permute-start(f32[512,512]{1,0:T(8,128)} %bitcast.66), channel_id=1, source_target_pairs={{1,0},{3,2},{5,4},{7,6},{9,8},{11,10},{13,12},{15,14},{17,16},{19,... | collective-permute-start | bytes 3145736 | tf_op jit(solution)/shard_map/ppermute | solution.py:109
  21.1 34.1 %copy-start.2 = (f32[512,512]{1,0:T(8,128)}, f32[512,512]{1,0:T(8,128)S(1)}, u32[]{:S(2)}) copy-start(f32[512,512]{1,0:T(8,128)S(1)} %fusion.7.two) | copy-start | bytes 3145732
  21.1 35.8 %collective-permute-start.1 = (f32[512,512]{1,0:T(8,128)S(1)}, f32[512,512]{1,0:T(8,128)}, u32[]{:S(2)}, u32[]{:S(2)}) collective-permute-start(f32[512,512]{1,0:T(8,128)S(1)} %fusion.7.two), channel_id=1, source_target_pairs={{6,4},{14,12},{22,20},{30,28},{35,37},{43,45},{51,53},{59,61},{70,... | collective-permute-start | bytes 3145736 | tf_op jit(solution)/shard_map/ppermute | solution.py:109
  23.1 49.3 %copy-start.1 = (f32[1,1,512,512]{3,2,1,0:T(8,128)S(1)}, f32[1,1,512,512]{3,2,1,0:T(8,128)}, u32[]{:S(2)}) copy-start(f32[1,1,512,512]{3,2,1,0:T(8,128)} %param.7) | copy-start | bytes 3145732
  50.0 11.8 %all-to-all-start.1 = ((f32[16,16,128]{2,1,0:T(8,128)}), f32[16,16,128]{2,1,0:T(8,128)S(1)}, u32[]{:S(2)}, u32[]{:S(2)}) async-start(f32[16,16,128]{2,1,0:T(8,128)} %landmark.1), calls=%async_computation.1 | async-start | bytes 262144 | tf_op jit(solution)/shard_map/all_to_all | solution.py:219
  53.4 8.5 %copy-start.14 = (f32[1,1,64,512]{3,2,1,0:T(8,128)S(1)}, f32[1,1,64,512]{3,2,1,0:T(8,128)}, u32[]{:S(2)}) copy-start(f32[1,1,64,512]{3,2,1,0:T(8,128)} %param.9) | copy-start | bytes 393220
  53.4 22.1 %collective-permute-start.3 = (f32[512,512]{1,0:T(8,128)S(1)}, f32[512,512]{1,0:T(8,128)}, u32[]{:S(2)}, u32[]{:S(2)}) collective-permute-start(f32[512,512]{1,0:T(8,128)S(1)} %fusion.7.two), channel_id=1, source_target_pairs={{4,2},{12,10},{20,18},{28,26},{37,39},{45,47},{53,55},{61,63},{68,... | collective-permute-start | bytes 3145736 | tf_op jit(solution)/shard_map/ppermute | solution.py:109
  55.3 21.6 %collective-permute-start.4 = (f32[512,512]{1,0:T(8,128)S(1)}, f32[512,512]{1,0:T(8,128)}, u32[]{:S(2)}, u32[]{:S(2)}) collective-permute-start(f32[512,512]{1,0:T(8,128)S(1)} %fusion.7.two), channel_id=1, source_target_pairs={{0,2},{8,10},{16,18},{24,26},{33,39},{41,47},{49,55},{57,63},{64,6... | collective-permute-start | bytes 3145736 | tf_op jit(solution)/shard_map/ppermute | solution.py:109
  56.9 20.6 %collective-permute-start.2 = (f32[512,512]{1,0:T(8,128)}, f32[512,512]{1,0:T(8,128)}, u32[]{:S(2)}, u32[]{:S(2)}) collective-permute-start(f32[512,512]{1,0:T(8,128)} %collective-permute-done.1), channel_id=1, source_target_pairs={{4,2},{12,10},{20,18},{28,26},{37,39},{45,47},{53,55},{61,63},{68,... | collective-permute-start | bytes 3145736 | tf_op jit(solution)/shard_map/ppermute | solution.py:109
  61.9 0.7 copy-start.16
  62.8 9.6 %collective-permute-start.5 = (f32[64,512]{1,0:T(8,128)S(1)}, f32[64,512]{1,0:T(8,128)S(1)}, u32[]{:S(2)}, u32[]{:S(2)}) collective-permute-start(f32[64,512]{1,0:T(8,128)S(1)} %convolution_add_fusion.10), channel_id=1, source_target_pairs={{1,0},{5,4},{7,6},{9,8},{13,12},{15,14},{17,16},{21,20},{23,22},{2... | collective-permute-start | bytes 393224 | tf_op jit(solution)/shard_map/ppermute | solution.py:109
  72.4 1.1 copy-start.6
  73.5 9.9 %collective-permute-start.6 = (f32[64,512]{1,0:T(8,128)}, f32[64,512]{1,0:T(8,128)S(1)}, u32[]{:S(2)}, u32[]{:S(2)}) collective-permute-start(f32[64,512]{1,0:T(8,128)} %convolution_add_fusion.9), channel_id=1, source_target_pairs={{6,2},{14,10},{22,18},{30,26},{35,39},{43,47},{51,55},{59,63},{70,... | collective-permute-start | bytes 393224 | tf_op jit(solution)/shard_map/ppermute | solution.py:109
  74.2 9.2 %collective-permute-start.7 = (f32[64,512]{1,0:T(8,128)}, f32[64,512]{1,0:T(8,128)}, u32[]{:S(2)}, u32[]{:S(2)}) collective-permute-start(f32[64,512]{1,0:T(8,128)} %convolution_add_fusion.9), channel_id=1, source_target_pairs={{4,2},{12,10},{20,18},{28,26},{37,39},{45,47},{53,55},{61,63},{68,... | collective-permute-start | bytes 393224 | tf_op jit(solution)/shard_map/ppermute | solution.py:109
  75.5 7.9 %collective-permute-start.8 = (f32[64,512]{1,0:T(8,128)}, f32[64,512]{1,0:T(8,128)}, u32[]{:S(2)}, u32[]{:S(2)}) collective-permute-start(f32[64,512]{1,0:T(8,128)} %convolution_add_fusion.9), channel_id=1, source_target_pairs={{0,2},{8,10},{16,18},{24,26},{33,39},{41,47},{49,55},{57,63},{64,6... | collective-permute-start | bytes 393224 | tf_op jit(solution)/shard_map/ppermute | solution.py:109
  76.8 6.6 %collective-permute-start.9 = (f32[64,512]{1,0:T(8,128)S(1)}, f32[64,512]{1,0:T(8,128)S(1)}, u32[]{:S(2)}, u32[]{:S(2)}) collective-permute-start(f32[64,512]{1,0:T(8,128)S(1)} %convolution_add_fusion.10), channel_id=1, source_target_pairs={{3,2},{11,10},{19,18},{27,26},{38,39},{46,47},{54,55},{62,63},{67,... | collective-permute-start | bytes 393224 | tf_op jit(solution)/shard_map/ppermute | solution.py:109
  83.4 0.7 copy-start.8
  84.5 1.8 %copy-start.10 = (f32[64,512]{1,0:T(8,128)}, f32[64,512]{1,0:T(8,128)S(1)}, u32[]{:S(2)}) copy-start(f32[64,512]{1,0:T(8,128)S(1)} %get-tuple-element.28) | copy-start | bytes 393220
  84.5 1.8 %copy-start.3 = (f32[512,512]{1,0:T(8,128)S(1)}, f32[512,512]{1,0:T(8,128)}, u32[]{:S(2)}) copy-start(f32[512,512]{1,0:T(8,128)} %copy-done.2) | copy-start | bytes 3145732
  86.3 2.4 %copy-start.5 = (f32[64,512]{1,0:T(8,128)}, f32[64,512]{1,0:T(8,128)S(1)}, u32[]{:S(2)}) copy-start(f32[64,512]{1,0:T(8,128)S(1)} %convolution_add_fusion.7) | copy-start | bytes 393220
  88.7 1.8 %copy-start.4 = (f32[512,512]{1,0:T(8,128)S(1)}, f32[512,512]{1,0:T(8,128)}, u32[]{:S(2)}) copy-start(f32[512,512]{1,0:T(8,128)} %get-tuple-element.16) | copy-start | bytes 3145732
  88.7 1.8 %copy-start.12 = (f32[1,64,512]{2,1,0:T(8,128)S(1)}, f32[1,64,512]{2,1,0:T(8,128)}, u32[]{:S(2)}) copy-start(f32[1,64,512]{2,1,0:T(8,128)} %param.10) | copy-start | bytes 393220
  90.9 8.1 %copy-start.11 = (f32[64,512]{1,0:T(8,128)}, f32[64,512]{1,0:T(8,128)S(1)}, u32[]{:S(2)}) copy-start(f32[64,512]{1,0:T(8,128)S(1)} %fusion.3) | copy-start | bytes 393220
  90.9 7.0 %collective-permute-start.10 = (f32[64,512]{1,0:T(8,128)S(1)}, f32[64,512]{1,0:T(8,128)S(1)}, u32[]{:S(2)}, u32[]{:S(2)}) collective-permute-start(f32[64,512]{1,0:T(8,128)S(1)} %fusion.3), channel_id=1, source_target_pairs={{26,18},{63,55},{90,82},{127,119},{154,146},{191,183},{218,210},{2... | collective-permute-start | bytes 393224 | tf_op jit(solution)/shard_map/ppermute | solution.py:109
  91.6 19.3 %collective-permute-start.17 = (f32[512,512]{1,0:T(8,128)S(1)}, f32[512,512]{1,0:T(8,128)}, u32[]{:S(2)}, u32[]{:S(2)}) collective-permute-start(f32[512,512]{1,0:T(8,128)S(1)} %copy-done.3), channel_id=1, source_target_pairs={{39,37},{47,45},{55,53},{63,61},{103,101},{111,109},{119,117},{127... | collective-permute-start | bytes 3145736 | tf_op jit(solution)/shard_map/ppermute | solution.py:109
  93.3 7.1 %collective-permute-start.19 = (f32[64,512]{1,0:T(8,128)}, f32[64,512]{1,0:T(8,128)}, u32[]{:S(2)}, u32[]{:S(2)}) collective-permute-start(f32[64,512]{1,0:T(8,128)} %convolution_add_fusion.6), channel_id=1, source_target_pairs={{2,0},{10,8},{18,16},{26,24},{39,33},{47,41},{55,49},{63,57},{66,6... | collective-permute-start | bytes 393224 | tf_op jit(solution)/shard_map/ppermute | solution.py:109
  94.6 16.3 %collective-permute-start.16 = (f32[512,512]{1,0:T(8,128)}, f32[512,512]{1,0:T(8,128)}, u32[]{:S(2)}, u32[]{:S(2)}) collective-permute-start(f32[512,512]{1,0:T(8,128)} %get-tuple-element.20), channel_id=1, source_target_pairs={{2,0},{10,8},{18,16},{26,24},{39,33},{47,41},{55,49},{63,57},{66,6... | collective-permute-start | bytes 3145736 | tf_op jit(solution)/shard_map/ppermute | solution.py:109
  96.3 14.6 %collective-permute-start.18 = (f32[512,512]{1,0:T(8,128)}, f32[512,512]{1,0:T(8,128)}, u32[]{:S(2)}, u32[]{:S(2)}) collective-permute-start(f32[512,512]{1,0:T(8,128)} %get-tuple-element.21), channel_id=1, source_target_pairs={{39,35},{47,43},{55,51},{63,59},{103,99},{111,107},{119,115},{127,... | collective-permute-start | bytes 3145736 | tf_op jit(solution)/shard_map/ppermute | solution.py:109
  99.0 2.6 %collective-permute-start.11 = (f32[64,512]{1,0:T(8,128)}, f32[64,512]{1,0:T(8,128)}, u32[]{:S(2)}, u32[]{:S(2)}) collective-permute-start(f32[64,512]{1,0:T(8,128)} %convolution_add_fusion.4), channel_id=1, source_target_pairs={{18,10},{55,47},{82,74},{119,111},{146,138},{183,175},{210,202},{2... | collective-permute-start | bytes 393224 | tf_op jit(solution)/shard_map/ppermute | solution.py:109
  100.4 5.0 %collective-permute-start.21 = (f32[64,512]{1,0:T(8,128)}, f32[64,512]{1,0:T(8,128)}, u32[]{:S(2)}, u32[]{:S(2)}) collective-permute-start(f32[64,512]{1,0:T(8,128)} %copy-done.5), channel_id=1, source_target_pairs={{39,35},{47,43},{55,51},{63,59},{103,99},{111,107},{119,115},{127,... | collective-permute-start | bytes 393224 | tf_op jit(solution)/shard_map/ppermute | solution.py:109
  101.7 4.4 %collective-permute-start.20 = (f32[64,512]{1,0:T(8,128)}, f32[64,512]{1,0:T(8,128)}, u32[]{:S(2)}, u32[]{:S(2)}) collective-permute-start(f32[64,512]{1,0:T(8,128)} %copy-done.10), channel_id=1, source_target_pairs={{2,4},{10,12},{18,20},{26,28},{39,37},{47,45},{55,53},{63,61},{66,... | collective-permute-start | bytes 393224 | tf_op jit(solution)/shard_map/ppermute | solution.py:109
  105.4 2.0 %collective-permute-start.12 = (f32[64,512]{1,0:T(8,128)}, f32[64,512]{1,0:T(8,128)S(1)}, u32[]{:S(2)}, u32[]{:S(2)}) collective-permute-start(f32[64,512]{1,0:T(8,128)} %fusion.4), channel_id=1, source_target_pairs={{10,6},{18,14},{26,22},{47,35},{55,43},{63,51},{74,70},{82,78},{90... | collective-permute-start | bytes 393224 | tf_op jit(solution)/shard_map/ppermute | solution.py:109
  106.0 2.1 %collective-permute-start.13 = (f32[64,512]{1,0:T(8,128)}, f32[64,512]{1,0:T(8,128)}, u32[]{:S(2)}, u32[]{:S(2)}) collective-permute-start(f32[64,512]{1,0:T(8,128)} %fusion.4), channel_id=1, source_target_pairs={{10,0},{18,8},{26,16},{47,33},{55,41},{63,49},{74,64},{82,72},{90,... | collective-permute-start | bytes 393224 | tf_op jit(solution)/shard_map/ppermute | solution.py:109
  107.4 2.5 %copy-start.13 = (f32[1,64,512]{2,1,0:T(8,128)S(1)}, f32[1,64,512]{2,1,0:T(8,128)}, u32[]{:S(2)}) copy-start(f32[1,64,512]{2,1,0:T(8,128)} %param.10) | copy-start | bytes 393220
  107.4 2.5 %collective-permute-start.14 = (f32[64,512]{1,0:T(8,128)}, f32[64,512]{1,0:T(8,128)S(1)}, u32[]{:S(2)}, u32[]{:S(2)}) collective-permute-start(f32[64,512]{1,0:T(8,128)} %fusion.4), channel_id=1, source_target_pairs={{10,4},{18,12},{26,20},{47,37},{55,45},{63,53},{74,68},{82,76},{90... | collective-permute-start | bytes 393224 | tf_op jit(solution)/shard_map/ppermute | solution.py:109
  108.2 1.7 %collective-permute-start.15 = (f32[64,512]{1,0:T(8,128)}, f32[64,512]{1,0:T(8,128)S(1)}, u32[]{:S(2)}, u32[]{:S(2)}) collective-permute-start(f32[64,512]{1,0:T(8,128)} %fusion.4), channel_id=1, source_target_pairs={{10,2},{18,10},{26,18},{47,39},{55,47},{63,55},{74,66},{82,74},{90... | collective-permute-start | bytes 393224 | tf_op jit(solution)/shard_map/ppermute | solution.py:109
  113.4 0.9 copy-start.7
  113.4 1.0 copy-start.9
  114.8 36.2 %collective-permute-start.22 = (f32[64,512]{1,0:T(8,128)S(1)}, f32[64,512]{1,0:T(8,128)S(1)}, u32[]{:S(2)}, u32[]{:S(2)}) collective-permute-start(f32[64,512]{1,0:T(8,128)S(1)} %get-tuple-element.30), channel_id=1, source_target_pairs={{0,1},{2,3},{4,5},{6,7},{8,9},{10,11},{12,13},{14,15},{16,17},{18,... | collective-permute-start | bytes 393224 | tf_op jit(solution)/shard_map/ppermute | solution.py:109

commit v3 on v2

--- a/solution.py
+++ b/solution.py
@@ -129,19 +129,20 @@
     return one(left[0], right[0]) + (one(left[0], right[1]) + one(left[1], right[0]))
 
 
+def copier(sems):
+    return lambda src, dst, k: pltpu.make_async_copy(src, dst, sems.at[k])
+
+
 def compose_kernel(flag, two, last, far, near, enter1, enter0, eight, m3, m2, m1, m0, r1, r0, r8, sems, out_sems):
-    def load(src, dst, k):
-        return pltpu.make_async_copy(src, dst, sems.at[k])
-
-    def store(src, dst, k):
-        return pltpu.make_async_copy(src, dst, out_sems.at[k])
-
-    @pl.when(flag[0] == 1)
+    load, store = copier(sems), copier(out_sems)
+    even = flag[0] == 1
+
+    @pl.when(even)
     def _():
         load(last, m3, 0).start()
         load(two, m1, 2).start()
 
-    @pl.when(flag[0] == 0)
+    @pl.when(jnp.logical_not(even))
     def _():
         load(two, m3, 0).start()
         load(last, m1, 2).start()
@@ -163,17 +164,87 @@
     store(r8, eight, 2).wait()
 
 
-def compose(even, two, last, far, near):
-    shape = (TEAM_STATES, TEAM_STATES)
+SQUARE = (TEAM_STATES, TEAM_STATES)
+ROWS = (COLS, TEAM_STATES)
+
+
+def compose(flag, two, last, far, near):
     return pl.pallas_call(
         compose_kernel,
-        out_shape=[jax.ShapeDtypeStruct(shape, jnp.float32)] * 3,
+        out_shape=[jax.ShapeDtypeStruct(SQUARE, jnp.float32)] * 3,
         in_specs=[pl.BlockSpec(memory_space=pltpu.SMEM)] + [pl.BlockSpec(memory_space=pl.ANY)] * 4,
         out_specs=[pl.BlockSpec(memory_space=pl.ANY)] * 3,
-        scratch_shapes=[pltpu.VMEM(shape, jnp.float32)] * 7
+        scratch_shapes=[pltpu.VMEM(SQUARE, jnp.float32)] * 7
         + [pltpu.SemaphoreType.DMA((4,)), pltpu.SemaphoreType.DMA((3,))],
         name="compose",
-    )(even.astype(jnp.int32)[None], two, last, far, near)
+    )(flag, two, last, far, near)
+
+
+def shift_kernel(
+    flag, two, last, far, near, eight, off_own, off_last, off_far, off_near, start,
+    shift2, shift1, shift0, total, leaving, m2, m1, m0, m8, sems,
+):
+    load = copier(sems)
+    even = flag[0] == 1
+    load(far, m2, 0).start()
+
+    @pl.when(even)
+    def _():
+        load(two, m1, 1).start()
+
+    @pl.when(jnp.logical_not(even))
+    def _():
+        load(last, m1, 1).start()
+
+    load(near, m0, 2).start()
+    load(eight, m8, 3).start()
+    moved = jnp.where(even, off_last[...], off_own[...])
+    off1 = jnp.where(even, off_own[...], off_last[...])
+    shift2[...] = moved
+    load(far, m2, 0).wait()
+    moved = product(split(moved), split(m2[...])) + off_far[...]
+    shift1[...] = moved
+    load(last, m1, 1).wait()
+    moved = product(split(moved), split(m1[...])) + off1
+    shift0[...] = moved
+    load(near, m0, 2).wait()
+    moved = product(split(moved), split(m0[...])) + off_near[...]
+    total[...] = moved
+    load(eight, m8, 3).wait()
+    leaving[...] = product(split(start[...]), split(m8[...])) + moved
+
+
+def shift(flag, maps, rows):
+    return pl.pallas_call(
+        shift_kernel,
+        out_shape=[jax.ShapeDtypeStruct(ROWS, jnp.float32)] * 5,
+        in_specs=[pl.BlockSpec(memory_space=pltpu.SMEM)]
+        + [pl.BlockSpec(memory_space=pl.ANY)] * 5
+        + [pl.BlockSpec(memory_space=pltpu.VMEM)] * 5,
+        out_specs=[pl.BlockSpec(memory_space=pltpu.VMEM)] * 5,
+        scratch_shapes=[pltpu.VMEM(SQUARE, jnp.float32)] * 4 + [pltpu.SemaphoreType.DMA((4,))],
+        name="shift",
+    )(flag, *maps, *rows)
+
+
+def hop_kernel(flag, arrived, eight, total, kept, out):
+    @pl.when(flag[0] == 1)
+    def _():
+        out[...] = product(split(arrived[...]), split(eight[...])) + total[...]
+
+    @pl.when(flag[0] == 0)
+    def _():
+        out[...] = kept[...]
+
+
+def hop(flag, arrived, eight, total, kept):
+    return pl.pallas_call(
+        hop_kernel,
+        out_shape=jax.ShapeDtypeStruct(ROWS, jnp.float32),
+        in_specs=[pl.BlockSpec(memory_space=pltpu.SMEM)] + [pl.BlockSpec(memory_space=pltpu.VMEM)] * 4,
+        out_specs=pl.BlockSpec(memory_space=pltpu.VMEM),
+        name="hop",
+    )(flag, arrived, eight, total, kept)
 
 
 def landmark_kernel(got, part):
@@ -228,7 +299,7 @@
     two_last = send(passing, FAR_IN)
 
     owner = jnp.arange(TEAM_STATES)[None, :] // STATES == jnp.arange(ROBOTS)[:, None]
-    spread = jnp.where(owner, obs_gain[0][None, :], 0.0)
+    spread = lax.optimization_barrier(jnp.where(owner, obs_gain[0][None, :], 0.0))
     driven = cot + jnp.einsum("rc,rn->cn", unfold(injected), spread, precision=HIGH)
     other_driven = send(driven, OTHER_PAIRS)
     own_driven = send(driven, WORKER_PAIR)
@@ -242,20 +313,16 @@
     off_far = send(offset, FAR_IN)
     off_near = send(offset, NEAR_IN)
 
-    map1 = pick(two, two_last)
-    enter1, enter0, eight = compose(even, two, two_last, two_far, two_near)
-    eight, enter0, enter1, off_last, off_far, off_near = lax.optimization_barrier(
-        (eight, enter0, enter1, off_last, off_far, off_near)
+    own_later, own_offset = lax.optimization_barrier(compose_driven(own_driven))
+    flag = even.astype(jnp.int32)[None]
+    enter1, enter0, eight = compose(flag, two, two_last, two_far, two_near)
+    off3, shift1, shift0, total, leaving = shift(
+        flag,
+        (two, two_last, two_far, two_near, eight),
+        (own_offset, off_last, off_far, off_near, terminal[0]),
     )
-    own_later, own_offset = compose_driven(own_driven)
-    off3 = pick(off_last, own_offset)
-    off1 = pick(own_offset, off_last)
-    shift1 = matmul(off3, two_far) + off_far
-    shift0 = matmul(shift1, map1) + off1
-    total = matmul(shift0, two_near) + off_near
 
     last_ring = STEPS // RING - 1
-    leaving = matmul(terminal[0], eight) + total
     incoming = send(leaving, ring_hop(last_ring))
     map_near = send(enter0, NEAR_OUT)
     map_far = send(two, FAR_OUT_ODD)
@@ -265,12 +332,14 @@
     shift_last = send(shift1, LAST_OUT_ODD)
     out = leaving
     for source in range(last_ring - 1, 0, -1):
-        leaving = matmul(incoming, eight) + total
-        out = jnp.where(ring == source, leaving, out)
+        out = hop((ring == source).astype(jnp.int32)[None], incoming, eight, total, out)
         if source > 1:
-            incoming = send(leaving, ring_hop(source))
+            incoming = send(out, ring_hop(source))
     arrived = [
-        send(out, down(last_pair)), send(out, down(near_pair)), send(out, down(far_pair)), send(out, down(own_pair))
+        send(out, down(last_pair)),
+        send(out, down(near_pair)),
+        send(out, down(far_pair)),
+        send(out, down(own_pair)),
     ]
     pair = (step % RING) // 2
     enter_map = jnp.where(pair == NEAR, map_near, jnp.where(pair == FAR, pick(passing, map_far), pick(enter1, map_last)))

time: 155 us -> 148 us (0.955)
  blocking collectives: 24.6 us -> 0 us
  starting transfers between devices: 41.1 us -> 55.4 us
  matrix products: 18.5 us -> 8.66 us
  Pallas kernels: 8.11 us -> 16.7 us
  waiting for transfers between devices: 52.4 us -> 56.3 us
  other arithmetic: 5.6 us -> 7.15 us
    all_to_all x1 -> x0, blocking collectives: 24.6 us -> none  [shards(): lax.all_to_all(jnp.concatenate([slices, packed], axis=1), 'team', 0, 0, t...]
    ppermute x23, waiting for transfers between devices: 49.2 us -> 39.8 us  [send(): return lax.ppermute(value, BOTH, pairs)]
    dot_general x11 -> x5, matrix products: 13.3 us -> 4.18 us  [matmul(): return jnp.dot(left, right, precision=HIGH)]
    all_to_all x0 -> x1, waiting for transfers between devices: none -> 8.89 us  [shards(): lax.all_to_all(jnp.concatenate([slices, packed], axis=1), 'team', 0, 0, t...]
    pallas_call x1 -> x4, Pallas kernels: 5.86 us -> 14.5 us  [the longest x1 5.83 us: compose(): pl.pallas_call(compose_kernel, out_shape=[jax.ShapeDtypeStruct(SQUARE, jn...]
    all_to_all x0 -> x1, starting transfers between devices: none -> 7.23 us  [shards(): lax.all_to_all(jnp.concatenate([slices, packed], axis=1), 'team', 0, 0, t...]
    ppermute x23, starting transfers between devices: 37.7 us -> 44.8 us  [send(): return lax.ppermute(value, BOTH, pairs)]
    all_to_all x1, waiting for transfers between devices: 3.21 us -> 7.66 us  [shards(): parts = lax.all_to_all(part, 'team', 0, 0, tiled=True)]
  transfers between devices with their start and end apart: 24 -> 25, of which waited for: 4 -> 5; matrix products, arithmetic and copies ran while one was open for 5% -> 7% of each run, Pallas kernels for 5% -> 11%
where the time goes in v3:
time: 148 us; the launch traced here: 147 us
  waiting for transfers between devices  56.3 us (38%)
  starting transfers between devices  55.4 us (37%)
  Pallas kernels  16.7 us (11%)
  matrix products  8.66 us (6%)
  other arithmetic  7.15 us (5%)
  local copies, waits for them, and re-layouts  1.9 us (1%)
    ppermute x23, starting transfers between devices, send(): return lax.ppermute(value, BOTH, pairs)  44.8 us
    ppermute x23, waiting for transfers between devices, send(): return lax.ppermute(value, BOTH, pairs)  39.8 us
    all_to_all x1, waiting for transfers between devices, shards(): lax.all_to_all(jnp.concatenate([slices, packed], axis=1), 'team', 0, 0, t...  8.89 us
    all_to_all x1, waiting for transfers between devices, shards(): parts = lax.all_to_all(part, 'team', 0, 0, tiled=True)  7.66 us
    all_to_all x1, starting transfers between devices, shards(): lax.all_to_all(jnp.concatenate([slices, packed], axis=1), 'team', 0, 0, t...  7.23 us
    pallas_call x1, Pallas kernels, compose(): pl.pallas_call(compose_kernel, out_shape=[jax.ShapeDtypeStruct(SQUARE, jn...  5.83 us
    pallas_call x1, Pallas kernels, shift(): pl.pallas_call(shift_kernel, out_shape=[jax.ShapeDtypeStruct(ROWS, jnp.fl...  4.7 us
    dot_general x5, matrix products, matmul(): return jnp.dot(left, right, precision=HIGH)  4.18 us
  transfers between devices with their start and end apart: 25, of which 5 were waited for; matrix products, arithmetic and copies ran while one was open for 7% of the time, Pallas kernels for 11%

profile of v3, /device:TPU:1, one launch (start us, length us, event | category | flops | bytes accessed | tf_op | source)
XLA Modules:
  0.0 147.1 jit_solution(6453461633269246935)
XLA Ops:
  0.6 5.0 %collective-permute-start = (f32[512,512]{1,0:T(8,128)}, f32[512,512]{1,0:T(8,128)S(1)}, u32[]{:S(2)}, u32[]{:S(2)}) collective-permute-start(f32[512,512]{1,0:T(8,128)} %bitcast.49), channel_id=1, source_target_pairs={{1,0},{3,2},{5,4},{7,6},{9,8},{11,10},{13,12},{15,14},{17,16},{19,... | collective-permute-start | bytes 3145736 | tf_op jit(solution)/shard_map/ppermute | solution.py:109
  5.7 1.0 convert_bitcast_fusion
  7.5 0.8 pad_maximum_fusion
  8.2 7.2 %all-to-all-start = ((f32[16,48,128]{2,1,0:T(8,128)}), f32[16,48,128]{2,1,0:T(8,128)}, u32[]{:S(2)}, u32[]{:S(2)}) async-start(f32[16,48,128]{2,1,0:T(8,128)} %pad_maximum_fusion), calls=%async_computation | async-start | bytes 786432 | tf_op jit(solution)/shard_map/all_to_all | solution.py:284
  15.5 2.2 %collective-permute-done = f32[512,512]{1,0:T(8,128)S(1)} collective-permute-done((f32[512,512]{1,0:T(8,128)}, f32[512,512]{1,0:T(8,128)S(1)}, u32[]{:S(2)}, u32[]{:S(2)}) %collective-permute-start) | collective-permute-done | bytes 1048608 | tf_op jit(solution)/shard_map/ppermute | solution.py:109
  17.6 1.9 %fusion.3.two = f32[512,512]{1,0:T(8,128)S(1)} fusion(f32[512,512]{1,0:T(8,128)S(1)} %collective-permute-done, pred[]{:T(512)S(6)} %eq.48, f32[1,1,512,512]{3,2,1,0:T(8,128)S(1)} %copy-done.1), kind=kOutput, calls=%fused_computation.13 | convolution fusion | flops 1611137024 | bytes 3145729 | tf_op jit(solution)/shard_map/dot_general | solution.py:295
  19.6 1.6 %collective-permute-start.1 = (f32[512,512]{1,0:T(8,128)S(1)}, f32[512,512]{1,0:T(8,128)}, u32[]{:S(2)}, u32[]{:S(2)}) collective-permute-start(f32[512,512]{1,0:T(8,128)S(1)} %fusion.3.two), channel_id=1, source_target_pairs={{6,4},{14,12},{22,20},{30,28},{35,37},{43,45},{51,53},{59,61},{70,... | collective-permute-start | bytes 3145736 | tf_op jit(solution)/shard_map/ppermute | solution.py:109
  21.2 8.9 %all-to-all-done.got = f32[16,48,128]{2,1,0:T(8,128)} async-done(((f32[16,48,128]{2,1,0:T(8,128)}), f32[16,48,128]{2,1,0:T(8,128)}, u32[]{:S(2)}, u32[]{:S(2)}) %all-to-all-start) | async-done | bytes 393248 | tf_op jit(solution)/shard_map/all_to_all | solution.py:284
  30.1 2.2 %landmark.1 = f32[16,16,128]{2,1,0:T(8,128)} custom-call(f32[16,48,128]{2,1,0:T(8,128)} %all-to-all-done.got), custom_call_target="tpu_custom_call" | custom-call | tf_op jit(solution)/shard_map/landmark/pallas_call | solution.py:285
  32.3 3.4 %all-to-all-start.1 = ((f32[16,16,128]{2,1,0:T(8,128)}), f32[16,16,128]{2,1,0:T(8,128)S(1)}, u32[]{:S(2)}, u32[]{:S(2)}) async-start(f32[16,16,128]{2,1,0:T(8,128)} %landmark.1), calls=%async_computation.1 | async-start | bytes 262144 | tf_op jit(solution)/shard_map/all_to_all | solution.py:290
  35.8 0.7 copy-done.7
  36.4 7.7 %all-to-all-done.1 = f32[16,16,128]{2,1,0:T(8,128)S(1)} async-done(((f32[16,16,128]{2,1,0:T(8,128)}), f32[16,16,128]{2,1,0:T(8,128)S(1)}, u32[]{:S(2)}, u32[]{:S(2)}) %all-to-all-start.1) | async-done | bytes 131104 | tf_op jit(solution)/shard_map/all_to_all | solution.py:290
  44.1 1.7 %collective-permute-start.3 = (f32[512,512]{1,0:T(8,128)S(1)}, f32[512,512]{1,0:T(8,128)}, u32[]{:S(2)}, u32[]{:S(2)}) collective-permute-start(f32[512,512]{1,0:T(8,128)S(1)} %fusion.3.two), channel_id=1, source_target_pairs={{4,2},{12,10},{20,18},{28,26},{37,39},{45,47},{53,55},{61,63},{68,... | collective-permute-start | bytes 3145736 | tf_op jit(solution)/shard_map/ppermute | solution.py:109
  45.8 1.6 %collective-permute-start.4 = (f32[512,512]{1,0:T(8,128)S(1)}, f32[512,512]{1,0:T(8,128)}, u32[]{:S(2)}, u32[]{:S(2)}) collective-permute-start(f32[512,512]{1,0:T(8,128)S(1)} %fusion.3.two), channel_id=1, source_target_pairs={{0,2},{8,10},{16,18},{24,26},{33,39},{41,47},{49,55},{57,63},{64,6... | collective-permute-start | bytes 3145736 | tf_op jit(solution)/shard_map/ppermute | solution.py:109
  47.4 1.7 %collective-permute-start.2 = (f32[512,512]{1,0:T(8,128)}, f32[512,512]{1,0:T(8,128)}, u32[]{:S(2)}, u32[]{:S(2)}) collective-permute-start(f32[512,512]{1,0:T(8,128)} %collective-permute-done.1), channel_id=1, source_target_pairs={{4,2},{12,10},{20,18},{28,26},{37,39},{45,47},{53,55},{61,63},{68,... | collective-permute-start | bytes 3145736 | tf_op jit(solution)/shard_map/ppermute | solution.py:109
  49.2 1.2 convolution_add_fusion.5
  50.3 11.8 %collective-permute-start.6 = (f32[64,512]{1,0:T(8,128)S(1)}, f32[64,512]{1,0:T(8,128)S(1)}, u32[]{:S(2)}, u32[]{:S(2)}) collective-permute-start(f32[64,512]{1,0:T(8,128)S(1)} %convolution_add_fusion.5), channel_id=1, source_target_pairs={{1,0},{5,4},{7,6},{9,8},{13,12},{15,14},{17,16},{21,20},{23,22},{2... | collective-permute-start | bytes 393224 | tf_op jit(solution)/shard_map/ppermute | solution.py:109
  62.1 0.7 collective-permute-start.5
  62.8 2.0 %collective-permute-done.6 = f32[64,512]{1,0:T(8,128)S(1)} collective-permute-done((f32[64,512]{1,0:T(8,128)S(1)}, f32[64,512]{1,0:T(8,128)S(1)}, u32[]{:S(2)}, u32[]{:S(2)}) %collective-permute-start.6) | collective-permute-done | bytes 131104 | tf_op jit(solution)/shard_map/ppermute | solution.py:109
  64.7 1.6 %collective-permute-start.17 = (f32[512,512]{1,0:T(8,128)S(1)}, f32[512,512]{1,0:T(8,128)}, u32[]{:S(2)}, u32[]{:S(2)}) collective-permute-start(f32[512,512]{1,0:T(8,128)S(1)} %fusion.3.two), channel_id=1, source_target_pairs={{39,37},{47,45},{55,53},{63,61},{103,101},{111,109},{119,117},{127... | collective-permute-start | bytes 3145736 | tf_op jit(solution)/shard_map/ppermute | solution.py:109
  66.4 1.1 convolution_add_fusion.3
  67.5 1.3 collective-permute-start.7
  68.8 1.1 convolution_add_fusion.4.off_own
  69.9 1.3 collective-permute-start.8
  71.2 1.3 collective-permute-start.9
  72.5 5.8 %compose.1 = (f32[512,512]{1,0:T(8,128)}, f32[512,512]{1,0:T(8,128)}, f32[512,512]{1,0:T(8,128)}) custom-call(s32[1]{0:T(128)} %bitcast.2.flag, f32[512,512]{1,0:T(8,128)} %copy-done.2, f32[512,512]{1,0:T(8,128)} %collective-permute-done.2.last, f32[512,512]{1,0:T(8,128)} %collective-permute-done.3.far, f32[512,512]{1,0:T(8,128)} %collective-permute-done.4.near), custom_call_target="tpu_custom_call" | custom-call | tf_op jit(solution)/shard_map/compose/pallas_call | solution.py:172
  78.3 1.7 %collective-permute-start.16 = (f32[512,512]{1,0:T(8,128)}, f32[512,512]{1,0:T(8,128)}, u32[]{:S(2)}, u32[]{:S(2)}) collective-permute-start(f32[512,512]{1,0:T(8,128)} %get-tuple-element.18), channel_id=1, source_target_pairs={{2,0},{10,8},{18,16},{26,24},{39,33},{47,41},{55,49},{63,57},{66,6... | collective-permute-start | bytes 3145736 | tf_op jit(solution)/shard_map/ppermute | solution.py:109
  80.0 1.6 %collective-permute-start.18 = (f32[512,512]{1,0:T(8,128)}, f32[512,512]{1,0:T(8,128)}, u32[]{:S(2)}, u32[]{:S(2)}) collective-permute-start(f32[512,512]{1,0:T(8,128)} %get-tuple-element.19), channel_id=1, source_target_pairs={{39,35},{47,43},{55,51},{63,59},{103,99},{111,107},{119,115},{127,... | collective-permute-start | bytes 3145736 | tf_op jit(solution)/shard_map/ppermute | solution.py:109
  81.6 0.7 broadcast_select_fusion.6
  82.3 4.7 %shift.1 = (f32[64,512]{1,0:T(8,128)}, f32[64,512]{1,0:T(8,128)}, f32[64,512]{1,0:T(8,128)}, f32[64,512]{1,0:T(8,128)}, f32[64,512]{1,0:T(8,128)}) custom-call(s32[1]{0:T(128)} %bitcast.2.flag, f32[512,512]{1,0:T(8,128)} %copy-done.2, f32[512,512]{1,0:T(8,128)} %collective-permute-done.2.last, f32[512,512]{1,0:T(8,128)} %collective-permute-done.3.far, ...), custom_call_target="tpu_custom_call" | custom-call | tf_op jit(solution)/shard_map/shift/pallas_call | solution.py:218
  87.0 1.3 collective-permute-start.10
  88.3 1.3 collective-permute-start.19
  89.7 2.0 %hop.2.kept = f32[64,512]{1,0:T(8,128)} custom-call(s32[1]{0:T(128)} %bitcast.1.flag, f32[64,512]{1,0:T(8,128)} %collective-permute-done.10.arrived, f32[512,512]{1,0:T(8,128)} %get-tuple-element.14.eight, f32[64,512]{1,0:T(8,128)} %get-tuple-element.17.total, f32[64,512]{1,0:T(8,128)} %get-tuple-element.16.kept), custom_call_target="tpu_custom_call" | custom-call | tf_op jit(solution)/shard_map/hop/pallas_call | solution.py:241
  91.6 1.3 collective-permute-start.11
  92.9 1.3 collective-permute-start.20
  94.2 1.3 collective-permute-start.21
  95.5 2.0 %hop.3 = f32[64,512]{1,0:T(8,128)} custom-call(s32[1]{0:T(128)} %bitcast.flag, f32[64,512]{1,0:T(8,128)} %collective-permute-done.11.arrived, f32[512,512]{1,0:T(8,128)} %get-tuple-element.14.eight, f32[64,512]{1,0:T(8,128)} %get-tuple-element.17.total, f32[64,512]{1,0:T(8,128)} %hop.2.kept), custom_call_target="tpu_custom_call" | custom-call | tf_op jit(solution)/shard_map/hop/pallas_call | solution.py:241
  97.5 1.3 collective-permute-start.12
  98.8 1.3 collective-permute-start.13
  100.2 0.8 collective-permute-start.14
  101.0 0.7 collective-permute-start.15
  101.7 1.0 select_select_fusion.2
  102.7 1.1 select_add_fusion
  103.8 2.5 %select_select_fusion = f32[512,512]{1,0:T(8,128)S(1)} fusion(f32[512,512]{1,0:T(8,128)} %collective-permute-done.16, f32[512,512]{1,0:T(8,128)S(1)} %copy-done.3, f32[512,512]{1,0:T(8,128)} %collective-permute-done.18, f32[512,512]{1,0:T(8,128)} %collective-permute-done.1, f32[512,512]{1,0:T(8,128)} %collective-permute-done.17, pred[]{:T(512)S(6)} %eq.57, ...), kind=kLoop, calls=%fused_computation.10 | loop fusion | flops 1048576 | bytes 6291459 | tf_op jit(solution)/shard_map/jit(_where)/select_n | solution.py:345
  107.7 1.3 collective-permute-start.22
  109.0 35.6 %collective-permute-done.22 = f32[64,512]{1,0:T(8,128)S(1)} collective-permute-done((f32[64,512]{1,0:T(8,128)S(1)}, f32[64,512]{1,0:T(8,128)S(1)}, u32[]{:S(2)}, u32[]{:S(2)}) %collective-permute-start.22) | collective-permute-done | bytes 131104 | tf_op jit(solution)/shard_map/ppermute | solution.py:109
  144.6 1.1 fusion.1
  145.7 1.4 fusion
  (47 shorter events, 2.3 us)
Async XLA Ops:
  0.6 145.1 %copy-start = (f32[1,1,64,512]{3,2,1,0:T(8,128)S(1)}, f32[1,1,64,512]{3,2,1,0:T(8,128)}, u32[]{:S(2)}) copy-start(f32[1,1,64,512]{3,2,1,0:T(8,128)} %param.8) | copy-start | bytes 393220
  0.6 17.0 %collective-permute-start = (f32[512,512]{1,0:T(8,128)}, f32[512,512]{1,0:T(8,128)S(1)}, u32[]{:S(2)}, u32[]{:S(2)}) collective-permute-start(f32[512,512]{1,0:T(8,128)} %bitcast.49), channel_id=1, source_target_pairs={{1,0},{3,2},{5,4},{7,6},{9,8},{11,10},{13,12},{15,14},{17,16},{19,... | collective-permute-start | bytes 3145736 | tf_op jit(solution)/shard_map/ppermute | solution.py:109
  6.6 0.7 copy-start.6
  6.7 10.9 %copy-start.1 = (f32[1,1,512,512]{3,2,1,0:T(8,128)S(1)}, f32[1,1,512,512]{3,2,1,0:T(8,128)}, u32[]{:S(2)}) copy-start(f32[1,1,512,512]{3,2,1,0:T(8,128)} %param.7) | copy-start | bytes 3145732
  8.2 21.9 %all-to-all-start = ((f32[16,48,128]{2,1,0:T(8,128)}), f32[16,48,128]{2,1,0:T(8,128)}, u32[]{:S(2)}, u32[]{:S(2)}) async-start(f32[16,48,128]{2,1,0:T(8,128)} %pad_maximum_fusion), calls=%async_computation | async-start | bytes 786432 | tf_op jit(solution)/shard_map/all_to_all | solution.py:284
  19.6 47.9 %copy-start.2 = (f32[512,512]{1,0:T(8,128)}, f32[512,512]{1,0:T(8,128)S(1)}, u32[]{:S(2)}) copy-start(f32[512,512]{1,0:T(8,128)S(1)} %fusion.3.two) | copy-start | bytes 3145732
  19.6 27.9 %collective-permute-start.1 = (f32[512,512]{1,0:T(8,128)S(1)}, f32[512,512]{1,0:T(8,128)}, u32[]{:S(2)}, u32[]{:S(2)}) collective-permute-start(f32[512,512]{1,0:T(8,128)S(1)} %fusion.3.two), channel_id=1, source_target_pairs={{6,4},{14,12},{22,20},{30,28},{35,37},{43,45},{51,53},{59,61},{70,... | collective-permute-start | bytes 3145736 | tf_op jit(solution)/shard_map/ppermute | solution.py:109
  32.3 11.8 %all-to-all-start.1 = ((f32[16,16,128]{2,1,0:T(8,128)}), f32[16,16,128]{2,1,0:T(8,128)S(1)}, u32[]{:S(2)}, u32[]{:S(2)}) async-start(f32[16,16,128]{2,1,0:T(8,128)} %landmark.1), calls=%async_computation.1 | async-start | bytes 262144 | tf_op jit(solution)/shard_map/all_to_all | solution.py:290
  35.8 0.7 copy-start.7
  44.1 25.7 %collective-permute-start.3 = (f32[512,512]{1,0:T(8,128)S(1)}, f32[512,512]{1,0:T(8,128)}, u32[]{:S(2)}, u32[]{:S(2)}) collective-permute-start(f32[512,512]{1,0:T(8,128)S(1)} %fusion.3.two), channel_id=1, source_target_pairs={{4,2},{12,10},{20,18},{28,26},{37,39},{45,47},{53,55},{61,63},{68,... | collective-permute-start | bytes 3145736 | tf_op jit(solution)/shard_map/ppermute | solution.py:109
  45.8 25.4 %collective-permute-start.4 = (f32[512,512]{1,0:T(8,128)S(1)}, f32[512,512]{1,0:T(8,128)}, u32[]{:S(2)}, u32[]{:S(2)}) collective-permute-start(f32[512,512]{1,0:T(8,128)S(1)} %fusion.3.two), channel_id=1, source_target_pairs={{0,2},{8,10},{16,18},{24,26},{33,39},{41,47},{49,55},{57,63},{64,6... | collective-permute-start | bytes 3145736 | tf_op jit(solution)/shard_map/ppermute | solution.py:109
  47.4 25.1 %collective-permute-start.2 = (f32[512,512]{1,0:T(8,128)}, f32[512,512]{1,0:T(8,128)}, u32[]{:S(2)}, u32[]{:S(2)}) collective-permute-start(f32[512,512]{1,0:T(8,128)} %collective-permute-done.1), channel_id=1, source_target_pairs={{4,2},{12,10},{20,18},{28,26},{37,39},{45,47},{53,55},{61,63},{68,... | collective-permute-start | bytes 3145736 | tf_op jit(solution)/shard_map/ppermute | solution.py:109
  50.3 14.4 %collective-permute-start.6 = (f32[64,512]{1,0:T(8,128)S(1)}, f32[64,512]{1,0:T(8,128)S(1)}, u32[]{:S(2)}, u32[]{:S(2)}) collective-permute-start(f32[64,512]{1,0:T(8,128)S(1)} %convolution_add_fusion.5), channel_id=1, source_target_pairs={{1,0},{5,4},{7,6},{9,8},{13,12},{15,14},{17,16},{21,20},{23,22},{2... | collective-permute-start | bytes 393224 | tf_op jit(solution)/shard_map/ppermute | solution.py:109
  62.1 5.4 %collective-permute-start.5 = (f32[64,512]{1,0:T(8,128)S(1)}, f32[64,512]{1,0:T(8,128)S(1)}, u32[]{:S(2)}, u32[]{:S(2)}) collective-permute-start(f32[64,512]{1,0:T(8,128)S(1)} %convolution_add_fusion.5), channel_id=1, source_target_pairs={{3,2},{11,10},{19,18},{27,26},{38,39},{46,47},{54,55},{62,63},{67,... | collective-permute-start | bytes 393224 | tf_op jit(solution)/shard_map/ppermute | solution.py:109
  64.7 39.0 %collective-permute-start.17 = (f32[512,512]{1,0:T(8,128)S(1)}, f32[512,512]{1,0:T(8,128)}, u32[]{:S(2)}, u32[]{:S(2)}) collective-permute-start(f32[512,512]{1,0:T(8,128)S(1)} %fusion.3.two), channel_id=1, source_target_pairs={{39,37},{47,45},{55,53},{63,61},{103,101},{111,109},{119,117},{127... | collective-permute-start | bytes 3145736 | tf_op jit(solution)/shard_map/ppermute | solution.py:109
  67.5 2.4 %copy-start.5 = (f32[64,512]{1,0:T(8,128)}, f32[64,512]{1,0:T(8,128)S(1)}, u32[]{:S(2)}) copy-start(f32[64,512]{1,0:T(8,128)S(1)} %collective-permute-done.5) | copy-start | bytes 393220
  67.5 12.5 %collective-permute-start.7 = (f32[64,512]{1,0:T(8,128)}, f32[64,512]{1,0:T(8,128)}, u32[]{:S(2)}, u32[]{:S(2)}) collective-permute-start(f32[64,512]{1,0:T(8,128)} %convolution_add_fusion.3), channel_id=1, source_target_pairs={{6,2},{14,10},{22,18},{30,26},{35,39},{43,47},{51,55},{59,63},{70,... | collective-permute-start | bytes 393224 | tf_op jit(solution)/shard_map/ppermute | solution.py:109
  69.9 12.4 %collective-permute-start.8 = (f32[64,512]{1,0:T(8,128)}, f32[64,512]{1,0:T(8,128)}, u32[]{:S(2)}, u32[]{:S(2)}) collective-permute-start(f32[64,512]{1,0:T(8,128)} %convolution_add_fusion.3), channel_id=1, source_target_pairs={{4,2},{12,10},{20,18},{28,26},{37,39},{45,47},{53,55},{61,63},{68,... | collective-permute-start | bytes 393224 | tf_op jit(solution)/shard_map/ppermute | solution.py:109
  71.2 11.1 %collective-permute-start.9 = (f32[64,512]{1,0:T(8,128)}, f32[64,512]{1,0:T(8,128)}, u32[]{:S(2)}, u32[]{:S(2)}) collective-permute-start(f32[64,512]{1,0:T(8,128)} %convolution_add_fusion.3), channel_id=1, source_target_pairs={{0,2},{8,10},{16,18},{24,26},{33,39},{41,47},{49,55},{57,63},{64,6... | collective-permute-start | bytes 393224 | tf_op jit(solution)/shard_map/ppermute | solution.py:109
  78.3 25.5 %collective-permute-start.16 = (f32[512,512]{1,0:T(8,128)}, f32[512,512]{1,0:T(8,128)}, u32[]{:S(2)}, u32[]{:S(2)}) collective-permute-start(f32[512,512]{1,0:T(8,128)} %get-tuple-element.18), channel_id=1, source_target_pairs={{2,0},{10,8},{18,16},{26,24},{39,33},{47,41},{55,49},{63,57},{66,6... | collective-permute-start | bytes 3145736 | tf_op jit(solution)/shard_map/ppermute | solution.py:109
  80.0 23.8 %collective-permute-start.18 = (f32[512,512]{1,0:T(8,128)}, f32[512,512]{1,0:T(8,128)}, u32[]{:S(2)}, u32[]{:S(2)}) collective-permute-start(f32[512,512]{1,0:T(8,128)} %get-tuple-element.19), channel_id=1, source_target_pairs={{39,35},{47,43},{55,51},{63,59},{103,99},{111,107},{119,115},{127,... | collective-permute-start | bytes 3145736 | tf_op jit(solution)/shard_map/ppermute | solution.py:109
  87.0 2.6 %collective-permute-start.10 = (f32[64,512]{1,0:T(8,128)}, f32[64,512]{1,0:T(8,128)}, u32[]{:S(2)}, u32[]{:S(2)}) collective-permute-start(f32[64,512]{1,0:T(8,128)} %get-tuple-element.16.kept), channel_id=1, source_target_pairs={{26,18},{63,55},{90,82},{127,119},{154,146},{191,183},{218,210},{2... | collective-permute-start | bytes 393224 | tf_op jit(solution)/shard_map/ppermute | solution.py:109
  88.3 4.6 %collective-permute-start.19 = (f32[64,512]{1,0:T(8,128)}, f32[64,512]{1,0:T(8,128)}, u32[]{:S(2)}, u32[]{:S(2)}) collective-permute-start(f32[64,512]{1,0:T(8,128)} %get-tuple-element.20), channel_id=1, source_target_pairs={{2,0},{10,8},{18,16},{26,24},{39,33},{47,41},{55,49},{63,57},{66,6... | collective-permute-start | bytes 393224 | tf_op jit(solution)/shard_map/ppermute | solution.py:109
  91.6 2.6 %collective-permute-start.11 = (f32[64,512]{1,0:T(8,128)}, f32[64,512]{1,0:T(8,128)}, u32[]{:S(2)}, u32[]{:S(2)}) collective-permute-start(f32[64,512]{1,0:T(8,128)} %hop.2.kept), channel_id=1, source_target_pairs={{18,10},{55,47},{82,74},{119,111},{146,138},{183,175},{210,202},{2... | collective-permute-start | bytes 393224 | tf_op jit(solution)/shard_map/ppermute | solution.py:109
  92.9 4.6 %collective-permute-start.20 = (f32[64,512]{1,0:T(8,128)}, f32[64,512]{1,0:T(8,128)}, u32[]{:S(2)}, u32[]{:S(2)}) collective-permute-start(f32[64,512]{1,0:T(8,128)} %get-tuple-element.21), channel_id=1, source_target_pairs={{2,4},{10,12},{18,20},{26,28},{39,37},{47,45},{55,53},{63,61},{66,... | collective-permute-start | bytes 393224 | tf_op jit(solution)/shard_map/ppermute | solution.py:109
  94.2 4.6 %collective-permute-start.21 = (f32[64,512]{1,0:T(8,128)}, f32[64,512]{1,0:T(8,128)}, u32[]{:S(2)}, u32[]{:S(2)}) collective-permute-start(f32[64,512]{1,0:T(8,128)} %get-tuple-element.22), channel_id=1, source_target_pairs={{39,35},{47,43},{55,51},{63,59},{103,99},{111,107},{119,115},{127,... | collective-permute-start | bytes 393224 | tf_op jit(solution)/shard_map/ppermute | solution.py:109
  97.5 2.7 %collective-permute-start.12 = (f32[64,512]{1,0:T(8,128)}, f32[64,512]{1,0:T(8,128)}, u32[]{:S(2)}, u32[]{:S(2)}) collective-permute-start(f32[64,512]{1,0:T(8,128)} %hop.3), channel_id=1, source_target_pairs={{10,6},{18,14},{26,22},{47,35},{55,43},{63,51},{74,70},{82,78},{90... | collective-permute-start | bytes 393224 | tf_op jit(solution)/shard_map/ppermute | solution.py:109
  98.8 2.1 %collective-permute-start.13 = (f32[64,512]{1,0:T(8,128)}, f32[64,512]{1,0:T(8,128)}, u32[]{:S(2)}, u32[]{:S(2)}) collective-permute-start(f32[64,512]{1,0:T(8,128)} %hop.3), channel_id=1, source_target_pairs={{10,0},{18,8},{26,16},{47,33},{55,41},{63,49},{74,64},{82,72},{90,... | collective-permute-start | bytes 393224 | tf_op jit(solution)/shard_map/ppermute | solution.py:109
  100.2 3.7 %copy-start.3 = (f32[512,512]{1,0:T(8,128)S(1)}, f32[512,512]{1,0:T(8,128)}, u32[]{:S(2)}) copy-start(f32[512,512]{1,0:T(8,128)} %get-tuple-element.19) | copy-start | bytes 3145732
  100.2 2.5 %collective-permute-start.14 = (f32[64,512]{1,0:T(8,128)}, f32[64,512]{1,0:T(8,128)S(1)}, u32[]{:S(2)}, u32[]{:S(2)}) collective-permute-start(f32[64,512]{1,0:T(8,128)} %hop.3), channel_id=1, source_target_pairs={{10,4},{18,12},{26,20},{47,37},{55,45},{63,53},{74,68},{82,76},{90... | collective-permute-start | bytes 393224 | tf_op jit(solution)/shard_map/ppermute | solution.py:109
  101.0 1.7 %collective-permute-start.15 = (f32[64,512]{1,0:T(8,128)}, f32[64,512]{1,0:T(8,128)S(1)}, u32[]{:S(2)}, u32[]{:S(2)}) collective-permute-start(f32[64,512]{1,0:T(8,128)} %hop.3), channel_id=1, source_target_pairs={{10,2},{18,10},{26,18},{47,39},{55,47},{63,55},{74,66},{82,74},{90... | collective-permute-start | bytes 393224 | tf_op jit(solution)/shard_map/ppermute | solution.py:109
  106.3 0.9 copy-start.4
  107.7 36.9 %collective-permute-start.22 = (f32[64,512]{1,0:T(8,128)S(1)}, f32[64,512]{1,0:T(8,128)S(1)}, u32[]{:S(2)}, u32[]{:S(2)}) collective-permute-start(f32[64,512]{1,0:T(8,128)S(1)} %get-tuple-element.30), channel_id=1, source_target_pairs={{0,1},{2,3},{4,5},{6,7},{8,9},{10,11},{12,13},{14,15},{16,17},{18,... | collective-permute-start | bytes 393224 | tf_op jit(solution)/shard_map/ppermute | solution.py:109

commit v4 on v3

--- a/solution.py
+++ b/solution.py
@@ -133,7 +133,9 @@
     return lambda src, dst, k: pltpu.make_async_copy(src, dst, sems.at[k])
 
 
-def compose_kernel(flag, two, last, far, near, enter1, enter0, eight, m3, m2, m1, m0, r1, r0, r8, sems, out_sems):
+def compose_kernel(
+    flag, two, last, far, near, shift1, shift0, enter1, enter0, eight, m3, m2, m1, m0, r1, r0, r8, sems, out_sems
+):
     load, store = copier(sems), copier(out_sems)
     even = flag[0] == 1
 
@@ -149,81 +151,95 @@
 
     load(far, m2, 1).start()
     load(near, m0, 3).start()
+    map_rows, shift_rows = pl.ds(0, TEAM_STATES), pl.ds(TEAM_STATES, COLS)
+    store(shift1, enter1.at[shift_rows], 3).start()
+    store(shift0, enter0.at[shift_rows], 4).start()
     load(last, m3, 0).wait()
     load(far, m2, 1).wait()
     r1[...] = product(split(m3[...]), split(m2[...]))
-    store(r1, enter1, 0).start()
+    store(r1, enter1.at[map_rows], 0).start()
     load(last, m1, 2).wait()
     r0[...] = product(split(r1[...]), split(m1[...]))
-    store(r0, enter0, 1).start()
+    store(r0, enter0.at[map_rows], 1).start()
     load(near, m0, 3).wait()
     r8[...] = product(split(r0[...]), split(m0[...]))
     store(r8, eight, 2).start()
-    store(r1, enter1, 0).wait()
-    store(r0, enter0, 1).wait()
+    store(shift1, enter1.at[shift_rows], 3).wait()
+    store(shift0, enter0.at[shift_rows], 4).wait()
+    store(r1, enter1.at[map_rows], 0).wait()
+    store(r0, enter0.at[map_rows], 1).wait()
     store(r8, eight, 2).wait()
 
 
 SQUARE = (TEAM_STATES, TEAM_STATES)
 ROWS = (COLS, TEAM_STATES)
-
-
-def compose(flag, two, last, far, near):
+TALL = (TEAM_STATES + COLS, TEAM_STATES)
+
+
+def compose(flag, maps, shifts):
     return pl.pallas_call(
         compose_kernel,
-        out_shape=[jax.ShapeDtypeStruct(SQUARE, jnp.float32)] * 3,
-        in_specs=[pl.BlockSpec(memory_space=pltpu.SMEM)] + [pl.BlockSpec(memory_space=pl.ANY)] * 4,
+        out_shape=[jax.ShapeDtypeStruct(shape, jnp.float32) for shape in (TALL, TALL, SQUARE)],
+        in_specs=[pl.BlockSpec(memory_space=pltpu.SMEM)] + [pl.BlockSpec(memory_space=pl.ANY)] * 6,
         out_specs=[pl.BlockSpec(memory_space=pl.ANY)] * 3,
         scratch_shapes=[pltpu.VMEM(SQUARE, jnp.float32)] * 7
-        + [pltpu.SemaphoreType.DMA((4,)), pltpu.SemaphoreType.DMA((3,))],
+        + [pltpu.SemaphoreType.DMA((4,)), pltpu.SemaphoreType.DMA((5,))],
         name="compose",
-    )(flag, two, last, far, near)
-
-
-def shift_kernel(
-    flag, two, last, far, near, eight, off_own, off_last, off_far, off_near, start,
-    shift2, shift1, shift0, total, leaving, m2, m1, m0, m8, sems,
+    )(flag, *maps, *shifts)
+
+
+def sweep_kernel(
+    flag, two, last, far, near, off_own, off_last, off_far, off_near, start,
+    shift2, shift1, shift0, total, leaving, m3, m2, m1, m0, sems,
 ):
     load = copier(sems)
     even = flag[0] == 1
-    load(far, m2, 0).start()
 
     @pl.when(even)
     def _():
-        load(two, m1, 1).start()
+        load(last, m3, 0).start()
+        load(far, m2, 1).start()
+        load(two, m1, 2).start()
 
     @pl.when(jnp.logical_not(even))
     def _():
-        load(last, m1, 1).start()
-
-    load(near, m0, 2).start()
-    load(eight, m8, 3).start()
-    moved = jnp.where(even, off_last[...], off_own[...])
+        load(two, m3, 0).start()
+        load(far, m2, 1).start()
+        load(last, m1, 2).start()
+
+    load(near, m0, 3).start()
+    off3 = jnp.where(even, off_last[...], off_own[...])
     off1 = jnp.where(even, off_own[...], off_last[...])
-    shift2[...] = moved
-    load(far, m2, 0).wait()
-    moved = product(split(moved), split(m2[...])) + off_far[...]
-    shift1[...] = moved
-    load(last, m1, 1).wait()
-    moved = product(split(moved), split(m1[...])) + off1
-    shift0[...] = moved
-    load(near, m0, 2).wait()
-    moved = product(split(moved), split(m0[...])) + off_near[...]
-    total[...] = moved
-    load(eight, m8, 3).wait()
-    leaving[...] = product(split(start[...]), split(m8[...])) + moved
-
-
-def shift(flag, maps, rows):
+    shift2[...] = off3
+    load(last, m3, 0).wait()
+    moved = product(split(start[...]), split(m3[...])) + off3
+    both = jnp.concatenate([moved, off3], axis=0)
+
+    def step(rows, weight, offset):
+        return product(split(rows), split(weight)) + jnp.concatenate([offset, offset], axis=0)
+
+    load(far, m2, 1).wait()
+    both = step(both, m2[...], off_far[...])
+    shift1[...] = both[COLS:]
+    load(last, m1, 2).wait()
+    both = step(both, m1[...], off1)
+    shift0[...] = both[COLS:]
+    load(near, m0, 3).wait()
+    both = step(both, m0[...], off_near[...])
+    total[...] = both[COLS:]
+    leaving[...] = both[:COLS]
+
+
+def sweep(flag, maps, rows):
     return pl.pallas_call(
-        shift_kernel,
+        sweep_kernel,
         out_shape=[jax.ShapeDtypeStruct(ROWS, jnp.float32)] * 5,
         in_specs=[pl.BlockSpec(memory_space=pltpu.SMEM)]
-        + [pl.BlockSpec(memory_space=pl.ANY)] * 5
+        + [pl.BlockSpec(memory_space=pl.ANY)] * 4
         + [pl.BlockSpec(memory_space=pltpu.VMEM)] * 5,
         out_specs=[pl.BlockSpec(memory_space=pltpu.VMEM)] * 5,
         scratch_shapes=[pltpu.VMEM(SQUARE, jnp.float32)] * 4 + [pltpu.SemaphoreType.DMA((4,))],
-        name="shift",
+        name="sweep",
     )(flag, *maps, *rows)
 
 
@@ -315,21 +331,18 @@
 
     own_later, own_offset = lax.optimization_barrier(compose_driven(own_driven))
     flag = even.astype(jnp.int32)[None]
-    enter1, enter0, eight = compose(flag, two, two_last, two_far, two_near)
-    off3, shift1, shift0, total, leaving = shift(
-        flag,
-        (two, two_last, two_far, two_near, eight),
-        (own_offset, off_last, off_far, off_near, terminal[0]),
+    maps = (two, two_last, two_far, two_near)
+    off3, shift1, shift0, total, leaving = sweep(
+        flag, maps, (own_offset, off_last, off_far, off_near, terminal[0])
     )
 
     last_ring = STEPS // RING - 1
     incoming = send(leaving, ring_hop(last_ring))
+    enter1, enter0, eight = compose(flag, maps, (shift1, shift0))
     map_near = send(enter0, NEAR_OUT)
     map_far = send(two, FAR_OUT_ODD)
     map_last = send(enter1, LAST_OUT_ODD)
-    shift_near = send(shift0, NEAR_OUT)
     shift_far = send(off3, FAR_OUT)
-    shift_last = send(shift1, LAST_OUT_ODD)
     out = leaving
     for source in range(last_ring - 1, 0, -1):
         out = hop((ring == source).astype(jnp.int32)[None], incoming, eight, total, out)
@@ -342,8 +355,13 @@
         send(out, down(own_pair)),
     ]
     pair = (step % RING) // 2
-    enter_map = jnp.where(pair == NEAR, map_near, jnp.where(pair == FAR, pick(passing, map_far), pick(enter1, map_last)))
-    enter_shift = jnp.where(pair == NEAR, shift_near, jnp.where(pair == FAR, shift_far, pick(shift1, shift_last)))
+
+    def mine(rows, at_far):
+        here = pick(enter1[rows], map_last[rows])
+        return jnp.where(pair == NEAR, map_near[rows], jnp.where(pair == FAR, at_far, here))
+
+    enter_map = mine(slice(0, TEAM_STATES), pick(passing, map_far))
+    enter_shift = mine(slice(TEAM_STATES, None), shift_far)
     enter_map, enter_shift = lax.optimization_barrier((enter_map, enter_shift))
     entry = (arrived[0] + arrived[1]) + (arrived[2] + arrived[3]) + jnp.where(ring == last_ring, terminal[0], 0.0)
     entry = lax.optimization_barrier(entry)

time: 148 us -> 156 us (1.054)
  the two profiles are of different devices: /device:TPU:1 before, /device:TPU:192 now
where the time goes in v4:
time: 156 us; the launch traced here: 155 us
  waiting for transfers between devices  75.3 us (48%)
  starting transfers between devices  41.7 us (27%)
  Pallas kernels  20 us (13%)
  matrix products  8 us (5%)
  other arithmetic  7.34 us (5%)
    ppermute x21, waiting for transfers between devices, send(): return lax.ppermute(value, BOTH, pairs)  59.9 us
    ppermute x21, starting transfers between devices, send(): return lax.ppermute(value, BOTH, pairs)  27.2 us
    pallas_call x1, Pallas kernels, compose(): pl.pallas_call(compose_kernel, out_shape=[jax.ShapeDtypeStruct(shape, jnp...  9.14 us
    all_to_all x1, waiting for transfers between devices, shards(): parts = lax.all_to_all(part, 'team', 0, 0, tiled=True)  8.61 us
    all_to_all x1, starting transfers between devices, shards(): lax.all_to_all(jnp.concatenate([slices, packed], axis=1), 'team', 0, 0, t...  7.25 us
    all_to_all x1, starting transfers between devices, shards(): parts = lax.all_to_all(part, 'team', 0, 0, tiled=True)  7.24 us
    all_to_all x1, waiting for transfers between devices, shards(): lax.all_to_all(jnp.concatenate([slices, packed], axis=1), 'team', 0, 0, t...  6.84 us
    pallas_call x1, Pallas kernels, sweep(): pl.pallas_call(sweep_kernel, out_shape=[jax.ShapeDtypeStruct(ROWS, jnp.fl...  4.72 us
  transfers between devices with their start and end apart: 23, of which 5 were waited for; matrix products, arithmetic and copies ran while one was open for 6% of the time, Pallas kernels for 4%

profile of v4, /device:TPU:192, one launch (start us, length us, event | category | flops | bytes accessed | tf_op | source)
XLA Modules:
  0.0 154.8 jit_solution(12890148969862044930)
XLA Ops:
  0.7 1.8 %collective-permute-start = (f32[512,512]{1,0:T(8,128)}, f32[512,512]{1,0:T(8,128)S(1)}, u32[]{:S(2)}, u32[]{:S(2)}) collective-permute-start(f32[512,512]{1,0:T(8,128)} %bitcast.49), channel_id=1, source_target_pairs={{1,0},{3,2},{5,4},{7,6},{9,8},{11,10},{13,12},{15,14},{17,16},{19,... | collective-permute-start | bytes 3145736 | tf_op jit(solution)/shard_map/ppermute | solution.py:109
  2.4 1.0 convert_bitcast_fusion
  3.7 0.8 pad_maximum_fusion
  4.4 7.2 %all-to-all-start = ((f32[16,48,128]{2,1,0:T(8,128)}), f32[16,48,128]{2,1,0:T(8,128)}, u32[]{:S(2)}, u32[]{:S(2)}) async-start(f32[16,48,128]{2,1,0:T(8,128)} %pad_maximum_fusion), calls=%async_computation | async-start | bytes 786432 | tf_op jit(solution)/shard_map/all_to_all | solution.py:300
  11.7 3.2 %collective-permute-done = f32[512,512]{1,0:T(8,128)S(1)} collective-permute-done((f32[512,512]{1,0:T(8,128)}, f32[512,512]{1,0:T(8,128)S(1)}, u32[]{:S(2)}, u32[]{:S(2)}) %collective-permute-start) | collective-permute-done | bytes 1048608 | tf_op jit(solution)/shard_map/ppermute | solution.py:109
  15.0 1.9 %fusion.5.two = f32[512,512]{1,0:T(8,128)S(1)} fusion(f32[512,512]{1,0:T(8,128)S(1)} %collective-permute-done, pred[]{:T(512)S(6)} %eq.48, f32[1,1,512,512]{3,2,1,0:T(8,128)S(1)} %copy-done.1), kind=kOutput, calls=%fused_computation.15 | convolution fusion | flops 1611137024 | bytes 3145729 | tf_op jit(solution)/shard_map/dot_general | solution.py:311
  16.9 1.7 %collective-permute-start.1 = (f32[512,512]{1,0:T(8,128)S(1)}, f32[512,512]{1,0:T(8,128)}, u32[]{:S(2)}, u32[]{:S(2)}) collective-permute-start(f32[512,512]{1,0:T(8,128)S(1)} %fusion.5.two), channel_id=1, source_target_pairs={{6,4},{14,12},{22,20},{30,28},{35,37},{43,45},{51,53},{59,61},{70,... | collective-permute-start | bytes 3145736 | tf_op jit(solution)/shard_map/ppermute | solution.py:109
  18.6 6.8 %all-to-all-done.got = f32[16,48,128]{2,1,0:T(8,128)} async-done(((f32[16,48,128]{2,1,0:T(8,128)}), f32[16,48,128]{2,1,0:T(8,128)}, u32[]{:S(2)}, u32[]{:S(2)}) %all-to-all-start) | async-done | bytes 393248 | tf_op jit(solution)/shard_map/all_to_all | solution.py:300
  25.4 2.2 %landmark.1 = f32[16,16,128]{2,1,0:T(8,128)} custom-call(f32[16,48,128]{2,1,0:T(8,128)} %all-to-all-done.got), custom_call_target="tpu_custom_call" | custom-call | tf_op jit(solution)/shard_map/landmark/pallas_call | solution.py:301
  27.6 7.2 %all-to-all-start.1 = ((f32[16,16,128]{2,1,0:T(8,128)}), f32[16,16,128]{2,1,0:T(8,128)S(1)}, u32[]{:S(2)}, u32[]{:S(2)}) async-start(f32[16,16,128]{2,1,0:T(8,128)} %landmark.1), calls=%async_computation.1 | async-start | bytes 262144 | tf_op jit(solution)/shard_map/all_to_all | solution.py:306
  34.9 8.6 %all-to-all-done.1 = f32[16,16,128]{2,1,0:T(8,128)S(1)} async-done(((f32[16,16,128]{2,1,0:T(8,128)}), f32[16,16,128]{2,1,0:T(8,128)S(1)}, u32[]{:S(2)}, u32[]{:S(2)}) %all-to-all-start.1) | async-done | bytes 131104 | tf_op jit(solution)/shard_map/all_to_all | solution.py:306
  43.6 1.6 %collective-permute-start.3 = (f32[512,512]{1,0:T(8,128)S(1)}, f32[512,512]{1,0:T(8,128)}, u32[]{:S(2)}, u32[]{:S(2)}) collective-permute-start(f32[512,512]{1,0:T(8,128)S(1)} %fusion.5.two), channel_id=1, source_target_pairs={{4,2},{12,10},{20,18},{28,26},{37,39},{45,47},{53,55},{61,63},{68,... | collective-permute-start | bytes 3145736 | tf_op jit(solution)/shard_map/ppermute | solution.py:109
  45.3 1.7 %collective-permute-start.4 = (f32[512,512]{1,0:T(8,128)S(1)}, f32[512,512]{1,0:T(8,128)}, u32[]{:S(2)}, u32[]{:S(2)}) collective-permute-start(f32[512,512]{1,0:T(8,128)S(1)} %fusion.5.two), channel_id=1, source_target_pairs={{0,2},{8,10},{16,18},{24,26},{33,39},{41,47},{49,55},{57,63},{64,6... | collective-permute-start | bytes 3145736 | tf_op jit(solution)/shard_map/ppermute | solution.py:109
  47.0 1.6 %collective-permute-start.2 = (f32[512,512]{1,0:T(8,128)}, f32[512,512]{1,0:T(8,128)}, u32[]{:S(2)}, u32[]{:S(2)}) collective-permute-start(f32[512,512]{1,0:T(8,128)} %collective-permute-done.1), channel_id=1, source_target_pairs={{4,2},{12,10},{20,18},{28,26},{37,39},{45,47},{53,55},{61,63},{68,... | collective-permute-start | bytes 3145736 | tf_op jit(solution)/shard_map/ppermute | solution.py:109
  48.6 1.2 convolution_add_fusion.5
  49.8 0.7 collective-permute-start.6
  50.4 1.3 collective-permute-start.5
  51.8 0.4 convolution_add_fusion.3
  52.2 0.7 collective-permute-start.7
  52.9 19.1 %collective-permute-done.5 = f32[64,512]{1,0:T(8,128)S(1)} collective-permute-done((f32[64,512]{1,0:T(8,128)S(1)}, f32[64,512]{1,0:T(8,128)S(1)}, u32[]{:S(2)}, u32[]{:S(2)}) %collective-permute-start.5) | collective-permute-done | bytes 131104 | tf_op jit(solution)/shard_map/ppermute | solution.py:109
  72.0 0.7 collective-permute-start.8
  72.7 1.1 convolution_add_fusion.4.off_own
  73.8 0.7 collective-permute-start.9
  74.4 0.7 broadcast_select_fusion.6
  75.2 0.6 copy-done.7
  75.8 4.7 %sweep.1 = (f32[64,512]{1,0:T(8,128)}, f32[64,512]{1,0:T(8,128)}, f32[64,512]{1,0:T(8,128)}, f32[64,512]{1,0:T(8,128)}, f32[64,512]{1,0:T(8,128)}) custom-call(s32[1]{0:T(128)} %bitcast.2.flag, f32[512,512]{1,0:T(8,128)} %copy-done.2, f32[512,512]{1,0:T(8,128)} %collective-permute-done.2.last, f32[512,512]{1,0:T(8,128)} %collective-permute-done.3.far, ...), custom_call_target="tpu_custom_call" | custom-call | tf_op jit(solution)/shard_map/sweep/pallas_call | solution.py:234
  80.6 9.1 %compose.1 = (f32[576,512]{1,0:T(8,128)}, f32[576,512]{1,0:T(8,128)}, f32[512,512]{1,0:T(8,128)}) custom-call(s32[1]{0:T(128)} %bitcast.2.flag, f32[512,512]{1,0:T(8,128)} %copy-done.2, f32[512,512]{1,0:T(8,128)} %collective-permute-done.2.last, f32[512,512]{1,0:T(8,128)} %collective-permute-done.3.far, f32[512,512]{1,0:T(8,128)} %collective-permute-done.4.near, ...), custom_call_target="tpu_custom_call" | custom-call | tf_op jit(solution)/shard_map/compose/pallas_call | solution.py:180
  89.7 1.7 %collective-permute-start.16 = (f32[576,512]{1,0:T(8,128)}, f32[576,512]{1,0:T(8,128)}, u32[]{:S(2)}, u32[]{:S(2)}) collective-permute-start(f32[576,512]{1,0:T(8,128)} %get-tuple-element.20), channel_id=1, source_target_pairs={{2,0},{10,8},{18,16},{26,24},{39,33},{47,41},{55,49},{63,57},{66,6... | collective-permute-start | bytes 3538952 | tf_op jit(solution)/shard_map/ppermute | solution.py:109
  91.4 1.7 %collective-permute-start.18 = (f32[576,512]{1,0:T(8,128)}, f32[576,512]{1,0:T(8,128)}, u32[]{:S(2)}, u32[]{:S(2)}) collective-permute-start(f32[576,512]{1,0:T(8,128)} %get-tuple-element.21), channel_id=1, source_target_pairs={{39,35},{47,43},{55,51},{63,59},{103,99},{111,107},{119,115},{127,... | collective-permute-start | bytes 3538952 | tf_op jit(solution)/shard_map/ppermute | solution.py:109
  93.1 1.7 %collective-permute-start.17 = (f32[512,512]{1,0:T(8,128)S(1)}, f32[512,512]{1,0:T(8,128)}, u32[]{:S(2)}, u32[]{:S(2)}) collective-permute-start(f32[512,512]{1,0:T(8,128)S(1)} %copy-done.3), channel_id=1, source_target_pairs={{39,37},{47,45},{55,53},{63,61},{103,101},{111,109},{119,117},{127... | collective-permute-start | bytes 3145736 | tf_op jit(solution)/shard_map/ppermute | solution.py:109
  94.7 1.3 collective-permute-start.10
  96.0 2.0 %hop.2.kept = f32[64,512]{1,0:T(8,128)} custom-call(s32[1]{0:T(128)} %bitcast.1.flag, f32[64,512]{1,0:T(8,128)} %collective-permute-done.10.arrived, f32[512,512]{1,0:T(8,128)} %get-tuple-element.18.eight, f32[64,512]{1,0:T(8,128)} %get-tuple-element.19.total, f32[64,512]{1,0:T(8,128)} %get-tuple-element.15.kept), custom_call_target="tpu_custom_call" | custom-call | tf_op jit(solution)/shard_map/hop/pallas_call | solution.py:257
  98.0 1.3 collective-permute-start.11
  99.3 2.0 %hop.3 = f32[64,512]{1,0:T(8,128)} custom-call(s32[1]{0:T(128)} %bitcast.flag, f32[64,512]{1,0:T(8,128)} %collective-permute-done.11.arrived, f32[512,512]{1,0:T(8,128)} %get-tuple-element.18.eight, f32[64,512]{1,0:T(8,128)} %get-tuple-element.19.total, f32[64,512]{1,0:T(8,128)} %hop.2.kept), custom_call_target="tpu_custom_call" | custom-call | tf_op jit(solution)/shard_map/hop/pallas_call | solution.py:257
  101.3 1.3 collective-permute-start.12
  102.6 1.3 collective-permute-start.13
  103.9 1.3 collective-permute-start.14
  105.2 1.3 collective-permute-start.15
  106.5 0.8 collective-permute-start.19
  107.3 1.2 select_add_fusion
  108.5 1.1 fusion.7
  109.6 2.5 %fusion.4 = f32[512,512]{1,0:T(8,128)S(1)} fusion(f32[576,512]{1,0:T(8,128)} %collective-permute-done.18, f32[576,512]{1,0:T(8,128)} %collective-permute-done.16, f32[576,512]{1,0:T(8,128)S(1)} %copy-done.4, f32[512,512]{1,0:T(8,128)} %collective-permute-done.1, f32[512,512]{1,0:T(8,128)} %collective-permute-done.17, pred[]{:T(512)S(6)} %eq.57, pred[]{:T(512)S(6)} %eq.56, ...), kind=kLoop, calls=%fused_computation.12 | loop fusion | flops 1048576 | bytes 6291459 | tf_op jit(solution)/shard_map/jit(_where)/select_n | solution.py:361
  112.1 0.5 fusion.2
  113.0 0.4 broadcast_select_fusion.4
  113.5 1.3 collective-permute-start.20
  114.8 37.5 %collective-permute-done.20 = f32[64,512]{1,0:T(8,128)S(1)} collective-permute-done((f32[64,512]{1,0:T(8,128)S(1)}, f32[64,512]{1,0:T(8,128)S(1)}, u32[]{:S(2)}, u32[]{:S(2)}) %collective-permute-start.20) | collective-permute-done | bytes 131104 | tf_op jit(solution)/shard_map/ppermute | solution.py:109
  152.3 1.1 fusion.1
  153.4 1.4 fusion
  (49 shorter events, 0.9 us)
Async XLA Ops:
  0.6 152.8 %copy-start = (f32[1,1,64,512]{3,2,1,0:T(8,128)S(1)}, f32[1,1,64,512]{3,2,1,0:T(8,128)}, u32[]{:S(2)}) copy-start(f32[1,1,64,512]{3,2,1,0:T(8,128)} %param.8) | copy-start | bytes 393220
  0.6 2.9 %copy-start.9 = (f32[1,1,64,32]{2,3,1,0:T(8,128)S(1)}, f32[1,1,64,32]{2,3,1,0:T(8,128)}, u32[]{:S(2)}) copy-start(f32[1,1,64,32]{2,3,1,0:T(8,128)} %param.12) | copy-start | bytes 24580
  0.7 14.3 %collective-permute-start = (f32[512,512]{1,0:T(8,128)}, f32[512,512]{1,0:T(8,128)S(1)}, u32[]{:S(2)}, u32[]{:S(2)}) collective-permute-start(f32[512,512]{1,0:T(8,128)} %bitcast.49), channel_id=1, source_target_pairs={{1,0},{3,2},{5,4},{7,6},{9,8},{11,10},{13,12},{15,14},{17,16},{19,... | collective-permute-start | bytes 3145736 | tf_op jit(solution)/shard_map/ppermute | solution.py:109
  3.5 11.5 %copy-start.1 = (f32[1,1,512,512]{3,2,1,0:T(8,128)S(1)}, f32[1,1,512,512]{3,2,1,0:T(8,128)}, u32[]{:S(2)}) copy-start(f32[1,1,512,512]{3,2,1,0:T(8,128)} %param.7) | copy-start | bytes 3145732
  4.4 21.0 %all-to-all-start = ((f32[16,48,128]{2,1,0:T(8,128)}), f32[16,48,128]{2,1,0:T(8,128)}, u32[]{:S(2)}, u32[]{:S(2)}) async-start(f32[16,48,128]{2,1,0:T(8,128)} %pad_maximum_fusion), calls=%async_computation | async-start | bytes 786432 | tf_op jit(solution)/shard_map/all_to_all | solution.py:300
  11.7 23.2 %copy-start.10 = (f32[1,512]{1,0:T(1,128)S(1)}, f32[1,512]{1,0:T(1,128)}, u32[]{:S(2)}) copy-start(f32[1,512]{1,0:T(1,128)} %param.13) | copy-start | bytes 6148
  16.9 35.3 %copy-start.2 = (f32[512,512]{1,0:T(8,128)}, f32[512,512]{1,0:T(8,128)S(1)}, u32[]{:S(2)}) copy-start(f32[512,512]{1,0:T(8,128)S(1)} %fusion.5.two) | copy-start | bytes 3145732
  16.9 30.1 %collective-permute-start.1 = (f32[512,512]{1,0:T(8,128)S(1)}, f32[512,512]{1,0:T(8,128)}, u32[]{:S(2)}, u32[]{:S(2)}) collective-permute-start(f32[512,512]{1,0:T(8,128)S(1)} %fusion.5.two), channel_id=1, source_target_pairs={{6,4},{14,12},{22,20},{30,28},{35,37},{43,45},{51,53},{59,61},{70,... | collective-permute-start | bytes 3145736 | tf_op jit(solution)/shard_map/ppermute | solution.py:109
  27.6 15.9 %all-to-all-start.1 = ((f32[16,16,128]{2,1,0:T(8,128)}), f32[16,16,128]{2,1,0:T(8,128)S(1)}, u32[]{:S(2)}, u32[]{:S(2)}) async-start(f32[16,16,128]{2,1,0:T(8,128)} %landmark.1), calls=%async_computation.1 | async-start | bytes 262144 | tf_op jit(solution)/shard_map/all_to_all | solution.py:306
  43.6 31.5 %collective-permute-start.3 = (f32[512,512]{1,0:T(8,128)S(1)}, f32[512,512]{1,0:T(8,128)}, u32[]{:S(2)}, u32[]{:S(2)}) collective-permute-start(f32[512,512]{1,0:T(8,128)S(1)} %fusion.5.two), channel_id=1, source_target_pairs={{4,2},{12,10},{20,18},{28,26},{37,39},{45,47},{53,55},{61,63},{68,... | collective-permute-start | bytes 3145736 | tf_op jit(solution)/shard_map/ppermute | solution.py:109
  45.3 29.9 %collective-permute-start.4 = (f32[512,512]{1,0:T(8,128)S(1)}, f32[512,512]{1,0:T(8,128)}, u32[]{:S(2)}, u32[]{:S(2)}) collective-permute-start(f32[512,512]{1,0:T(8,128)S(1)} %fusion.5.two), channel_id=1, source_target_pairs={{0,2},{8,10},{16,18},{24,26},{33,39},{41,47},{49,55},{57,63},{64,6... | collective-permute-start | bytes 3145736 | tf_op jit(solution)/shard_map/ppermute | solution.py:109
  47.0 28.2 %collective-permute-start.2 = (f32[512,512]{1,0:T(8,128)}, f32[512,512]{1,0:T(8,128)}, u32[]{:S(2)}, u32[]{:S(2)}) collective-permute-start(f32[512,512]{1,0:T(8,128)} %collective-permute-done.1), channel_id=1, source_target_pairs={{4,2},{12,10},{20,18},{28,26},{37,39},{45,47},{53,55},{61,63},{68,... | collective-permute-start | bytes 3145736 | tf_op jit(solution)/shard_map/ppermute | solution.py:109
  49.8 2.0 %collective-permute-start.6 = (f32[64,512]{1,0:T(8,128)S(1)}, f32[64,512]{1,0:T(8,128)S(1)}, u32[]{:S(2)}, u32[]{:S(2)}) collective-permute-start(f32[64,512]{1,0:T(8,128)S(1)} %convolution_add_fusion.5), channel_id=1, source_target_pairs={{1,0},{5,4},{7,6},{9,8},{13,12},{15,14},{17,16},{21,20},{23,22},{2... | collective-permute-start | bytes 393224 | tf_op jit(solution)/shard_map/ppermute | solution.py:109
  50.4 21.6 %collective-permute-start.5 = (f32[64,512]{1,0:T(8,128)S(1)}, f32[64,512]{1,0:T(8,128)S(1)}, u32[]{:S(2)}, u32[]{:S(2)}) collective-permute-start(f32[64,512]{1,0:T(8,128)S(1)} %convolution_add_fusion.5), channel_id=1, source_target_pairs={{3,2},{11,10},{19,18},{27,26},{38,39},{46,47},{54,55},{62,63},{67,... | collective-permute-start | bytes 393224 | tf_op jit(solution)/shard_map/ppermute | solution.py:109
  52.2 21.6 %collective-permute-start.7 = (f32[64,512]{1,0:T(8,128)S(1)}, f32[64,512]{1,0:T(8,128)S(1)}, u32[]{:S(2)}, u32[]{:S(2)}) collective-permute-start(f32[64,512]{1,0:T(8,128)S(1)} %convolution_add_fusion.3), channel_id=1, source_target_pairs={{6,2},{14,10},{22,18},{30,26},{35,39},{43,47},{51,55},{59,63},{70,... | collective-permute-start | bytes 393224 | tf_op jit(solution)/shard_map/ppermute | solution.py:109
  72.0 3.1 %collective-permute-start.8 = (f32[64,512]{1,0:T(8,128)S(1)}, f32[64,512]{1,0:T(8,128)S(1)}, u32[]{:S(2)}, u32[]{:S(2)}) collective-permute-start(f32[64,512]{1,0:T(8,128)S(1)} %convolution_add_fusion.3), channel_id=1, source_target_pairs={{4,2},{12,10},{20,18},{28,26},{37,39},{45,47},{53,55},{61,63},{68,... | collective-permute-start | bytes 393224 | tf_op jit(solution)/shard_map/ppermute | solution.py:109
  73.8 1.4 copy-start.6
  73.8 1.4 collective-permute-start.9
  75.1 0.6 copy-start.7
  75.1 0.7 copy-start.8
  80.5 12.5 %copy-start.3 = (f32[512,512]{1,0:T(8,128)S(1)}, f32[512,512]{1,0:T(8,128)}, u32[]{:S(2)}) copy-start(f32[512,512]{1,0:T(8,128)} %copy-done.2) | copy-start | bytes 3145732
  89.7 18.8 %collective-permute-start.16 = (f32[576,512]{1,0:T(8,128)}, f32[576,512]{1,0:T(8,128)}, u32[]{:S(2)}, u32[]{:S(2)}) collective-permute-start(f32[576,512]{1,0:T(8,128)} %get-tuple-element.20), channel_id=1, source_target_pairs={{2,0},{10,8},{18,16},{26,24},{39,33},{47,41},{55,49},{63,57},{66,6... | collective-permute-start | bytes 3538952 | tf_op jit(solution)/shard_map/ppermute | solution.py:109
  91.4 17.2 %collective-permute-start.18 = (f32[576,512]{1,0:T(8,128)}, f32[576,512]{1,0:T(8,128)}, u32[]{:S(2)}, u32[]{:S(2)}) collective-permute-start(f32[576,512]{1,0:T(8,128)} %get-tuple-element.21), channel_id=1, source_target_pairs={{39,35},{47,43},{55,51},{63,59},{103,99},{111,107},{119,115},{127,... | collective-permute-start | bytes 3538952 | tf_op jit(solution)/shard_map/ppermute | solution.py:109
  93.1 16.6 %collective-permute-start.17 = (f32[512,512]{1,0:T(8,128)S(1)}, f32[512,512]{1,0:T(8,128)}, u32[]{:S(2)}, u32[]{:S(2)}) collective-permute-start(f32[512,512]{1,0:T(8,128)S(1)} %copy-done.3), channel_id=1, source_target_pairs={{39,37},{47,45},{55,53},{63,61},{103,101},{111,109},{119,117},{127... | collective-permute-start | bytes 3145736 | tf_op jit(solution)/shard_map/ppermute | solution.py:109
  94.7 1.3 collective-permute-start.10
  98.0 1.3 collective-permute-start.11
  101.3 2.6 %collective-permute-start.12 = (f32[64,512]{1,0:T(8,128)}, f32[64,512]{1,0:T(8,128)}, u32[]{:S(2)}, u32[]{:S(2)}) collective-permute-start(f32[64,512]{1,0:T(8,128)} %hop.3), channel_id=1, source_target_pairs={{10,6},{18,14},{26,22},{47,35},{55,43},{63,51},{74,70},{82,78},{90... | collective-permute-start | bytes 393224 | tf_op jit(solution)/shard_map/ppermute | solution.py:109
  102.6 2.6 %collective-permute-start.13 = (f32[64,512]{1,0:T(8,128)}, f32[64,512]{1,0:T(8,128)}, u32[]{:S(2)}, u32[]{:S(2)}) collective-permute-start(f32[64,512]{1,0:T(8,128)} %hop.3), channel_id=1, source_target_pairs={{10,0},{18,8},{26,16},{47,33},{55,41},{63,49},{74,64},{82,72},{90,... | collective-permute-start | bytes 393224 | tf_op jit(solution)/shard_map/ppermute | solution.py:109
  103.9 2.6 %collective-permute-start.14 = (f32[64,512]{1,0:T(8,128)}, f32[64,512]{1,0:T(8,128)}, u32[]{:S(2)}, u32[]{:S(2)}) collective-permute-start(f32[64,512]{1,0:T(8,128)} %hop.3), channel_id=1, source_target_pairs={{10,4},{18,12},{26,20},{47,37},{55,45},{63,53},{74,68},{82,76},{90... | collective-permute-start | bytes 393224 | tf_op jit(solution)/shard_map/ppermute | solution.py:109
  105.2 2.1 %collective-permute-start.15 = (f32[64,512]{1,0:T(8,128)}, f32[64,512]{1,0:T(8,128)}, u32[]{:S(2)}, u32[]{:S(2)}) collective-permute-start(f32[64,512]{1,0:T(8,128)} %hop.3), channel_id=1, source_target_pairs={{10,2},{18,10},{26,18},{47,39},{55,47},{63,55},{74,66},{82,74},{90... | collective-permute-start | bytes 393224 | tf_op jit(solution)/shard_map/ppermute | solution.py:109
  106.5 3.2 %copy-start.4 = (f32[576,512]{1,0:T(8,128)S(1)}, f32[576,512]{1,0:T(8,128)}, u32[]{:S(2)}) copy-start(f32[576,512]{1,0:T(8,128)} %get-tuple-element.21) | copy-start | bytes 3538948
  106.5 2.0 %collective-permute-start.19 = (f32[64,512]{1,0:T(8,128)}, f32[64,512]{1,0:T(8,128)S(1)}, u32[]{:S(2)}, u32[]{:S(2)}) collective-permute-start(f32[64,512]{1,0:T(8,128)} %get-tuple-element.22), channel_id=1, source_target_pairs={{2,4},{10,12},{18,20},{26,28},{39,37},{47,45},{55,53},{63,61},{66,... | collective-permute-start | bytes 393224 | tf_op jit(solution)/shard_map/ppermute | solution.py:109
  112.1 0.9 copy-start.5
  113.5 38.8 %collective-permute-start.20 = (f32[64,512]{1,0:T(8,128)S(1)}, f32[64,512]{1,0:T(8,128)S(1)}, u32[]{:S(2)}, u32[]{:S(2)}) collective-permute-start(f32[64,512]{1,0:T(8,128)S(1)} %get-tuple-element.30), channel_id=1, source_target_pairs={{0,1},{2,3},{4,5},{6,7},{8,9},{10,11},{12,13},{14,15},{16,17},{18,... | collective-permute-start | bytes 393224 | tf_op jit(solution)/shard_map/ppermute | solution.py:109

commit v5 on v4

--- a/solution.py
+++ b/solution.py
@@ -180,7 +180,9 @@
     return pl.pallas_call(
         compose_kernel,
         out_shape=[jax.ShapeDtypeStruct(shape, jnp.float32) for shape in (TALL, TALL, SQUARE)],
-        in_specs=[pl.BlockSpec(memory_space=pltpu.SMEM)] + [pl.BlockSpec(memory_space=pl.ANY)] * 6,
+        in_specs=[pl.BlockSpec(memory_space=pltpu.SMEM)]
+        + [pl.BlockSpec(memory_space=pl.ANY)] * 4
+        + [pl.BlockSpec(memory_space=pltpu.VMEM)] * 2,
         out_specs=[pl.BlockSpec(memory_space=pl.ANY)] * 3,
         scratch_shapes=[pltpu.VMEM(SQUARE, jnp.float32)] * 7
         + [pltpu.SemaphoreType.DMA((4,)), pltpu.SemaphoreType.DMA((5,))],
@@ -261,6 +263,75 @@
         out_specs=pl.BlockSpec(memory_space=pltpu.VMEM),
         name="hop",
     )(flag, arrived, eight, total, kept)
+
+
+def enter_kernel(
+    code, got0, got1, got2, got3, start, driven_high,
+    near_map, far_pass, far_map, own_map, last_map, far_shift, matrix, other,
+    passing, running, m, shift, mh, sems,
+):
+    load = copier(sems)
+    role, is_last, even = code[0] % 8, (code[0] // 8) % 2 == 1, code[0] // 16 == 1
+    map_rows, shift_rows = pl.ds(0, TEAM_STATES), pl.ds(TEAM_STATES, COLS)
+
+    def fetch(table, offsets):
+        load(table, m, 0).start()
+        load(offsets, shift, 1).start()
+
+    @pl.when(jnp.logical_or(role == 0, role == 4))
+    def _():
+        fetch(own_map.at[map_rows], own_map.at[shift_rows])
+
+    @pl.when(role == 1)
+    def _():
+        fetch(near_map.at[map_rows], near_map.at[shift_rows])
+
+    @pl.when(role == 2)
+    def _():
+        fetch(far_pass, far_shift)
+
+    @pl.when(role == 3)
+    def _():
+        fetch(far_map, far_shift)
+
+    @pl.when(role == 5)
+    def _():
+        fetch(last_map.at[map_rows], last_map.at[shift_rows])
+
+    @pl.when(even)
+    def _():
+        load(other, mh, 2).start()
+
+    @pl.when(jnp.logical_not(even))
+    def _():
+        load(matrix, mh, 2).start()
+
+    entry = (got0[...] + got1[...]) + (got2[...] + got3[...]) + jnp.where(is_last, start[...], 0.0)
+    load(far_pass, m, 0).wait()
+    load(far_shift, shift, 1).wait()
+    enter = jnp.where(role == 0, entry, product(split(entry), split(m[...])) + shift[...])
+    load(other, mh, 2).wait()
+    middle = product(split(enter), split(mh[...])) + driven_high[...]
+    passing[...] = jnp.where(even, enter, middle)
+    running[...] = jnp.where(even, middle, enter)
+
+
+def enter_pair(code, rows, tables):
+    return pl.pallas_call(
+        enter_kernel,
+        out_shape=[jax.ShapeDtypeStruct(ROWS, jnp.float32)] * 2,
+        in_specs=[pl.BlockSpec(memory_space=pltpu.SMEM)]
+        + [pl.BlockSpec(memory_space=pltpu.VMEM)] * 6
+        + [pl.BlockSpec(memory_space=pl.ANY)] * 8,
+        out_specs=[pl.BlockSpec(memory_space=pltpu.VMEM)] * 2,
+        scratch_shapes=[
+            pltpu.VMEM(SQUARE, jnp.float32),
+            pltpu.VMEM(ROWS, jnp.float32),
+            pltpu.VMEM(SQUARE, jnp.float32),
+            pltpu.SemaphoreType.DMA((3,)),
+        ],
+        name="enter",
+    )(code, *rows, *tables)
 
 
 def landmark_kernel(got, part):
@@ -355,23 +426,18 @@
         send(out, down(own_pair)),
     ]
     pair = (step % RING) // 2
-
-    def mine(rows, at_far):
-        here = pick(enter1[rows], map_last[rows])
-        return jnp.where(pair == NEAR, map_near[rows], jnp.where(pair == FAR, at_far, here))
-
-    enter_map = mine(slice(0, TEAM_STATES), pick(passing, map_far))
-    enter_shift = mine(slice(TEAM_STATES, None), shift_far)
-    enter_map, enter_shift = lax.optimization_barrier((enter_map, enter_shift))
-    entry = (arrived[0] + arrived[1]) + (arrived[2] + arrived[3]) + jnp.where(ring == last_ring, terminal[0], 0.0)
-    entry = lax.optimization_barrier(entry)
-    enter = jnp.where(pair == 3, entry, matmul(entry, enter_map) + enter_shift)
-    enter = lax.optimization_barrier(enter)
-    driven_high = jnp.where(pair == pick(own_pair(0), own_pair(1)), own_later, later)
-    middle = matmul(enter, high) + driven_high
-    passed = send(pick(enter, middle), TO_PARTNER)
+    is_own = pair == pick(own_pair(0), own_pair(1))
+    driven_high = lax.optimization_barrier(jnp.where(is_own, own_later, later))
+    role = jnp.where(pair == NEAR, 1, jnp.where(pair == FAR, pick(2, 3), jnp.where(pair == 3, 0, pick(4, 5))))
+    code = role + 8 * (ring == last_ring).astype(jnp.int32) + 16 * even.astype(jnp.int32)
+    passing_on, held = enter_pair(
+        code.astype(jnp.int32)[None],
+        (*arrived, terminal[0], driven_high),
+        (map_near, passing, map_far, enter1, map_last, shift_far, matrix, other_matrix),
+    )
+    passed = send(passing_on, TO_PARTNER)
     holds = step % 2 == team % 2
-    running = jnp.where(holds, pick(middle, enter), passed)
+    running = jnp.where(holds, held, passed)
     running = lax.optimization_barrier(running)
     grad = jnp.einsum("cn,cm->nm", running, state, precision=HIGH).astype(jnp.bfloat16)
     adjoint = matmul(running, matrix) + driven

time: 156 us -> 151 us (0.968)
  the two profiles are of different devices: /device:TPU:192 before, /device:TPU:1 now
where the time goes in v5:
time: 151 us; the launch traced here: 150 us
  waiting for transfers between devices  67.1 us (44%)
  starting transfers between devices  46.8 us (31%)
  Pallas kernels  21.9 us (15%)
  matrix products  7.08 us (5%)
  local copies, waits for them, and re-layouts  3.26 us (2%)
  other arithmetic  2.57 us (2%)
    ppermute x21, waiting for transfers between devices, send(): return lax.ppermute(value, BOTH, pairs)  50.4 us
    ppermute x21, starting transfers between devices, send(): return lax.ppermute(value, BOTH, pairs)  36.2 us
    all_to_all x1, waiting for transfers between devices, shards(): parts = lax.all_to_all(part, 'team', 0, 0, tiled=True)  8.33 us
    all_to_all x1, waiting for transfers between devices, shards(): lax.all_to_all(jnp.concatenate([slices, packed], axis=1), 'team', 0, 0, t...  8.29 us
    all_to_all x1, starting transfers between devices, shards(): lax.all_to_all(jnp.concatenate([slices, packed], axis=1), 'team', 0, 0, t...  7.23 us
    pallas_call x1, Pallas kernels, compose(): pl.pallas_call(compose_kernel, out_shape=[jax.ShapeDtypeStruct(shape, jnp...  6.98 us
    pallas_call x1, Pallas kernels, sweep(): pl.pallas_call(sweep_kernel, out_shape=[jax.ShapeDtypeStruct(ROWS, jnp.fl...  4.72 us
    pallas_call x1, Pallas kernels, enter_pair(): pl.pallas_call(enter_kernel, out_shape=[jax.ShapeDtypeStruct(ROWS, jnp.fl...  4.06 us
  transfers between devices with their start and end apart: 23, of which 5 were waited for; matrix products, arithmetic and copies ran while one was open for 5% of the time, Pallas kernels for 12%

profile of v5, /device:TPU:1, one launch (start us, length us, event | category | flops | bytes accessed | tf_op | source)
XLA Modules:
  0.0 150.0 jit_solution(18250589927385558643)
XLA Ops:
  0.7 5.0 %collective-permute-start = (f32[512,512]{1,0:T(8,128)}, f32[512,512]{1,0:T(8,128)S(1)}, u32[]{:S(2)}, u32[]{:S(2)}) collective-permute-start(f32[512,512]{1,0:T(8,128)} %bitcast.46), channel_id=1, source_target_pairs={{1,0},{3,2},{5,4},{7,6},{9,8},{11,10},{13,12},{15,14},{17,16},{19,... | collective-permute-start | bytes 3145736 | tf_op jit(solution)/shard_map/ppermute | solution.py:109
  5.7 1.0 convert_bitcast_fusion
  6.7 0.1 copy.12
  6.9 0.8 pad_maximum_fusion
  7.7 7.2 %all-to-all-start = ((f32[16,48,128]{2,1,0:T(8,128)}), f32[16,48,128]{2,1,0:T(8,128)}, u32[]{:S(2)}, u32[]{:S(2)}) async-start(f32[16,48,128]{2,1,0:T(8,128)} %pad_maximum_fusion), calls=%async_computation | async-start | bytes 786432 | tf_op jit(solution)/shard_map/all_to_all | solution.py:371
  14.9 2.7 %collective-permute-done.other = f32[512,512]{1,0:T(8,128)S(1)} collective-permute-done((f32[512,512]{1,0:T(8,128)}, f32[512,512]{1,0:T(8,128)S(1)}, u32[]{:S(2)}, u32[]{:S(2)}) %collective-permute-start) | collective-permute-done | bytes 1048608 | tf_op jit(solution)/shard_map/ppermute | solution.py:109
  17.7 1.9 %fusion.2.two = f32[512,512]{1,0:T(8,128)S(1)} fusion(f32[512,512]{1,0:T(8,128)S(1)} %collective-permute-done.other, pred[]{:T(512)S(6)} %eq.48, f32[1,1,512,512]{3,2,1,0:T(8,128)S(1)} %copy-done.1), kind=kOutput, calls=%fused_computation.7 | convolution fusion | flops 1611137024 | bytes 3145729 | tf_op jit(solution)/shard_map/dot_general | solution.py:382
  19.6 1.7 %collective-permute-start.1 = (f32[512,512]{1,0:T(8,128)S(1)}, f32[512,512]{1,0:T(8,128)}, u32[]{:S(2)}, u32[]{:S(2)}) collective-permute-start(f32[512,512]{1,0:T(8,128)S(1)} %fusion.2.two), channel_id=1, source_target_pairs={{6,4},{14,12},{22,20},{30,28},{35,37},{43,45},{51,53},{59,61},{70,... | collective-permute-start | bytes 3145736 | tf_op jit(solution)/shard_map/ppermute | solution.py:109
  21.3 8.3 %all-to-all-done.got = f32[16,48,128]{2,1,0:T(8,128)} async-done(((f32[16,48,128]{2,1,0:T(8,128)}), f32[16,48,128]{2,1,0:T(8,128)}, u32[]{:S(2)}, u32[]{:S(2)}) %all-to-all-start) | async-done | bytes 393248 | tf_op jit(solution)/shard_map/all_to_all | solution.py:371
  29.5 2.2 %landmark.1 = f32[16,16,128]{2,1,0:T(8,128)} custom-call(f32[16,48,128]{2,1,0:T(8,128)} %all-to-all-done.got), custom_call_target="tpu_custom_call" | custom-call | tf_op jit(solution)/shard_map/landmark/pallas_call | solution.py:372
  31.8 3.4 %all-to-all-start.1 = ((f32[16,16,128]{2,1,0:T(8,128)}), f32[16,16,128]{2,1,0:T(8,128)S(1)}, u32[]{:S(2)}, u32[]{:S(2)}) async-start(f32[16,16,128]{2,1,0:T(8,128)} %landmark.1), calls=%async_computation.1 | async-start | bytes 262144 | tf_op jit(solution)/shard_map/all_to_all | solution.py:377
  35.2 8.3 %all-to-all-done.1 = f32[16,16,128]{2,1,0:T(8,128)S(1)} async-done(((f32[16,16,128]{2,1,0:T(8,128)}), f32[16,16,128]{2,1,0:T(8,128)S(1)}, u32[]{:S(2)}, u32[]{:S(2)}) %all-to-all-start.1) | async-done | bytes 131104 | tf_op jit(solution)/shard_map/all_to_all | solution.py:377
  43.7 1.7 %collective-permute-start.3 = (f32[512,512]{1,0:T(8,128)S(1)}, f32[512,512]{1,0:T(8,128)}, u32[]{:S(2)}, u32[]{:S(2)}) collective-permute-start(f32[512,512]{1,0:T(8,128)S(1)} %fusion.2.two), channel_id=1, source_target_pairs={{4,2},{12,10},{20,18},{28,26},{37,39},{45,47},{53,55},{61,63},{68,... | collective-permute-start | bytes 3145736 | tf_op jit(solution)/shard_map/ppermute | solution.py:109
  45.4 1.6 %collective-permute-start.4 = (f32[512,512]{1,0:T(8,128)S(1)}, f32[512,512]{1,0:T(8,128)}, u32[]{:S(2)}, u32[]{:S(2)}) collective-permute-start(f32[512,512]{1,0:T(8,128)S(1)} %fusion.2.two), channel_id=1, source_target_pairs={{0,2},{8,10},{16,18},{24,26},{33,39},{41,47},{49,55},{57,63},{64,6... | collective-permute-start | bytes 3145736 | tf_op jit(solution)/shard_map/ppermute | solution.py:109
  47.0 1.7 %collective-permute-start.2 = (f32[512,512]{1,0:T(8,128)}, f32[512,512]{1,0:T(8,128)}, u32[]{:S(2)}, u32[]{:S(2)}) collective-permute-start(f32[512,512]{1,0:T(8,128)} %collective-permute-done.1.far_pass), channel_id=1, source_target_pairs={{4,2},{12,10},{20,18},{28,26},{37,39},{45,47},{53,55},{61,63},{68,... | collective-permute-start | bytes 3145736 | tf_op jit(solution)/shard_map/ppermute | solution.py:109
  48.7 1.2 convolution_add_fusion.3
  49.8 11.7 %collective-permute-start.6 = (f32[64,512]{1,0:T(8,128)S(1)}, f32[64,512]{1,0:T(8,128)S(1)}, u32[]{:S(2)}, u32[]{:S(2)}) collective-permute-start(f32[64,512]{1,0:T(8,128)S(1)} %convolution_add_fusion.3), channel_id=1, source_target_pairs={{1,0},{5,4},{7,6},{9,8},{13,12},{15,14},{17,16},{21,20},{23,22},{2... | collective-permute-start | bytes 393224 | tf_op jit(solution)/shard_map/ppermute | solution.py:109
  61.5 0.7 collective-permute-start.5
  62.2 2.1 %collective-permute-done.6 = f32[64,512]{1,0:T(8,128)S(1)} collective-permute-done((f32[64,512]{1,0:T(8,128)S(1)}, f32[64,512]{1,0:T(8,128)S(1)}, u32[]{:S(2)}, u32[]{:S(2)}) %collective-permute-start.6) | collective-permute-done | bytes 131104 | tf_op jit(solution)/shard_map/ppermute | solution.py:109
  64.3 0.4 convolution_add_fusion.1
  64.7 0.7 collective-permute-start.7
  65.4 0.7 collective-permute-start.8
  66.1 1.1 convolution_add_fusion.2.off_own
  67.2 1.7 %collective-permute-start.17 = (f32[512,512]{1,0:T(8,128)S(1)}, f32[512,512]{1,0:T(8,128)}, u32[]{:S(2)}, u32[]{:S(2)}) collective-permute-start(f32[512,512]{1,0:T(8,128)S(1)} %fusion.2.two), channel_id=1, source_target_pairs={{39,37},{47,45},{55,53},{63,61},{103,101},{111,109},{119,117},{127... | collective-permute-start | bytes 3145736 | tf_op jit(solution)/shard_map/ppermute | solution.py:109
  68.9 0.7 collective-permute-start.9
  69.6 0.6 copy-done.15
  70.2 4.7 %sweep.1 = (f32[64,512]{1,0:T(8,128)}, f32[64,512]{1,0:T(8,128)}, f32[64,512]{1,0:T(8,128)}, f32[64,512]{1,0:T(8,128)}, f32[64,512]{1,0:T(8,128)}) custom-call(s32[1]{0:T(128)} %bitcast.3.flag, f32[512,512]{1,0:T(8,128)} %copy-done.4, f32[512,512]{1,0:T(8,128)} %collective-permute-done.2.last, f32[512,512]{1,0:T(8,128)} %collective-permute-done.3.far, ...), custom_call_target="tpu_custom_call" | custom-call | tf_op jit(solution)/shard_map/sweep/pallas_call | solution.py:236
  75.0 7.0 %compose.1 = (f32[576,512]{1,0:T(8,128)}, f32[576,512]{1,0:T(8,128)}, f32[512,512]{1,0:T(8,128)}) custom-call(s32[1]{0:T(128)} %bitcast.3.flag, f32[512,512]{1,0:T(8,128)} %copy-done.4, f32[512,512]{1,0:T(8,128)} %collective-permute-done.2.last, f32[512,512]{1,0:T(8,128)} %collective-permute-done.3.far, f32[512,512]{1,0:T(8,128)} %collective-permute-done.4.near, ...), custom_call_target="tpu_custom_call" | custom-call | tf_op jit(solution)/shard_map/compose/pallas_call | solution.py:180
  82.0 0.9 collective-permute-start.16
  82.8 1.7 %collective-permute-start.18 = (f32[576,512]{1,0:T(8,128)}, f32[576,512]{1,0:T(8,128)}, u32[]{:S(2)}, u32[]{:S(2)}) collective-permute-start(f32[576,512]{1,0:T(8,128)} %get-tuple-element.22.own_map), channel_id=1, source_target_pairs={{39,35},{47,43},{55,51},{63,59},{103,99},{111,107},{119,115},{127,... | collective-permute-start | bytes 3538952 | tf_op jit(solution)/shard_map/ppermute | solution.py:109
  84.5 0.7 collective-permute-start.10
  85.2 0.6 copy-done.13
  85.9 2.0 %hop.2.kept = f32[64,512]{1,0:T(8,128)} custom-call(s32[1]{0:T(128)} %bitcast.2.flag, f32[64,512]{1,0:T(8,128)} %copy-done.13, f32[512,512]{1,0:T(8,128)} %get-tuple-element.18.eight, f32[64,512]{1,0:T(8,128)} %get-tuple-element.19.total, f32[64,512]{1,0:T(8,128)} %get-tuple-element.15.kept), custom_call_target="tpu_custom_call" | custom-call | tf_op jit(solution)/shard_map/hop/pallas_call | solution.py:259
  87.9 0.7 collective-permute-start.11
  88.5 0.7 collective-permute-start.19
  89.2 0.6 copy-done.16
  89.9 1.9 %hop.3 = f32[64,512]{1,0:T(8,128)} custom-call(s32[1]{0:T(128)} %bitcast.1.flag, f32[64,512]{1,0:T(8,128)} %copy-done.16, f32[512,512]{1,0:T(8,128)} %get-tuple-element.18.eight, f32[64,512]{1,0:T(8,128)} %get-tuple-element.19.total, f32[64,512]{1,0:T(8,128)} %hop.2.kept), custom_call_target="tpu_custom_call" | custom-call | tf_op jit(solution)/shard_map/hop/pallas_call | solution.py:259
  91.8 0.7 collective-permute-start.12
  92.6 0.7 collective-permute-start.13
  93.3 0.7 collective-permute-start.14
  94.0 0.7 collective-permute-start.15
  94.6 0.7 broadcast_select_fusion.4.driven_high
  95.4 1.1 copy-done.5
  96.5 4.1 %enter.1 = (f32[64,512]{1,0:T(8,128)}, f32[64,512]{1,0:T(8,128)}) custom-call(s32[1]{0:T(128)} %bitcast.code, f32[64,512]{1,0:T(8,128)} %copy-done.7, f32[64,512]{1,0:T(8,128)} %copy-done.8, f32[64,512]{1,0:T(8,128)} %copy-done.9, f32[64,512]{1,0:T(8,128)} %copy-done.10, f32[64,512]{1,0:T(8,128)} %bitcast.51, f32[64,512]{1,0:T(8,128)} %broadcast_select_fusion.4.driven_high, ...), custom_call_target="tpu_custom_call" | custom-call | tf_op jit(solution)/shard_map/enter/pallas_call | solution.py:320
  100.5 1.3 collective-permute-start.20
  101.9 45.6 %collective-permute-done.20 = f32[64,512]{1,0:T(8,128)S(1)} collective-permute-done((f32[64,512]{1,0:T(8,128)}, f32[64,512]{1,0:T(8,128)S(1)}, u32[]{:S(2)}, u32[]{:S(2)}) %collective-permute-start.20) | collective-permute-done | bytes 131104 | tf_op jit(solution)/shard_map/ppermute | solution.py:109
  147.5 1.1 fusion.1
  148.6 1.4 fusion
  (64 shorter events, 0.4 us)
Async XLA Ops:
  0.6 148.0 %copy-start = (f32[1,1,64,512]{3,2,1,0:T(8,128)S(1)}, f32[1,1,64,512]{3,2,1,0:T(8,128)}, u32[]{:S(2)}) copy-start(f32[1,1,64,512]{3,2,1,0:T(8,128)} %param.8) | copy-start | bytes 393220
  0.6 6.2 %copy-start.17 = (f32[1,1,64,32]{2,3,1,0:T(8,128)S(1)}, f32[1,1,64,32]{2,3,1,0:T(8,128)}, u32[]{:S(2)}) copy-start(f32[1,1,64,32]{2,3,1,0:T(8,128)} %param.12) | copy-start | bytes 24580
  0.7 17.0 %collective-permute-start = (f32[512,512]{1,0:T(8,128)}, f32[512,512]{1,0:T(8,128)S(1)}, u32[]{:S(2)}, u32[]{:S(2)}) collective-permute-start(f32[512,512]{1,0:T(8,128)} %bitcast.46), channel_id=1, source_target_pairs={{1,0},{3,2},{5,4},{7,6},{9,8},{11,10},{13,12},{15,14},{17,16},{19,... | collective-permute-start | bytes 3145736 | tf_op jit(solution)/shard_map/ppermute | solution.py:109
  6.7 10.9 %copy-start.1 = (f32[1,1,512,512]{3,2,1,0:T(8,128)S(1)}, f32[1,1,512,512]{3,2,1,0:T(8,128)}, u32[]{:S(2)}) copy-start(f32[1,1,512,512]{3,2,1,0:T(8,128)} %param.7) | copy-start | bytes 3145732
  7.7 21.8 %all-to-all-start = ((f32[16,48,128]{2,1,0:T(8,128)}), f32[16,48,128]{2,1,0:T(8,128)}, u32[]{:S(2)}, u32[]{:S(2)}) async-start(f32[16,48,128]{2,1,0:T(8,128)} %pad_maximum_fusion), calls=%async_computation | async-start | bytes 786432 | tf_op jit(solution)/shard_map/all_to_all | solution.py:371
  14.9 20.3 %copy-start.18 = (f32[1,512]{1,0:T(1,128)S(1)}, f32[1,512]{1,0:T(1,128)}, u32[]{:S(2)}) copy-start(f32[1,512]{1,0:T(1,128)} %param.13) | copy-start | bytes 6148
  17.7 48.4 %copy-start.3 = (f32[512,512]{1,0:T(8,128)}, f32[512,512]{1,0:T(8,128)S(1)}, u32[]{:S(2)}) copy-start(f32[512,512]{1,0:T(8,128)S(1)} %collective-permute-done.other) | copy-start | bytes 3145732
  19.6 47.6 %copy-start.4 = (f32[512,512]{1,0:T(8,128)}, f32[512,512]{1,0:T(8,128)S(1)}, u32[]{:S(2)}) copy-start(f32[512,512]{1,0:T(8,128)S(1)} %fusion.2.two) | copy-start | bytes 3145732
  19.6 27.4 %collective-permute-start.1 = (f32[512,512]{1,0:T(8,128)S(1)}, f32[512,512]{1,0:T(8,128)}, u32[]{:S(2)}, u32[]{:S(2)}) collective-permute-start(f32[512,512]{1,0:T(8,128)S(1)} %fusion.2.two), channel_id=1, source_target_pairs={{6,4},{14,12},{22,20},{30,28},{35,37},{43,45},{51,53},{59,61},{70,... | collective-permute-start | bytes 3145736 | tf_op jit(solution)/shard_map/ppermute | solution.py:109
  31.8 11.8 %all-to-all-start.1 = ((f32[16,16,128]{2,1,0:T(8,128)}), f32[16,16,128]{2,1,0:T(8,128)S(1)}, u32[]{:S(2)}, u32[]{:S(2)}) async-start(f32[16,16,128]{2,1,0:T(8,128)} %landmark.1), calls=%async_computation.1 | async-start | bytes 262144 | tf_op jit(solution)/shard_map/all_to_all | solution.py:377
  43.7 25.9 %collective-permute-start.3 = (f32[512,512]{1,0:T(8,128)S(1)}, f32[512,512]{1,0:T(8,128)}, u32[]{:S(2)}, u32[]{:S(2)}) collective-permute-start(f32[512,512]{1,0:T(8,128)S(1)} %fusion.2.two), channel_id=1, source_target_pairs={{4,2},{12,10},{20,18},{28,26},{37,39},{45,47},{53,55},{61,63},{68,... | collective-permute-start | bytes 3145736 | tf_op jit(solution)/shard_map/ppermute | solution.py:109
  45.4 24.2 %collective-permute-start.4 = (f32[512,512]{1,0:T(8,128)S(1)}, f32[512,512]{1,0:T(8,128)}, u32[]{:S(2)}, u32[]{:S(2)}) collective-permute-start(f32[512,512]{1,0:T(8,128)S(1)} %fusion.2.two), channel_id=1, source_target_pairs={{0,2},{8,10},{16,18},{24,26},{33,39},{41,47},{49,55},{57,63},{64,6... | collective-permute-start | bytes 3145736 | tf_op jit(solution)/shard_map/ppermute | solution.py:109
  47.0 22.6 %collective-permute-start.2 = (f32[512,512]{1,0:T(8,128)}, f32[512,512]{1,0:T(8,128)}, u32[]{:S(2)}, u32[]{:S(2)}) collective-permute-start(f32[512,512]{1,0:T(8,128)} %collective-permute-done.1.far_pass), channel_id=1, source_target_pairs={{4,2},{12,10},{20,18},{28,26},{37,39},{45,47},{53,55},{61,63},{68,... | collective-permute-start | bytes 3145736 | tf_op jit(solution)/shard_map/ppermute | solution.py:109
  49.8 14.5 %collective-permute-start.6 = (f32[64,512]{1,0:T(8,128)S(1)}, f32[64,512]{1,0:T(8,128)S(1)}, u32[]{:S(2)}, u32[]{:S(2)}) collective-permute-start(f32[64,512]{1,0:T(8,128)S(1)} %convolution_add_fusion.3), channel_id=1, source_target_pairs={{1,0},{5,4},{7,6},{9,8},{13,12},{15,14},{17,16},{21,20},{23,22},{2... | collective-permute-start | bytes 393224 | tf_op jit(solution)/shard_map/ppermute | solution.py:109
  61.5 3.9 %collective-permute-start.5 = (f32[64,512]{1,0:T(8,128)S(1)}, f32[64,512]{1,0:T(8,128)S(1)}, u32[]{:S(2)}, u32[]{:S(2)}) collective-permute-start(f32[64,512]{1,0:T(8,128)S(1)} %convolution_add_fusion.3), channel_id=1, source_target_pairs={{3,2},{11,10},{19,18},{27,26},{38,39},{46,47},{54,55},{62,63},{67,... | collective-permute-start | bytes 393224 | tf_op jit(solution)/shard_map/ppermute | solution.py:109
  64.7 2.5 %collective-permute-start.7 = (f32[64,512]{1,0:T(8,128)S(1)}, f32[64,512]{1,0:T(8,128)S(1)}, u32[]{:S(2)}, u32[]{:S(2)}) collective-permute-start(f32[64,512]{1,0:T(8,128)S(1)} %convolution_add_fusion.1), channel_id=1, source_target_pairs={{6,2},{14,10},{22,18},{30,26},{35,39},{43,47},{51,55},{59,63},{70,... | collective-permute-start | bytes 393224 | tf_op jit(solution)/shard_map/ppermute | solution.py:109
  65.4 3.5 %collective-permute-start.8 = (f32[64,512]{1,0:T(8,128)S(1)}, f32[64,512]{1,0:T(8,128)S(1)}, u32[]{:S(2)}, u32[]{:S(2)}) collective-permute-start(f32[64,512]{1,0:T(8,128)S(1)} %convolution_add_fusion.1), channel_id=1, source_target_pairs={{4,2},{12,10},{20,18},{28,26},{37,39},{45,47},{53,55},{61,63},{68,... | collective-permute-start | bytes 393224 | tf_op jit(solution)/shard_map/ppermute | solution.py:109
  67.2 2.4 %copy-start.12 = (f32[64,512]{1,0:T(8,128)}, f32[64,512]{1,0:T(8,128)S(1)}, u32[]{:S(2)}) copy-start(f32[64,512]{1,0:T(8,128)S(1)} %collective-permute-done.7.off_last) | copy-start | bytes 393220
  67.2 25.4 %collective-permute-start.17 = (f32[512,512]{1,0:T(8,128)S(1)}, f32[512,512]{1,0:T(8,128)}, u32[]{:S(2)}, u32[]{:S(2)}) collective-permute-start(f32[512,512]{1,0:T(8,128)S(1)} %fusion.2.two), channel_id=1, source_target_pairs={{39,37},{47,45},{55,53},{63,61},{103,101},{111,109},{119,117},{127... | collective-permute-start | bytes 3145736 | tf_op jit(solution)/shard_map/ppermute | solution.py:109
  68.9 0.8 copy-start.14
  68.9 0.7 collective-permute-start.9
  69.6 0.7 copy-start.15
  75.0 9.6 %copy-start.11 = (f32[64,512]{1,0:T(8,128)S(1)}, f32[64,512]{1,0:T(8,128)}, u32[]{:S(2)}) copy-start(f32[64,512]{1,0:T(8,128)} %get-tuple-element.15.kept) | copy-start | bytes 393220
  82.0 6.6 %copy-start.19 = (f32[64,512]{1,0:T(8,128)S(1)}, f32[64,512]{1,0:T(8,128)}, u32[]{:S(2)}) copy-start(f32[64,512]{1,0:T(8,128)} %get-tuple-element.23) | copy-start | bytes 393220
  82.0 13.4 %collective-permute-start.16 = (f32[576,512]{1,0:T(8,128)}, f32[576,512]{1,0:T(8,128)S(1)}, u32[]{:S(2)}, u32[]{:S(2)}) collective-permute-start(f32[576,512]{1,0:T(8,128)} %get-tuple-element.21), channel_id=1, source_target_pairs={{2,0},{10,8},{18,16},{26,24},{39,33},{47,41},{55,49},{63,57},{66,6... | collective-permute-start | bytes 3538952 | tf_op jit(solution)/shard_map/ppermute | solution.py:109
  82.8 12.5 %collective-permute-start.18 = (f32[576,512]{1,0:T(8,128)}, f32[576,512]{1,0:T(8,128)}, u32[]{:S(2)}, u32[]{:S(2)}) collective-permute-start(f32[576,512]{1,0:T(8,128)} %get-tuple-element.22.own_map), channel_id=1, source_target_pairs={{39,35},{47,43},{55,51},{63,59},{103,99},{111,107},{119,115},{127,... | collective-permute-start | bytes 3538952 | tf_op jit(solution)/shard_map/ppermute | solution.py:109
  84.5 0.7 collective-permute-start.10
  85.2 0.7 copy-start.13
  87.9 1.4 collective-permute-start.11
  88.5 4.7 %collective-permute-start.19 = (f32[64,512]{1,0:T(8,128)S(1)}, f32[64,512]{1,0:T(8,128)S(1)}, u32[]{:S(2)}, u32[]{:S(2)}) collective-permute-start(f32[64,512]{1,0:T(8,128)S(1)} %copy-done.19), channel_id=1, source_target_pairs={{2,4},{10,12},{18,20},{26,28},{39,37},{47,45},{55,53},{63,61},{66,... | collective-permute-start | bytes 393224 | tf_op jit(solution)/shard_map/ppermute | solution.py:109
  89.2 0.7 copy-start.16
  91.8 2.1 %collective-permute-start.12 = (f32[64,512]{1,0:T(8,128)}, f32[64,512]{1,0:T(8,128)S(1)}, u32[]{:S(2)}, u32[]{:S(2)}) collective-permute-start(f32[64,512]{1,0:T(8,128)} %hop.3), channel_id=1, source_target_pairs={{10,6},{18,14},{26,22},{47,35},{55,43},{63,51},{74,70},{82,78},{90... | collective-permute-start | bytes 393224 | tf_op jit(solution)/shard_map/ppermute | solution.py:109
  92.6 2.8 %collective-permute-start.13 = (f32[64,512]{1,0:T(8,128)}, f32[64,512]{1,0:T(8,128)S(1)}, u32[]{:S(2)}, u32[]{:S(2)}) collective-permute-start(f32[64,512]{1,0:T(8,128)} %hop.3), channel_id=1, source_target_pairs={{10,0},{18,8},{26,16},{47,33},{55,41},{63,49},{74,64},{82,72},{90,... | collective-permute-start | bytes 393224 | tf_op jit(solution)/shard_map/ppermute | solution.py:109
  93.3 3.2 %copy-start.6 = (f32[64,512]{1,0:T(8,128)}, f32[64,512]{1,0:T(8,128)S(1)}, u32[]{:S(2)}) copy-start(f32[64,512]{1,0:T(8,128)S(1)} %collective-permute-done.19.far_shift) | copy-start | bytes 393220
  93.3 2.1 %collective-permute-start.14 = (f32[64,512]{1,0:T(8,128)}, f32[64,512]{1,0:T(8,128)S(1)}, u32[]{:S(2)}, u32[]{:S(2)}) collective-permute-start(f32[64,512]{1,0:T(8,128)} %hop.3), channel_id=1, source_target_pairs={{10,4},{18,12},{26,20},{47,37},{55,45},{63,53},{74,68},{82,76},{90... | collective-permute-start | bytes 393224 | tf_op jit(solution)/shard_map/ppermute | solution.py:109
  93.9 2.5 %copy-start.7 = (f32[64,512]{1,0:T(8,128)}, f32[64,512]{1,0:T(8,128)S(1)}, u32[]{:S(2)}) copy-start(f32[64,512]{1,0:T(8,128)S(1)} %collective-permute-done.12.got0) | copy-start | bytes 393220
  94.0 1.4 collective-permute-start.15
  95.3 1.1 copy-start.8
  95.3 1.1 copy-start.9
  95.3 1.1 copy-start.10
  95.4 1.1 copy-start.5
  96.5 51.0 %copy-start.2 = (f32[1,1,512,512]{3,2,1,0:T(8,128)S(1)}, f32[1,1,512,512]{3,2,1,0:T(8,128)}, u32[]{:S(2)}) copy-start(f32[1,1,512,512]{3,2,1,0:T(8,128)} %param.7) | copy-start | bytes 3145732
  100.5 46.9 %collective-permute-start.20 = (f32[64,512]{1,0:T(8,128)}, f32[64,512]{1,0:T(8,128)S(1)}, u32[]{:S(2)}, u32[]{:S(2)}) collective-permute-start(f32[64,512]{1,0:T(8,128)} %get-tuple-element.25), channel_id=1, source_target_pairs={{0,1},{2,3},{4,5},{6,7},{8,9},{10,11},{12,13},{14,15},{16,17},{18,... | collective-permute-start | bytes 393224 | tf_op jit(solution)/shard_map/ppermute | solution.py:109

commit v6 on v3

--- a/solution.py
+++ b/solution.py
@@ -133,27 +133,47 @@
     return lambda src, dst, k: pltpu.make_async_copy(src, dst, sems.at[k])
 
 
-def compose_kernel(flag, two, last, far, near, enter1, enter0, eight, m3, m2, m1, m0, r1, r0, r8, sems, out_sems):
+HALF = TEAM_STATES // 2
+
+
+def half_loads(load, parts, dst, k):
+    tops = [load(part, dst.at[pl.ds(i * HALF, HALF)], k + i) for i, part in enumerate(parts)]
+    return tops
+
+
+def run(copies, wait=False):
+    for copy in copies:
+        if wait:
+            copy.wait()
+        else:
+            copy.start()
+
+
+def compose_kernel(
+    flag, two, last_a, last_b, far, near, enter1, enter0, eight, m3, m2, m1, m0, r1, r0, r8, sems, out_sems
+):
     load, store = copier(sems), copier(out_sems)
     even = flag[0] == 1
+    last = (last_a, last_b)
+    own = (two.at[pl.ds(0, HALF)], two.at[pl.ds(HALF, HALF)])
 
     @pl.when(even)
     def _():
-        load(last, m3, 0).start()
-        load(two, m1, 2).start()
+        run(half_loads(load, last, m3, 0))
+        run(half_loads(load, own, m1, 4))
 
     @pl.when(jnp.logical_not(even))
     def _():
-        load(two, m3, 0).start()
-        load(last, m1, 2).start()
-
-    load(far, m2, 1).start()
+        run(half_loads(load, own, m3, 0))
+        run(half_loads(load, last, m1, 4))
+
+    load(far, m2, 2).start()
     load(near, m0, 3).start()
-    load(last, m3, 0).wait()
-    load(far, m2, 1).wait()
+    run(half_loads(load, last, m3, 0), True)
+    load(far, m2, 2).wait()
     r1[...] = product(split(m3[...]), split(m2[...]))
     store(r1, enter1, 0).start()
-    load(last, m1, 2).wait()
+    run(half_loads(load, last, m1, 4), True)
     r0[...] = product(split(r1[...]), split(m1[...]))
     store(r0, enter0, 1).start()
     load(near, m0, 3).wait()
@@ -172,29 +192,32 @@
     return pl.pallas_call(
         compose_kernel,
         out_shape=[jax.ShapeDtypeStruct(SQUARE, jnp.float32)] * 3,
-        in_specs=[pl.BlockSpec(memory_space=pltpu.SMEM)] + [pl.BlockSpec(memory_space=pl.ANY)] * 4,
+        in_specs=[pl.BlockSpec(memory_space=pltpu.SMEM)] + [pl.BlockSpec(memory_space=pl.ANY)] * 5,
         out_specs=[pl.BlockSpec(memory_space=pl.ANY)] * 3,
         scratch_shapes=[pltpu.VMEM(SQUARE, jnp.float32)] * 7
-        + [pltpu.SemaphoreType.DMA((4,)), pltpu.SemaphoreType.DMA((3,))],
+        + [pltpu.SemaphoreType.DMA((6,)), pltpu.SemaphoreType.DMA((3,))],
         name="compose",
-    )(flag, two, last, far, near)
+    )(flag, two, *last, far, near)
 
 
 def shift_kernel(
-    flag, two, last, far, near, eight, off_own, off_last, off_far, off_near, start,
+    flag, two, last_a, last_b, far, near, eight, off_own, off_last, off_far, off_near, start,
     shift2, shift1, shift0, total, leaving, m2, m1, m0, m8, sems,
 ):
     load = copier(sems)
     even = flag[0] == 1
     load(far, m2, 0).start()
 
+    last = (last_a, last_b)
+    own = (two.at[pl.ds(0, HALF)], two.at[pl.ds(HALF, HALF)])
+
     @pl.when(even)
     def _():
-        load(two, m1, 1).start()
+        run(half_loads(load, own, m1, 4))
 
     @pl.when(jnp.logical_not(even))
     def _():
-        load(last, m1, 1).start()
+        run(half_loads(load, last, m1, 4))
 
     load(near, m0, 2).start()
     load(eight, m8, 3).start()
@@ -204,7 +227,7 @@
     load(far, m2, 0).wait()
     moved = product(split(moved), split(m2[...])) + off_far[...]
     shift1[...] = moved
-    load(last, m1, 1).wait()
+    run(half_loads(load, last, m1, 4), True)
     moved = product(split(moved), split(m1[...])) + off1
     shift0[...] = moved
     load(near, m0, 2).wait()
@@ -219,10 +242,10 @@
         shift_kernel,
         out_shape=[jax.ShapeDtypeStruct(ROWS, jnp.float32)] * 5,
         in_specs=[pl.BlockSpec(memory_space=pltpu.SMEM)]
-        + [pl.BlockSpec(memory_space=pl.ANY)] * 5
+        + [pl.BlockSpec(memory_space=pl.ANY)] * 6
         + [pl.BlockSpec(memory_space=pltpu.VMEM)] * 5,
         out_specs=[pl.BlockSpec(memory_space=pltpu.VMEM)] * 5,
-        scratch_shapes=[pltpu.VMEM(SQUARE, jnp.float32)] * 4 + [pltpu.SemaphoreType.DMA((4,))],
+        scratch_shapes=[pltpu.VMEM(SQUARE, jnp.float32)] * 4 + [pltpu.SemaphoreType.DMA((6,))],
         name="shift",
     )(flag, *maps, *rows)
 
@@ -293,10 +316,10 @@
     high = pick(other_matrix, matrix)
     low = pick(matrix, other_matrix)
     two = jnp.dot(high, low, precision=lax.Precision.HIGHEST)
-    passing = send(two, LAST_STEP)
+    passing = [send(two[:HALF], LAST_STEP), send(two[HALF:], LAST_STEP)]
     two_far = send(two, FAR_IN)
     two_near = send(two, NEAR_IN)
-    two_last = send(passing, FAR_IN)
+    two_last = [send(passing[0], FAR_IN), send(passing[1], FAR_IN)]
 
     owner = jnp.arange(TEAM_STATES)[None, :] // STATES == jnp.arange(ROBOTS)[:, None]
     spread = lax.optimization_barrier(jnp.where(owner, obs_gain[0][None, :], 0.0))
@@ -318,7 +341,7 @@
     enter1, enter0, eight = compose(flag, two, two_last, two_far, two_near)
     off3, shift1, shift0, total, leaving = shift(
         flag,
-        (two, two_last, two_far, two_near, eight),
+        (two, *two_last, two_far, two_near, eight),
         (own_offset, off_last, off_far, off_near, terminal[0]),
     )
 
@@ -342,7 +365,7 @@
         send(out, down(own_pair)),
     ]
     pair = (step % RING) // 2
-    enter_map = jnp.where(pair == NEAR, map_near, jnp.where(pair == FAR, pick(passing, map_far), pick(enter1, map_last)))
+    enter_map = jnp.where(pair == NEAR, map_near, jnp.where(pair == FAR, pick(jnp.concatenate(passing, axis=0), map_far), pick(enter1, map_last)))
     enter_shift = jnp.where(pair == NEAR, shift_near, jnp.where(pair == FAR, shift_far, pick(shift1, shift_last)))
     enter_map, enter_shift = lax.optimization_barrier((enter_map, enter_shift))
     entry = (arrived[0] + arrived[1]) + (arrived[2] + arrived[3]) + jnp.where(ring == last_ring, terminal[0], 0.0)

time: 148 us -> 159 us (1.074)
  waiting for transfers between devices: 56.3 us -> 64.6 us
  local copies, waits for them, and re-layouts: 1.9 us -> 3.89 us
    ppermute x23 -> x25, waiting for transfers between devices: 39.8 us -> 44.9 us  [send(): return lax.ppermute(value, BOTH, pairs)]
    all_to_all x1, waiting for transfers between devices: 8.89 us -> 12 us  [shards(): lax.all_to_all(jnp.concatenate([slices, packed], axis=1), 'team', 0, 0, t...]
    all_to_all x1, starting transfers between devices: 7.23 us -> 10.2 us  [shards(): lax.all_to_all(jnp.concatenate([slices, packed], axis=1), 'team', 0, 0, t...]
    ppermute x23 -> x25, starting transfers between devices: 44.8 us -> 42.6 us  [send(): return lax.ppermute(value, BOTH, pairs)]
  transfers between devices with their start and end apart: 25 -> 27, of which waited for: 5 -> 4; matrix products, arithmetic and copies ran while one was open for 7% -> 3% of each run, Pallas kernels for 11% -> 11%
where the time goes in v6:
time: 159 us; the launch traced here: 158 us
  waiting for transfers between devices  64.6 us (41%)
  starting transfers between devices  56.2 us (35%)
  Pallas kernels  16.8 us (11%)
  matrix products  7.75 us (5%)
  other arithmetic  7.46 us (5%)
  local copies, waits for them, and re-layouts  3.89 us (2%)
    ppermute x25, waiting for transfers between devices, send(): return lax.ppermute(value, BOTH, pairs)  44.9 us
    ppermute x25, starting transfers between devices, send(): return lax.ppermute(value, BOTH, pairs)  42.6 us
    all_to_all x1, waiting for transfers between devices, shards(): lax.all_to_all(jnp.concatenate([slices, packed], axis=1), 'team', 0, 0, t...  12 us
    all_to_all x1, starting transfers between devices, shards(): lax.all_to_all(jnp.concatenate([slices, packed], axis=1), 'team', 0, 0, t...  10.2 us
    all_to_all x1, waiting for transfers between devices, shards(): parts = lax.all_to_all(part, 'team', 0, 0, tiled=True)  7.66 us
    pallas_call x1, Pallas kernels, compose(): pl.pallas_call(compose_kernel, out_shape=[jax.ShapeDtypeStruct(SQUARE, jn...  5.9 us
    pallas_call x1, Pallas kernels, shift(): pl.pallas_call(shift_kernel, out_shape=[jax.ShapeDtypeStruct(ROWS, jnp.fl...  4.72 us
    dot_general x5, matrix products, matmul(): return jnp.dot(left, right, precision=HIGH)  4.18 us
  transfers between devices with their start and end apart: 27, of which 4 were waited for; matrix products, arithmetic and copies ran while one was open for 3% of the time, Pallas kernels for 11%

profile of v6, /device:TPU:1, one launch (start us, length us, event | category | flops | bytes accessed | tf_op | source)
XLA Modules:
  0.0 157.7 jit_solution(16757030846076189028)
XLA Ops:
  0.6 0.8 fusion.19
  1.4 1.0 convert_bitcast_fusion
  2.6 0.8 pad_maximum_fusion
  3.4 10.2 %all-to-all-start = ((f32[16,48,128]{2,1,0:T(8,128)}), f32[16,48,128]{2,1,0:T(8,128)S(1)}, u32[]{:S(2)}, u32[]{:S(2)}) async-start(f32[16,48,128]{2,1,0:T(8,128)} %pad_maximum_fusion), calls=%async_computation | async-start | bytes 786432 | tf_op jit(solution)/shard_map/all_to_all | solution.py:307
  13.6 2.5 %collective-permute-start = (f32[512,512]{1,0:T(8,128)S(1)}, f32[512,512]{1,0:T(8,128)S(1)}, u32[]{:S(2)}, u32[]{:S(2)}) collective-permute-start(f32[512,512]{1,0:T(8,128)S(1)} %bitcast.49), channel_id=1, source_target_pairs={{1,0},{3,2},{5,4},{7,6},{9,8},{11,10},{13,12},{15,14},{17,16},{19,... | collective-permute-start | bytes 3145736 | tf_op jit(solution)/shard_map/ppermute | solution.py:109
  16.1 12.0 %all-to-all-done.got = f32[16,48,128]{2,1,0:T(8,128)S(1)} async-done(((f32[16,48,128]{2,1,0:T(8,128)}), f32[16,48,128]{2,1,0:T(8,128)S(1)}, u32[]{:S(2)}, u32[]{:S(2)}) %all-to-all-start) | async-done | bytes 393248 | tf_op jit(solution)/shard_map/all_to_all | solution.py:307
  28.1 0.7 copy-done.5
  28.8 2.2 %landmark.1 = f32[16,16,128]{2,1,0:T(8,128)} custom-call(f32[16,48,128]{2,1,0:T(8,128)} %copy-done.5), custom_call_target="tpu_custom_call" | custom-call | tf_op jit(solution)/shard_map/landmark/pallas_call | solution.py:308
  31.1 3.4 %all-to-all-start.1 = ((f32[16,16,128]{2,1,0:T(8,128)}), f32[16,16,128]{2,1,0:T(8,128)S(1)}, u32[]{:S(2)}, u32[]{:S(2)}) async-start(f32[16,16,128]{2,1,0:T(8,128)} %landmark.1), calls=%async_computation.1 | async-start | bytes 262144 | tf_op jit(solution)/shard_map/all_to_all | solution.py:313
  34.5 0.7 copy-done.10
  35.2 7.7 %all-to-all-done.1 = f32[16,16,128]{2,1,0:T(8,128)S(1)} async-done(((f32[16,16,128]{2,1,0:T(8,128)}), f32[16,16,128]{2,1,0:T(8,128)S(1)}, u32[]{:S(2)}, u32[]{:S(2)}) %all-to-all-start.1) | async-done | bytes 131104 | tf_op jit(solution)/shard_map/all_to_all | solution.py:313
  42.9 1.9 %fusion.5.two = f32[512,512]{1,0:T(8,128)S(1)} fusion(f32[512,512]{1,0:T(8,128)S(1)} %collective-permute-done, pred[]{:T(512)S(6)} %eq.48, f32[1,1,512,512]{3,2,1,0:T(8,128)S(1)} %copy-done.1), kind=kOutput, calls=%fused_computation.15 | convolution fusion | flops 1611137024 | bytes 3145729 | tf_op jit(solution)/shard_map/dot_general | solution.py:318
  44.8 1.0 fusion.18
  45.9 1.7 %collective-permute-start.5 = (f32[512,512]{1,0:T(8,128)S(1)}, f32[512,512]{1,0:T(8,128)}, u32[]{:S(2)}, u32[]{:S(2)}) collective-permute-start(f32[512,512]{1,0:T(8,128)S(1)} %fusion.5.two), channel_id=1, source_target_pairs={{4,2},{12,10},{20,18},{28,26},{37,39},{45,47},{53,55},{61,63},{68,... | collective-permute-start | bytes 3145736 | tf_op jit(solution)/shard_map/ppermute | solution.py:109
  47.6 1.6 %collective-permute-start.6 = (f32[512,512]{1,0:T(8,128)S(1)}, f32[512,512]{1,0:T(8,128)}, u32[]{:S(2)}, u32[]{:S(2)}) collective-permute-start(f32[512,512]{1,0:T(8,128)S(1)} %fusion.5.two), channel_id=1, source_target_pairs={{0,2},{8,10},{16,18},{24,26},{33,39},{41,47},{49,55},{57,63},{64,6... | collective-permute-start | bytes 3145736 | tf_op jit(solution)/shard_map/ppermute | solution.py:109
  49.2 1.5 collective-permute-start.1
  50.7 1.5 collective-permute-start.3
  52.5 11.1 %collective-permute-start.8 = (f32[64,512]{1,0:T(8,128)S(1)}, f32[64,512]{1,0:T(8,128)S(1)}, u32[]{:S(2)}, u32[]{:S(2)}) collective-permute-start(f32[64,512]{1,0:T(8,128)S(1)} %convolution_add_fusion.5), channel_id=1, source_target_pairs={{1,0},{5,4},{7,6},{9,8},{13,12},{15,14},{17,16},{21,20},{23,22},{2... | collective-permute-start | bytes 393224 | tf_op jit(solution)/shard_map/ppermute | solution.py:109
  63.5 1.9 %collective-permute-done.8 = f32[64,512]{1,0:T(8,128)S(1)} collective-permute-done((f32[64,512]{1,0:T(8,128)S(1)}, f32[64,512]{1,0:T(8,128)S(1)}, u32[]{:S(2)}, u32[]{:S(2)}) %collective-permute-start.8) | collective-permute-done | bytes 131104 | tf_op jit(solution)/shard_map/ppermute | solution.py:109
  66.1 0.7 collective-permute-start.2
  66.9 0.7 collective-permute-start.4
  67.6 1.1 convolution_add_fusion.3
  68.7 1.3 collective-permute-start.10
  70.0 1.1 convolution_add_fusion.4.off_own
  71.1 1.7 %collective-permute-start.19 = (f32[512,512]{1,0:T(8,128)S(1)}, f32[512,512]{1,0:T(8,128)}, u32[]{:S(2)}, u32[]{:S(2)}) collective-permute-start(f32[512,512]{1,0:T(8,128)S(1)} %fusion.5.two), channel_id=1, source_target_pairs={{39,37},{47,45},{55,53},{63,61},{103,101},{111,109},{119,117},{127... | collective-permute-start | bytes 3145736 | tf_op jit(solution)/shard_map/ppermute | solution.py:109
  72.8 1.3 collective-permute-start.11
  74.1 1.3 collective-permute-start.9
  75.4 5.9 %compose.1 = (f32[512,512]{1,0:T(8,128)}, f32[512,512]{1,0:T(8,128)}, f32[512,512]{1,0:T(8,128)}) custom-call(s32[1]{0:T(128)} %bitcast.2.flag, f32[512,512]{1,0:T(8,128)} %copy-done.2, f32[256,512]{1,0:T(8,128)} %copy-done.3, f32[256,512]{1,0:T(8,128)} %copy-done.4, f32[512,512]{1,0:T(8,128)} %collective-permute-done.5.far, ...), custom_call_target="tpu_custom_call" | custom-call | tf_op jit(solution)/shard_map/compose/pallas_call | solution.py:192
  81.3 1.6 %collective-permute-start.18 = (f32[512,512]{1,0:T(8,128)}, f32[512,512]{1,0:T(8,128)}, u32[]{:S(2)}, u32[]{:S(2)}) collective-permute-start(f32[512,512]{1,0:T(8,128)} %get-tuple-element.18), channel_id=1, source_target_pairs={{2,0},{10,8},{18,16},{26,24},{39,33},{47,41},{55,49},{63,57},{66,6... | collective-permute-start | bytes 3145736 | tf_op jit(solution)/shard_map/ppermute | solution.py:109
  82.9 1.7 %collective-permute-start.20 = (f32[512,512]{1,0:T(8,128)}, f32[512,512]{1,0:T(8,128)}, u32[]{:S(2)}, u32[]{:S(2)}) collective-permute-start(f32[512,512]{1,0:T(8,128)} %get-tuple-element.19), channel_id=1, source_target_pairs={{39,35},{47,43},{55,51},{63,59},{103,99},{111,107},{119,115},{127,... | collective-permute-start | bytes 3145736 | tf_op jit(solution)/shard_map/ppermute | solution.py:109
  85.3 4.7 %shift.1 = (f32[64,512]{1,0:T(8,128)}, f32[64,512]{1,0:T(8,128)}, f32[64,512]{1,0:T(8,128)}, f32[64,512]{1,0:T(8,128)}, f32[64,512]{1,0:T(8,128)}) custom-call(s32[1]{0:T(128)} %bitcast.2.flag, f32[512,512]{1,0:T(8,128)} %copy-done.2, f32[256,512]{1,0:T(8,128)} %copy-done.3, f32[256,512]{1,0:T(8,128)} %copy-done.4, f32[512,512]{1,0:T(8,128)} %collective-permute-done.5.far, ...), custom_call_target="tpu_custom_call" | custom-call | tf_op jit(solution)/shard_map/shift/pallas_call | solution.py:241
  90.0 1.3 collective-permute-start.12
  91.3 1.3 collective-permute-start.21
  92.6 2.0 %hop.2.kept = f32[64,512]{1,0:T(8,128)} custom-call(s32[1]{0:T(128)} %bitcast.1.flag, f32[64,512]{1,0:T(8,128)} %collective-permute-done.12.arrived, f32[512,512]{1,0:T(8,128)} %get-tuple-element.14.eight, f32[64,512]{1,0:T(8,128)} %get-tuple-element.17.total, f32[64,512]{1,0:T(8,128)} %get-tuple-element.16.kept), custom_call_target="tpu_custom_call" | custom-call | tf_op jit(solution)/shard_map/hop/pallas_call | solution.py:264
  94.6 1.3 collective-permute-start.13
  95.9 1.3 collective-permute-start.22
  97.2 1.3 collective-permute-start.23
  98.5 2.0 %hop.3 = f32[64,512]{1,0:T(8,128)} custom-call(s32[1]{0:T(128)} %bitcast.flag, f32[64,512]{1,0:T(8,128)} %collective-permute-done.13.arrived, f32[512,512]{1,0:T(8,128)} %get-tuple-element.14.eight, f32[64,512]{1,0:T(8,128)} %get-tuple-element.17.total, f32[64,512]{1,0:T(8,128)} %hop.2.kept), custom_call_target="tpu_custom_call" | custom-call | tf_op jit(solution)/shard_map/hop/pallas_call | solution.py:264
  100.5 1.3 collective-permute-start.14
  101.8 1.3 collective-permute-start.15
  103.1 0.8 collective-permute-start.16
  104.6 1.0 select_select_fusion.1
  105.6 1.1 select_add_fusion
  106.7 2.8 %fusion.4 = f32[512,512]{1,0:T(8,128)S(1)} fusion(f32[512,512]{1,0:T(8,128)} %collective-permute-done.18, f32[512,512]{1,0:T(8,128)} %collective-permute-done.19, f32[256,512]{1,0:T(8,128)} %collective-permute-done.3, f32[256,512]{1,0:T(8,128)} %collective-permute-done.1, f32[512,512]{1,0:T(8,128)S(1)} %copy-done.6, f32[512,512]{1,0:T(8,128)} %collective-permute-done.20, ...), kind=kLoop, calls=%fused_computation.12 | loop fusion | flops 1310720 | bytes 6291459 | tf_op jit(solution)/shard_map/jit(_where)/select_n | solution.py:368
  110.9 1.3 collective-permute-start.24
  112.2 42.9 %collective-permute-done.24 = f32[64,512]{1,0:T(8,128)S(1)} collective-permute-done((f32[64,512]{1,0:T(8,128)S(1)}, f32[64,512]{1,0:T(8,128)S(1)}, u32[]{:S(2)}, u32[]{:S(2)}) %collective-permute-start.24) | collective-permute-done | bytes 131104 | tf_op jit(solution)/shard_map/ppermute | solution.py:109
  155.2 1.1 fusion.1
  156.3 1.4 fusion
  (58 shorter events, 4.0 us)
Async XLA Ops:
  0.6 155.7 %copy-start = (f32[1,1,64,512]{3,2,1,0:T(8,128)S(1)}, f32[1,1,64,512]{3,2,1,0:T(8,128)}, u32[]{:S(2)}) copy-start(f32[1,1,64,512]{3,2,1,0:T(8,128)} %param.8) | copy-start | bytes 393220
  2.4 11.2 %copy-start.1 = (f32[1,1,512,512]{3,2,1,0:T(8,128)S(1)}, f32[1,1,512,512]{3,2,1,0:T(8,128)}, u32[]{:S(2)}) copy-start(f32[1,1,512,512]{3,2,1,0:T(8,128)} %param.7) | copy-start | bytes 3145732
  3.4 24.7 %all-to-all-start = ((f32[16,48,128]{2,1,0:T(8,128)}), f32[16,48,128]{2,1,0:T(8,128)S(1)}, u32[]{:S(2)}, u32[]{:S(2)}) async-start(f32[16,48,128]{2,1,0:T(8,128)} %pad_maximum_fusion), calls=%async_computation | async-start | bytes 786432 | tf_op jit(solution)/shard_map/all_to_all | solution.py:307
  13.6 29.3 %collective-permute-start = (f32[512,512]{1,0:T(8,128)S(1)}, f32[512,512]{1,0:T(8,128)S(1)}, u32[]{:S(2)}, u32[]{:S(2)}) collective-permute-start(f32[512,512]{1,0:T(8,128)S(1)} %bitcast.49), channel_id=1, source_target_pairs={{1,0},{3,2},{5,4},{7,6},{9,8},{11,10},{13,12},{15,14},{17,16},{19,... | collective-permute-start | bytes 3145736 | tf_op jit(solution)/shard_map/ppermute | solution.py:109
  28.1 0.7 copy-start.5
  31.1 11.8 %all-to-all-start.1 = ((f32[16,16,128]{2,1,0:T(8,128)}), f32[16,16,128]{2,1,0:T(8,128)S(1)}, u32[]{:S(2)}, u32[]{:S(2)}) async-start(f32[16,16,128]{2,1,0:T(8,128)} %landmark.1), calls=%async_computation.1 | async-start | bytes 262144 | tf_op jit(solution)/shard_map/all_to_all | solution.py:313
  34.5 0.7 copy-start.10
  44.8 26.2 %copy-start.2 = (f32[512,512]{1,0:T(8,128)}, f32[512,512]{1,0:T(8,128)S(1)}, u32[]{:S(2)}) copy-start(f32[512,512]{1,0:T(8,128)S(1)} %fusion.5.two) | copy-start | bytes 3145732
  44.8 7.4 %copy-start.9 = (f32[1,1,64,512]{3,2,1,0:T(8,128)S(1)}, f32[1,1,64,512]{3,2,1,0:T(8,128)}, u32[]{:S(2)}) copy-start(f32[1,1,64,512]{3,2,1,0:T(8,128)} %param.9) | copy-start | bytes 393220
  45.9 28.2 %collective-permute-start.5 = (f32[512,512]{1,0:T(8,128)S(1)}, f32[512,512]{1,0:T(8,128)}, u32[]{:S(2)}, u32[]{:S(2)}) collective-permute-start(f32[512,512]{1,0:T(8,128)S(1)} %fusion.5.two), channel_id=1, source_target_pairs={{4,2},{12,10},{20,18},{28,26},{37,39},{45,47},{53,55},{61,63},{68,... | collective-permute-start | bytes 3145736 | tf_op jit(solution)/shard_map/ppermute | solution.py:109
  47.6 27.8 %collective-permute-start.6 = (f32[512,512]{1,0:T(8,128)S(1)}, f32[512,512]{1,0:T(8,128)}, u32[]{:S(2)}, u32[]{:S(2)}) collective-permute-start(f32[512,512]{1,0:T(8,128)S(1)} %fusion.5.two), channel_id=1, source_target_pairs={{0,2},{8,10},{16,18},{24,26},{33,39},{41,47},{49,55},{57,63},{64,6... | collective-permute-start | bytes 3145736 | tf_op jit(solution)/shard_map/ppermute | solution.py:109
  49.2 16.9 %collective-permute-start.1 = (f32[256,512]{1,0:T(8,128)}, f32[256,512]{1,0:T(8,128)}, u32[]{:S(2)}, u32[]{:S(2)}) collective-permute-start(f32[256,512]{1,0:T(8,128)} %get-tuple-element.27), channel_id=1, source_target_pairs={{6,4},{14,12},{22,20},{30,28},{35,37},{43,45},{51,53},{59,61},{70,... | collective-permute-start | bytes 1572872 | tf_op jit(solution)/shard_map/ppermute | solution.py:109
  50.7 16.2 %collective-permute-start.3 = (f32[256,512]{1,0:T(8,128)}, f32[256,512]{1,0:T(8,128)}, u32[]{:S(2)}, u32[]{:S(2)}) collective-permute-start(f32[256,512]{1,0:T(8,128)} %get-tuple-element.26), channel_id=1, source_target_pairs={{6,4},{14,12},{22,20},{30,28},{35,37},{43,45},{51,53},{59,61},{70,... | collective-permute-start | bytes 1572872 | tf_op jit(solution)/shard_map/ppermute | solution.py:109
  52.5 13.0 %collective-permute-start.8 = (f32[64,512]{1,0:T(8,128)S(1)}, f32[64,512]{1,0:T(8,128)S(1)}, u32[]{:S(2)}, u32[]{:S(2)}) collective-permute-start(f32[64,512]{1,0:T(8,128)S(1)} %convolution_add_fusion.5), channel_id=1, source_target_pairs={{1,0},{5,4},{7,6},{9,8},{13,12},{15,14},{17,16},{21,20},{23,22},{2... | collective-permute-start | bytes 393224 | tf_op jit(solution)/shard_map/ppermute | solution.py:109
  65.5 3.2 %collective-permute-start.7 = (f32[64,512]{1,0:T(8,128)S(1)}, f32[64,512]{1,0:T(8,128)S(1)}, u32[]{:S(2)}, u32[]{:S(2)}) collective-permute-start(f32[64,512]{1,0:T(8,128)S(1)} %convolution_add_fusion.5), channel_id=1, source_target_pairs={{3,2},{11,10},{19,18},{27,26},{38,39},{46,47},{54,55},{62,63},{67,... | collective-permute-start | bytes 393224 | tf_op jit(solution)/shard_map/ppermute | solution.py:109
  66.1 4.9 %collective-permute-start.2 = (f32[256,512]{1,0:T(8,128)}, f32[256,512]{1,0:T(8,128)S(1)}, u32[]{:S(2)}, u32[]{:S(2)}) collective-permute-start(f32[256,512]{1,0:T(8,128)} %collective-permute-done.1), channel_id=1, source_target_pairs={{4,2},{12,10},{20,18},{28,26},{37,39},{45,47},{53,55},{61,63},{68,... | collective-permute-start | bytes 1572872 | tf_op jit(solution)/shard_map/ppermute | solution.py:109
  66.9 5.9 %collective-permute-start.4 = (f32[256,512]{1,0:T(8,128)}, f32[256,512]{1,0:T(8,128)S(1)}, u32[]{:S(2)}, u32[]{:S(2)}) collective-permute-start(f32[256,512]{1,0:T(8,128)} %collective-permute-done.3), channel_id=1, source_target_pairs={{4,2},{12,10},{20,18},{28,26},{37,39},{45,47},{53,55},{61,63},{68,... | collective-permute-start | bytes 1572872 | tf_op jit(solution)/shard_map/ppermute | solution.py:109
  68.7 2.4 %copy-start.8 = (f32[64,512]{1,0:T(8,128)}, f32[64,512]{1,0:T(8,128)S(1)}, u32[]{:S(2)}) copy-start(f32[64,512]{1,0:T(8,128)S(1)} %collective-permute-done.7) | copy-start | bytes 393220
  68.7 14.3 %collective-permute-start.10 = (f32[64,512]{1,0:T(8,128)}, f32[64,512]{1,0:T(8,128)}, u32[]{:S(2)}, u32[]{:S(2)}) collective-permute-start(f32[64,512]{1,0:T(8,128)} %convolution_add_fusion.3), channel_id=1, source_target_pairs={{4,2},{12,10},{20,18},{28,26},{37,39},{45,47},{53,55},{61,63},{68,... | collective-permute-start | bytes 393224 | tf_op jit(solution)/shard_map/ppermute | solution.py:109
  71.1 4.3 %copy-start.3 = (f32[256,512]{1,0:T(8,128)}, f32[256,512]{1,0:T(8,128)S(1)}, u32[]{:S(2)}) copy-start(f32[256,512]{1,0:T(8,128)S(1)} %collective-permute-done.2.last_a) | copy-start | bytes 1572868
  71.1 35.6 %collective-permute-start.19 = (f32[512,512]{1,0:T(8,128)S(1)}, f32[512,512]{1,0:T(8,128)}, u32[]{:S(2)}, u32[]{:S(2)}) collective-permute-start(f32[512,512]{1,0:T(8,128)S(1)} %fusion.5.two), channel_id=1, source_target_pairs={{39,37},{47,45},{55,53},{63,61},{103,101},{111,109},{119,117},{127... | collective-permute-start | bytes 3145736 | tf_op jit(solution)/shard_map/ppermute | solution.py:109
  72.7 2.6 %copy-start.4 = (f32[256,512]{1,0:T(8,128)}, f32[256,512]{1,0:T(8,128)S(1)}, u32[]{:S(2)}) copy-start(f32[256,512]{1,0:T(8,128)S(1)} %collective-permute-done.4.last_b) | copy-start | bytes 1572868
  72.8 12.5 %collective-permute-start.11 = (f32[64,512]{1,0:T(8,128)}, f32[64,512]{1,0:T(8,128)}, u32[]{:S(2)}, u32[]{:S(2)}) collective-permute-start(f32[64,512]{1,0:T(8,128)} %convolution_add_fusion.3), channel_id=1, source_target_pairs={{0,2},{8,10},{16,18},{24,26},{33,39},{41,47},{49,55},{57,63},{64,6... | collective-permute-start | bytes 393224 | tf_op jit(solution)/shard_map/ppermute | solution.py:109
  74.1 11.2 %collective-permute-start.9 = (f32[64,512]{1,0:T(8,128)}, f32[64,512]{1,0:T(8,128)}, u32[]{:S(2)}, u32[]{:S(2)}) collective-permute-start(f32[64,512]{1,0:T(8,128)} %convolution_add_fusion.3), channel_id=1, source_target_pairs={{6,2},{14,10},{22,18},{30,26},{35,39},{43,47},{51,55},{59,63},{70,... | collective-permute-start | bytes 393224 | tf_op jit(solution)/shard_map/ppermute | solution.py:109
  81.3 25.4 %collective-permute-start.18 = (f32[512,512]{1,0:T(8,128)}, f32[512,512]{1,0:T(8,128)}, u32[]{:S(2)}, u32[]{:S(2)}) collective-permute-start(f32[512,512]{1,0:T(8,128)} %get-tuple-element.18), channel_id=1, source_target_pairs={{2,0},{10,8},{18,16},{26,24},{39,33},{47,41},{55,49},{63,57},{66,6... | collective-permute-start | bytes 3145736 | tf_op jit(solution)/shard_map/ppermute | solution.py:109
  82.9 23.8 %collective-permute-start.20 = (f32[512,512]{1,0:T(8,128)}, f32[512,512]{1,0:T(8,128)}, u32[]{:S(2)}, u32[]{:S(2)}) collective-permute-start(f32[512,512]{1,0:T(8,128)} %get-tuple-element.19), channel_id=1, source_target_pairs={{39,35},{47,43},{55,51},{63,59},{103,99},{111,107},{119,115},{127,... | collective-permute-start | bytes 3145736 | tf_op jit(solution)/shard_map/ppermute | solution.py:109
  90.0 2.6 %collective-permute-start.12 = (f32[64,512]{1,0:T(8,128)}, f32[64,512]{1,0:T(8,128)}, u32[]{:S(2)}, u32[]{:S(2)}) collective-permute-start(f32[64,512]{1,0:T(8,128)} %get-tuple-element.16.kept), channel_id=1, source_target_pairs={{26,18},{63,55},{90,82},{127,119},{154,146},{191,183},{218,210},{2... | collective-permute-start | bytes 393224 | tf_op jit(solution)/shard_map/ppermute | solution.py:109
  91.3 4.6 %collective-permute-start.21 = (f32[64,512]{1,0:T(8,128)}, f32[64,512]{1,0:T(8,128)}, u32[]{:S(2)}, u32[]{:S(2)}) collective-permute-start(f32[64,512]{1,0:T(8,128)} %get-tuple-element.20), channel_id=1, source_target_pairs={{2,0},{10,8},{18,16},{26,24},{39,33},{47,41},{55,49},{63,57},{66,6... | collective-permute-start | bytes 393224 | tf_op jit(solution)/shard_map/ppermute | solution.py:109
  94.6 2.6 %collective-permute-start.13 = (f32[64,512]{1,0:T(8,128)}, f32[64,512]{1,0:T(8,128)}, u32[]{:S(2)}, u32[]{:S(2)}) collective-permute-start(f32[64,512]{1,0:T(8,128)} %hop.2.kept), channel_id=1, source_target_pairs={{18,10},{55,47},{82,74},{119,111},{146,138},{183,175},{210,202},{2... | collective-permute-start | bytes 393224 | tf_op jit(solution)/shard_map/ppermute | solution.py:109
  95.9 4.6 %collective-permute-start.22 = (f32[64,512]{1,0:T(8,128)}, f32[64,512]{1,0:T(8,128)}, u32[]{:S(2)}, u32[]{:S(2)}) collective-permute-start(f32[64,512]{1,0:T(8,128)} %get-tuple-element.21), channel_id=1, source_target_pairs={{2,4},{10,12},{18,20},{26,28},{39,37},{47,45},{55,53},{63,61},{66,... | collective-permute-start | bytes 393224 | tf_op jit(solution)/shard_map/ppermute | solution.py:109
  97.2 4.6 %collective-permute-start.23 = (f32[64,512]{1,0:T(8,128)}, f32[64,512]{1,0:T(8,128)}, u32[]{:S(2)}, u32[]{:S(2)}) collective-permute-start(f32[64,512]{1,0:T(8,128)} %get-tuple-element.22), channel_id=1, source_target_pairs={{39,35},{47,43},{55,51},{63,59},{103,99},{111,107},{119,115},{127,... | collective-permute-start | bytes 393224 | tf_op jit(solution)/shard_map/ppermute | solution.py:109
  100.5 2.6 %collective-permute-start.14 = (f32[64,512]{1,0:T(8,128)}, f32[64,512]{1,0:T(8,128)}, u32[]{:S(2)}, u32[]{:S(2)}) collective-permute-start(f32[64,512]{1,0:T(8,128)} %hop.3), channel_id=1, source_target_pairs={{10,6},{18,14},{26,22},{47,35},{55,43},{63,51},{74,70},{82,78},{90... | collective-permute-start | bytes 393224 | tf_op jit(solution)/shard_map/ppermute | solution.py:109
  101.8 2.1 %collective-permute-start.15 = (f32[64,512]{1,0:T(8,128)}, f32[64,512]{1,0:T(8,128)}, u32[]{:S(2)}, u32[]{:S(2)}) collective-permute-start(f32[64,512]{1,0:T(8,128)} %hop.3), channel_id=1, source_target_pairs={{10,0},{18,8},{26,16},{47,33},{55,41},{63,49},{74,64},{82,72},{90,... | collective-permute-start | bytes 393224 | tf_op jit(solution)/shard_map/ppermute | solution.py:109
  103.1 3.7 %copy-start.6 = (f32[512,512]{1,0:T(8,128)S(1)}, f32[512,512]{1,0:T(8,128)}, u32[]{:S(2)}) copy-start(f32[512,512]{1,0:T(8,128)} %get-tuple-element.19) | copy-start | bytes 3145732
  103.1 2.5 %collective-permute-start.16 = (f32[64,512]{1,0:T(8,128)}, f32[64,512]{1,0:T(8,128)S(1)}, u32[]{:S(2)}, u32[]{:S(2)}) collective-permute-start(f32[64,512]{1,0:T(8,128)} %hop.3), channel_id=1, source_target_pairs={{10,4},{18,12},{26,20},{47,37},{55,45},{63,53},{74,68},{82,76},{90... | collective-permute-start | bytes 393224 | tf_op jit(solution)/shard_map/ppermute | solution.py:109
  103.9 1.7 %collective-permute-start.17 = (f32[64,512]{1,0:T(8,128)}, f32[64,512]{1,0:T(8,128)S(1)}, u32[]{:S(2)}, u32[]{:S(2)}) collective-permute-start(f32[64,512]{1,0:T(8,128)} %hop.3), channel_id=1, source_target_pairs={{10,2},{18,10},{26,18},{47,39},{55,47},{63,55},{74,66},{82,74},{90... | collective-permute-start | bytes 393224 | tf_op jit(solution)/shard_map/ppermute | solution.py:109
  109.6 0.9 copy-start.7
  110.9 44.2 %collective-permute-start.24 = (f32[64,512]{1,0:T(8,128)S(1)}, f32[64,512]{1,0:T(8,128)S(1)}, u32[]{:S(2)}, u32[]{:S(2)}) collective-permute-start(f32[64,512]{1,0:T(8,128)S(1)} %get-tuple-element.32), channel_id=1, source_target_pairs={{0,1},{2,3},{4,5},{6,7},{8,9},{10,11},{12,13},{14,15},{16,17},{18,... | collective-permute-start | bytes 393224 | tf_op jit(solution)/shard_map/ppermute | solution.py:109

commit v7 on v2

--- a/solution.py
+++ b/solution.py
@@ -129,51 +129,71 @@
     return one(left[0], right[0]) + (one(left[0], right[1]) + one(left[1], right[0]))
 
 
-def compose_kernel(flag, two, last, far, near, enter1, enter0, eight, m3, m2, m1, m0, r1, r0, r8, sems, out_sems):
+def compose_kernel(
+    flag, two, last, far, near, off_own, off_last, off_far, off_near, start,
+    enter1, enter0, eight, shift1, shift0, total, leaving,
+    m3, m2, m1, m0, r1, r0, r8, sems, out_sems,
+):
     def load(src, dst, k):
         return pltpu.make_async_copy(src, dst, sems.at[k])
 
     def store(src, dst, k):
         return pltpu.make_async_copy(src, dst, out_sems.at[k])
 
-    @pl.when(flag[0] == 1)
+    even = flag[0] == 1
+
+    @pl.when(even)
     def _():
         load(last, m3, 0).start()
         load(two, m1, 2).start()
 
-    @pl.when(flag[0] == 0)
+    @pl.when(jnp.logical_not(even))
     def _():
         load(two, m3, 0).start()
         load(last, m1, 2).start()
 
     load(far, m2, 1).start()
     load(near, m0, 3).start()
+    off3 = jnp.where(even, off_last[...], off_own[...])
+    off1 = jnp.where(even, off_own[...], off_last[...])
     load(last, m3, 0).wait()
     load(far, m2, 1).wait()
-    r1[...] = product(split(m3[...]), split(m2[...]))
+    weight = split(m2[...])
+    r1[...] = product(split(m3[...]), weight)
     store(r1, enter1, 0).start()
+    moved = product(split(off3), weight) + off_far[...]
+    shift1[...] = moved
     load(last, m1, 2).wait()
-    r0[...] = product(split(r1[...]), split(m1[...]))
+    weight = split(m1[...])
+    r0[...] = product(split(r1[...]), weight)
     store(r0, enter0, 1).start()
+    moved = product(split(moved), weight) + off1
+    shift0[...] = moved
     load(near, m0, 3).wait()
-    r8[...] = product(split(r0[...]), split(m0[...]))
+    weight = split(m0[...])
+    r8[...] = product(split(r0[...]), weight)
     store(r8, eight, 2).start()
+    moved = product(split(moved), weight) + off_near[...]
+    total[...] = moved
+    leaving[...] = product(split(start[...]), split(r8[...])) + moved
     store(r1, enter1, 0).wait()
     store(r0, enter0, 1).wait()
     store(r8, eight, 2).wait()
 
 
-def compose(even, two, last, far, near):
+def compose(even, maps, rows):
     shape = (TEAM_STATES, TEAM_STATES)
+    small = (COLS, TEAM_STATES)
+    spaces = [pl.BlockSpec(memory_space=pl.ANY)] * 4 + [pl.BlockSpec(memory_space=pltpu.VMEM)] * 5
     return pl.pallas_call(
         compose_kernel,
-        out_shape=[jax.ShapeDtypeStruct(shape, jnp.float32)] * 3,
-        in_specs=[pl.BlockSpec(memory_space=pltpu.SMEM)] + [pl.BlockSpec(memory_space=pl.ANY)] * 4,
-        out_specs=[pl.BlockSpec(memory_space=pl.ANY)] * 3,
+        out_shape=[jax.ShapeDtypeStruct(shape, jnp.float32)] * 3 + [jax.ShapeDtypeStruct(small, jnp.float32)] * 4,
+        in_specs=[pl.BlockSpec(memory_space=pltpu.SMEM)] + spaces,
+        out_specs=[pl.BlockSpec(memory_space=pl.ANY)] * 3 + [pl.BlockSpec(memory_space=pltpu.VMEM)] * 4,
         scratch_shapes=[pltpu.VMEM(shape, jnp.float32)] * 7
         + [pltpu.SemaphoreType.DMA((4,)), pltpu.SemaphoreType.DMA((3,))],
         name="compose",
-    )(even.astype(jnp.int32)[None], two, last, far, near)
+    )(even.astype(jnp.int32)[None], *maps, *rows)
 
 
 def landmark_kernel(got, part):
@@ -228,7 +248,7 @@
     two_last = send(passing, FAR_IN)
 
     owner = jnp.arange(TEAM_STATES)[None, :] // STATES == jnp.arange(ROBOTS)[:, None]
-    spread = jnp.where(owner, obs_gain[0][None, :], 0.0)
+    spread = lax.optimization_barrier(jnp.where(owner, obs_gain[0][None, :], 0.0))
     driven = cot + jnp.einsum("rc,rn->cn", unfold(injected), spread, precision=HIGH)
     other_driven = send(driven, OTHER_PAIRS)
     own_driven = send(driven, WORKER_PAIR)
@@ -242,20 +262,13 @@
     off_far = send(offset, FAR_IN)
     off_near = send(offset, NEAR_IN)
 
-    map1 = pick(two, two_last)
-    enter1, enter0, eight = compose(even, two, two_last, two_far, two_near)
-    eight, enter0, enter1, off_last, off_far, off_near = lax.optimization_barrier(
-        (eight, enter0, enter1, off_last, off_far, off_near)
+    own_later, own_offset = lax.optimization_barrier(compose_driven(own_driven))
+    enter1, enter0, eight, shift1, shift0, total, leaving = compose(
+        even, (two, two_last, two_far, two_near), (own_offset, off_last, off_far, off_near, terminal[0])
     )
-    own_later, own_offset = compose_driven(own_driven)
     off3 = pick(off_last, own_offset)
-    off1 = pick(own_offset, off_last)
-    shift1 = matmul(off3, two_far) + off_far
-    shift0 = matmul(shift1, map1) + off1
-    total = matmul(shift0, two_near) + off_near
 
     last_ring = STEPS // RING - 1
-    leaving = matmul(terminal[0], eight) + total
     incoming = send(leaving, ring_hop(last_ring))
     map_near = send(enter0, NEAR_OUT)
     map_far = send(two, FAR_OUT_ODD)

time: 155 us -> 149 us (0.961)
  blocking collectives: 24.6 us -> 0 us
  starting transfers between devices: 41.1 us -> 53.1 us
  waiting for transfers between devices: 52.4 us -> 60.3 us
  matrix products: 18.5 us -> 12.7 us
  Pallas kernels: 8.11 us -> 10.7 us
  other arithmetic: 5.6 us -> 7.77 us
    all_to_all x1 -> x0, blocking collectives: 24.6 us -> none  [shards(): lax.all_to_all(jnp.concatenate([slices, packed], axis=1), 'team', 0, 0, t...]
    all_to_all x0 -> x1, waiting for transfers between devices: none -> 8.86 us  [shards(): lax.all_to_all(jnp.concatenate([slices, packed], axis=1), 'team', 0, 0, t...]
    all_to_all x0 -> x1, starting transfers between devices: none -> 7.23 us  [shards(): lax.all_to_all(jnp.concatenate([slices, packed], axis=1), 'team', 0, 0, t...]
    ppermute x23, waiting for transfers between devices: 49.2 us -> 43.8 us  [send(): return lax.ppermute(value, BOTH, pairs)]
    dot_general x11 -> x7, matrix products: 13.3 us -> 8.26 us  [matmul(): return jnp.dot(left, right, precision=HIGH)]
    ppermute x23, starting transfers between devices: 37.7 us -> 42.4 us  [send(): return lax.ppermute(value, BOTH, pairs)]
    all_to_all x1, waiting for transfers between devices: 3.21 us -> 7.68 us  [shards(): parts = lax.all_to_all(part, 'team', 0, 0, tiled=True)]
    pallas_call x1, Pallas kernels: 5.86 us -> 8.46 us  [compose(): pl.pallas_call(compose_kernel, out_shape=[jax.ShapeDtypeStruct(shape, jnp...]
  transfers between devices with their start and end apart: 24 -> 25, of which waited for: 4 -> 5; matrix products, arithmetic and copies ran while one was open for 5% -> 10% of each run, Pallas kernels for 5% -> 7%
where the time goes in v7:
time: 149 us; the launch traced here: 148 us
  waiting for transfers between devices  60.3 us (40%)
  starting transfers between devices  53.1 us (36%)
  matrix products  12.7 us (9%)
  Pallas kernels  10.7 us (7%)
  other arithmetic  7.77 us (5%)
  local copies, waits for them, and re-layouts  2.81 us (2%)
    ppermute x23, waiting for transfers between devices, send(): return lax.ppermute(value, BOTH, pairs)  43.8 us
    ppermute x23, starting transfers between devices, send(): return lax.ppermute(value, BOTH, pairs)  42.4 us
    all_to_all x1, waiting for transfers between devices, shards(): lax.all_to_all(jnp.concatenate([slices, packed], axis=1), 'team', 0, 0, t...  8.86 us
    pallas_call x1, Pallas kernels, compose(): pl.pallas_call(compose_kernel, out_shape=[jax.ShapeDtypeStruct(shape, jnp...  8.46 us
    dot_general x7, matrix products, matmul(): return jnp.dot(left, right, precision=HIGH)  8.26 us
    all_to_all x1, waiting for transfers between devices, shards(): parts = lax.all_to_all(part, 'team', 0, 0, tiled=True)  7.68 us
    all_to_all x1, starting transfers between devices, shards(): lax.all_to_all(jnp.concatenate([slices, packed], axis=1), 'team', 0, 0, t...  7.23 us
    all_to_all x1, starting transfers between devices, shards(): parts = lax.all_to_all(part, 'team', 0, 0, tiled=True)  3.41 us
  transfers between devices with their start and end apart: 25, of which 5 were waited for; matrix products, arithmetic and copies ran while one was open for 10% of the time, Pallas kernels for 7%

profile of v7, /device:TPU:1, one launch (start us, length us, event | category | flops | bytes accessed | tf_op | source)
XLA Modules:
  0.0 148.4 jit_solution(185040752035688216)
XLA Ops:
  0.6 5.0 %collective-permute-start = (f32[512,512]{1,0:T(8,128)}, f32[512,512]{1,0:T(8,128)S(1)}, u32[]{:S(2)}, u32[]{:S(2)}) collective-permute-start(f32[512,512]{1,0:T(8,128)} %bitcast.51), channel_id=1, source_target_pairs={{1,0},{3,2},{5,4},{7,6},{9,8},{11,10},{13,12},{15,14},{17,16},{19,... | collective-permute-start | bytes 3145736 | tf_op jit(solution)/shard_map/ppermute | solution.py:109
  5.7 1.0 convert_bitcast_fusion
  7.5 0.8 pad_maximum_fusion
  8.2 7.2 %all-to-all-start = ((f32[16,48,128]{2,1,0:T(8,128)}), f32[16,48,128]{2,1,0:T(8,128)}, u32[]{:S(2)}, u32[]{:S(2)}) async-start(f32[16,48,128]{2,1,0:T(8,128)} %pad_maximum_fusion), calls=%async_computation | async-start | bytes 786432 | tf_op jit(solution)/shard_map/all_to_all | solution.py:233
  15.5 2.2 %collective-permute-done = f32[512,512]{1,0:T(8,128)S(1)} collective-permute-done((f32[512,512]{1,0:T(8,128)}, f32[512,512]{1,0:T(8,128)S(1)}, u32[]{:S(2)}, u32[]{:S(2)}) %collective-permute-start) | collective-permute-done | bytes 1048608 | tf_op jit(solution)/shard_map/ppermute | solution.py:109
  17.6 1.9 %fusion.3.two = f32[512,512]{1,0:T(8,128)S(1)} fusion(f32[512,512]{1,0:T(8,128)S(1)} %collective-permute-done, pred[]{:T(512)S(6)} %eq.48, f32[1,1,512,512]{3,2,1,0:T(8,128)S(1)} %copy-done.1), kind=kOutput, calls=%fused_computation.15 | convolution fusion | flops 1611137024 | bytes 3145729 | tf_op jit(solution)/shard_map/dot_general | solution.py:244
  19.6 1.7 %collective-permute-start.1 = (f32[512,512]{1,0:T(8,128)S(1)}, f32[512,512]{1,0:T(8,128)}, u32[]{:S(2)}, u32[]{:S(2)}) collective-permute-start(f32[512,512]{1,0:T(8,128)S(1)} %fusion.3.two), channel_id=1, source_target_pairs={{6,4},{14,12},{22,20},{30,28},{35,37},{43,45},{51,53},{59,61},{70,... | collective-permute-start | bytes 3145736 | tf_op jit(solution)/shard_map/ppermute | solution.py:109
  21.2 8.9 %all-to-all-done.got = f32[16,48,128]{2,1,0:T(8,128)} async-done(((f32[16,48,128]{2,1,0:T(8,128)}), f32[16,48,128]{2,1,0:T(8,128)}, u32[]{:S(2)}, u32[]{:S(2)}) %all-to-all-start) | async-done | bytes 393248 | tf_op jit(solution)/shard_map/all_to_all | solution.py:233
  30.1 2.2 %landmark.1 = f32[16,16,128]{2,1,0:T(8,128)} custom-call(f32[16,48,128]{2,1,0:T(8,128)} %all-to-all-done.got), custom_call_target="tpu_custom_call" | custom-call | tf_op jit(solution)/shard_map/landmark/pallas_call | solution.py:234
  32.3 3.4 %all-to-all-start.1 = ((f32[16,16,128]{2,1,0:T(8,128)}), f32[16,16,128]{2,1,0:T(8,128)S(1)}, u32[]{:S(2)}, u32[]{:S(2)}) async-start(f32[16,16,128]{2,1,0:T(8,128)} %landmark.1), calls=%async_computation.1 | async-start | bytes 262144 | tf_op jit(solution)/shard_map/all_to_all | solution.py:239
  35.8 0.7 copy-done.15
  36.4 7.7 %all-to-all-done.1 = f32[16,16,128]{2,1,0:T(8,128)S(1)} async-done(((f32[16,16,128]{2,1,0:T(8,128)}), f32[16,16,128]{2,1,0:T(8,128)S(1)}, u32[]{:S(2)}, u32[]{:S(2)}) %all-to-all-start.1) | async-done | bytes 131104 | tf_op jit(solution)/shard_map/all_to_all | solution.py:239
  44.2 1.7 %collective-permute-start.3 = (f32[512,512]{1,0:T(8,128)S(1)}, f32[512,512]{1,0:T(8,128)}, u32[]{:S(2)}, u32[]{:S(2)}) collective-permute-start(f32[512,512]{1,0:T(8,128)S(1)} %fusion.3.two), channel_id=1, source_target_pairs={{4,2},{12,10},{20,18},{28,26},{37,39},{45,47},{53,55},{61,63},{68,... | collective-permute-start | bytes 3145736 | tf_op jit(solution)/shard_map/ppermute | solution.py:109
  45.9 1.6 %collective-permute-start.4 = (f32[512,512]{1,0:T(8,128)S(1)}, f32[512,512]{1,0:T(8,128)}, u32[]{:S(2)}, u32[]{:S(2)}) collective-permute-start(f32[512,512]{1,0:T(8,128)S(1)} %fusion.3.two), channel_id=1, source_target_pairs={{0,2},{8,10},{16,18},{24,26},{33,39},{41,47},{49,55},{57,63},{64,6... | collective-permute-start | bytes 3145736 | tf_op jit(solution)/shard_map/ppermute | solution.py:109
  47.6 1.7 %collective-permute-start.2 = (f32[512,512]{1,0:T(8,128)}, f32[512,512]{1,0:T(8,128)}, u32[]{:S(2)}, u32[]{:S(2)}) collective-permute-start(f32[512,512]{1,0:T(8,128)} %collective-permute-done.1), channel_id=1, source_target_pairs={{4,2},{12,10},{20,18},{28,26},{37,39},{45,47},{53,55},{61,63},{68,... | collective-permute-start | bytes 3145736 | tf_op jit(solution)/shard_map/ppermute | solution.py:109
  49.2 1.2 convolution_add_fusion.7
  50.4 11.7 %collective-permute-start.6 = (f32[64,512]{1,0:T(8,128)S(1)}, f32[64,512]{1,0:T(8,128)S(1)}, u32[]{:S(2)}, u32[]{:S(2)}) collective-permute-start(f32[64,512]{1,0:T(8,128)S(1)} %convolution_add_fusion.7), channel_id=1, source_target_pairs={{1,0},{5,4},{7,6},{9,8},{13,12},{15,14},{17,16},{21,20},{23,22},{2... | collective-permute-start | bytes 393224 | tf_op jit(solution)/shard_map/ppermute | solution.py:109
  62.1 0.7 collective-permute-start.5
  62.8 2.1 %collective-permute-done.6 = f32[64,512]{1,0:T(8,128)S(1)} collective-permute-done((f32[64,512]{1,0:T(8,128)S(1)}, f32[64,512]{1,0:T(8,128)S(1)}, u32[]{:S(2)}, u32[]{:S(2)}) %collective-permute-start.6) | collective-permute-done | bytes 131104 | tf_op jit(solution)/shard_map/ppermute | solution.py:109
  65.5 0.7 collective-permute-start.7
  66.1 0.7 collective-permute-start.8
  66.8 1.1 convolution_add_fusion.6.off_own
  67.9 0.7 collective-permute-start.9
  68.6 0.7 broadcast_select_fusion.7
  69.3 1.7 %collective-permute-start.17 = (f32[512,512]{1,0:T(8,128)S(1)}, f32[512,512]{1,0:T(8,128)}, u32[]{:S(2)}, u32[]{:S(2)}) collective-permute-start(f32[512,512]{1,0:T(8,128)S(1)} %fusion.3.two), channel_id=1, source_target_pairs={{39,37},{47,45},{55,53},{63,61},{103,101},{111,109},{119,117},{127... | collective-permute-start | bytes 3145736 | tf_op jit(solution)/shard_map/ppermute | solution.py:109
  71.0 0.6 copy-done.13
  71.6 8.5 %compose.1 = (f32[512,512]{1,0:T(8,128)}, f32[512,512]{1,0:T(8,128)}, f32[512,512]{1,0:T(8,128)}, f32[64,512]{1,0:T(8,128)}, f32[64,512]{1,0:T(8,128)}, /*index=5*/f32[64,512]{1,0:T(8,128)}, f32[64,512]{1,0:T(8,128)}) custom-call(s32[1]{0:T(128)} %bitcast.flag, f32[512,512]{1,0:T(8,128)} %copy-done.2, f32[512,512]{1,0:T(8,128)} %collective-permute-done.2.last, ...), custom_call_target="tpu_custom_call" | custom-call | tf_op jit(solution)/shard_map/compose/pallas_call | solution.py:188
  80.1 0.8 collective-permute-start.10
  80.9 0.7 broadcast_select_fusion.5
  81.6 1.3 collective-permute-start.20
  82.9 1.7 %collective-permute-start.16 = (f32[512,512]{1,0:T(8,128)}, f32[512,512]{1,0:T(8,128)}, u32[]{:S(2)}, u32[]{:S(2)}) collective-permute-start(f32[512,512]{1,0:T(8,128)} %get-tuple-element.17), channel_id=1, source_target_pairs={{2,0},{10,8},{18,16},{26,24},{39,33},{47,41},{55,49},{63,57},{66,6... | collective-permute-start | bytes 3145736 | tf_op jit(solution)/shard_map/ppermute | solution.py:109
  84.5 1.7 %collective-permute-start.18 = (f32[512,512]{1,0:T(8,128)}, f32[512,512]{1,0:T(8,128)}, u32[]{:S(2)}, u32[]{:S(2)}) collective-permute-start(f32[512,512]{1,0:T(8,128)} %get-tuple-element.18), channel_id=1, source_target_pairs={{39,35},{47,43},{55,51},{63,59},{103,99},{111,107},{119,115},{127,... | collective-permute-start | bytes 3145736 | tf_op jit(solution)/shard_map/ppermute | solution.py:109
  86.2 2.3 %convolution_add_fusion.4 = f32[64,512]{1,0:T(8,128)} fusion(f32[64,512]{1,0:T(8,128)S(1)} %copy-done.10, f32[64,512]{1,0:T(8,128)S(1)} %collective-permute-done.10, f32[512,512]{1,0:T(8,128)} %get-tuple-element.15), kind=kOutput, calls=%fused_computation.8 | convolution fusion | flops 100696064 | bytes 1441792 | tf_op jit(solution)/shard_map/dot_general | solution.py:22
  88.6 1.3 collective-permute-start.11
  89.9 1.3 collective-permute-start.19
  91.2 1.3 collective-permute-start.21
  92.5 2.4 %select_select_fusion.3 = f32[64,512]{1,0:T(8,128)} fusion(f32[64,512]{1,0:T(8,128)} %convolution_add_fusion.4, f32[64,512]{1,0:T(8,128)} %get-tuple-element.14, pred[]{:T(512)S(6)} %eq.54, pred[]{:T(512)S(6)} %eq.50, f32[64,512]{1,0:T(8,128)S(1)} %copy-done.11, f32[64,512]{1,0:T(8,128)} %collective-permute-done.11, f32[512,512]{1,0:T(8,128)} %get-tuple-element.15), kind=kOutput, calls=%fused_computation.23 | convolution fusion | flops 100761600 | bytes 1703938 | tf_op jit(solution)/shard_map/dot_general | solution.py:22
  94.9 1.3 collective-permute-start.14
  96.2 1.3 collective-permute-start.15
  97.6 0.8 collective-permute-start.12
  98.4 0.7 collective-permute-start.13
  99.0 1.0 select_select_fusion.2
  100.1 1.0 select_add_fusion
  101.2 2.5 %select_select_fusion = f32[512,512]{1,0:T(8,128)S(1)} fusion(f32[512,512]{1,0:T(8,128)} %collective-permute-done.16, f32[512,512]{1,0:T(8,128)S(1)} %copy-done.4, f32[512,512]{1,0:T(8,128)} %collective-permute-done.18, f32[512,512]{1,0:T(8,128)} %collective-permute-done.1, f32[512,512]{1,0:T(8,128)} %collective-permute-done.17, pred[]{:T(512)S(6)} %eq.57, ...), kind=kLoop, calls=%fused_computation.12 | loop fusion | flops 1048576 | bytes 6291459 | tf_op jit(solution)/shard_map/jit(_where)/select_n | solution.py:289
  105.1 1.3 collective-permute-start.22
  106.4 39.5 %collective-permute-done.22 = f32[64,512]{1,0:T(8,128)S(1)} collective-permute-done((f32[64,512]{1,0:T(8,128)S(1)}, f32[64,512]{1,0:T(8,128)S(1)}, u32[]{:S(2)}, u32[]{:S(2)}) %collective-permute-start.22) | collective-permute-done | bytes 131104 | tf_op jit(solution)/shard_map/ppermute | solution.py:109
  145.9 1.1 fusion.1
  147.0 1.4 fusion
  (63 shorter events, 3.1 us)
Async XLA Ops:
  0.6 146.4 %copy-start = (f32[1,1,64,512]{3,2,1,0:T(8,128)S(1)}, f32[1,1,64,512]{3,2,1,0:T(8,128)}, u32[]{:S(2)}) copy-start(f32[1,1,64,512]{3,2,1,0:T(8,128)} %param.8) | copy-start | bytes 393220
  0.6 17.0 %collective-permute-start = (f32[512,512]{1,0:T(8,128)}, f32[512,512]{1,0:T(8,128)S(1)}, u32[]{:S(2)}, u32[]{:S(2)}) collective-permute-start(f32[512,512]{1,0:T(8,128)} %bitcast.51), channel_id=1, source_target_pairs={{1,0},{3,2},{5,4},{7,6},{9,8},{11,10},{13,12},{15,14},{17,16},{19,... | collective-permute-start | bytes 3145736 | tf_op jit(solution)/shard_map/ppermute | solution.py:109
  6.6 0.7 copy-start.14
  6.7 10.9 %copy-start.1 = (f32[1,1,512,512]{3,2,1,0:T(8,128)S(1)}, f32[1,1,512,512]{3,2,1,0:T(8,128)}, u32[]{:S(2)}) copy-start(f32[1,1,512,512]{3,2,1,0:T(8,128)} %param.7) | copy-start | bytes 3145732
  8.2 21.8 %all-to-all-start = ((f32[16,48,128]{2,1,0:T(8,128)}), f32[16,48,128]{2,1,0:T(8,128)}, u32[]{:S(2)}, u32[]{:S(2)}) async-start(f32[16,48,128]{2,1,0:T(8,128)} %pad_maximum_fusion), calls=%async_computation | async-start | bytes 786432 | tf_op jit(solution)/shard_map/all_to_all | solution.py:233
  19.6 49.7 %copy-start.2 = (f32[512,512]{1,0:T(8,128)}, f32[512,512]{1,0:T(8,128)S(1)}, u32[]{:S(2)}) copy-start(f32[512,512]{1,0:T(8,128)S(1)} %fusion.3.two) | copy-start | bytes 3145732
  19.6 28.0 %collective-permute-start.1 = (f32[512,512]{1,0:T(8,128)S(1)}, f32[512,512]{1,0:T(8,128)}, u32[]{:S(2)}, u32[]{:S(2)}) collective-permute-start(f32[512,512]{1,0:T(8,128)S(1)} %fusion.3.two), channel_id=1, source_target_pairs={{6,4},{14,12},{22,20},{30,28},{35,37},{43,45},{51,53},{59,61},{70,... | collective-permute-start | bytes 3145736 | tf_op jit(solution)/shard_map/ppermute | solution.py:109
  32.3 11.8 %all-to-all-start.1 = ((f32[16,16,128]{2,1,0:T(8,128)}), f32[16,16,128]{2,1,0:T(8,128)S(1)}, u32[]{:S(2)}, u32[]{:S(2)}) async-start(f32[16,16,128]{2,1,0:T(8,128)} %landmark.1), calls=%async_computation.1 | async-start | bytes 262144 | tf_op jit(solution)/shard_map/all_to_all | solution.py:239
  35.7 0.7 copy-start.15
  44.2 26.7 %collective-permute-start.3 = (f32[512,512]{1,0:T(8,128)S(1)}, f32[512,512]{1,0:T(8,128)}, u32[]{:S(2)}, u32[]{:S(2)}) collective-permute-start(f32[512,512]{1,0:T(8,128)S(1)} %fusion.3.two), channel_id=1, source_target_pairs={{4,2},{12,10},{20,18},{28,26},{37,39},{45,47},{53,55},{61,63},{68,... | collective-permute-start | bytes 3145736 | tf_op jit(solution)/shard_map/ppermute | solution.py:109
  45.9 25.0 %collective-permute-start.4 = (f32[512,512]{1,0:T(8,128)S(1)}, f32[512,512]{1,0:T(8,128)}, u32[]{:S(2)}, u32[]{:S(2)}) collective-permute-start(f32[512,512]{1,0:T(8,128)S(1)} %fusion.3.two), channel_id=1, source_target_pairs={{0,2},{8,10},{16,18},{24,26},{33,39},{41,47},{49,55},{57,63},{64,6... | collective-permute-start | bytes 3145736 | tf_op jit(solution)/shard_map/ppermute | solution.py:109
  47.6 23.4 %collective-permute-start.2 = (f32[512,512]{1,0:T(8,128)}, f32[512,512]{1,0:T(8,128)}, u32[]{:S(2)}, u32[]{:S(2)}) collective-permute-start(f32[512,512]{1,0:T(8,128)} %collective-permute-done.1), channel_id=1, source_target_pairs={{4,2},{12,10},{20,18},{28,26},{37,39},{45,47},{53,55},{61,63},{68,... | collective-permute-start | bytes 3145736 | tf_op jit(solution)/shard_map/ppermute | solution.py:109
  50.4 14.4 %collective-permute-start.6 = (f32[64,512]{1,0:T(8,128)S(1)}, f32[64,512]{1,0:T(8,128)S(1)}, u32[]{:S(2)}, u32[]{:S(2)}) collective-permute-start(f32[64,512]{1,0:T(8,128)S(1)} %convolution_add_fusion.7), channel_id=1, source_target_pairs={{1,0},{5,4},{7,6},{9,8},{13,12},{15,14},{17,16},{21,20},{23,22},{2... | collective-permute-start | bytes 393224 | tf_op jit(solution)/shard_map/ppermute | solution.py:109
  62.1 4.1 %collective-permute-start.5 = (f32[64,512]{1,0:T(8,128)S(1)}, f32[64,512]{1,0:T(8,128)S(1)}, u32[]{:S(2)}, u32[]{:S(2)}) collective-permute-start(f32[64,512]{1,0:T(8,128)S(1)} %convolution_add_fusion.7), channel_id=1, source_target_pairs={{3,2},{11,10},{19,18},{27,26},{38,39},{46,47},{54,55},{62,63},{67,... | collective-permute-start | bytes 393224 | tf_op jit(solution)/shard_map/ppermute | solution.py:109
  64.8 0.7 copy-start.5
  65.5 2.5 %collective-permute-start.7 = (f32[64,512]{1,0:T(8,128)S(1)}, f32[64,512]{1,0:T(8,128)S(1)}, u32[]{:S(2)}, u32[]{:S(2)}) collective-permute-start(f32[64,512]{1,0:T(8,128)S(1)} %convolution_add_fusion.5), channel_id=1, source_target_pairs={{6,2},{14,10},{22,18},{30,26},{35,39},{43,47},{51,55},{59,63},{70,... | collective-permute-start | bytes 393224 | tf_op jit(solution)/shard_map/ppermute | solution.py:109
  66.1 3.1 %collective-permute-start.8 = (f32[64,512]{1,0:T(8,128)S(1)}, f32[64,512]{1,0:T(8,128)S(1)}, u32[]{:S(2)}, u32[]{:S(2)}) collective-permute-start(f32[64,512]{1,0:T(8,128)S(1)} %convolution_add_fusion.5), channel_id=1, source_target_pairs={{4,2},{12,10},{20,18},{28,26},{37,39},{45,47},{53,55},{61,63},{68,... | collective-permute-start | bytes 393224 | tf_op jit(solution)/shard_map/ppermute | solution.py:109
  67.9 1.3 copy-start.8
  67.9 3.0 %collective-permute-start.9 = (f32[64,512]{1,0:T(8,128)S(1)}, f32[64,512]{1,0:T(8,128)S(1)}, u32[]{:S(2)}, u32[]{:S(2)}) collective-permute-start(f32[64,512]{1,0:T(8,128)S(1)} %convolution_add_fusion.5), channel_id=1, source_target_pairs={{0,2},{8,10},{16,18},{24,26},{33,39},{41,47},{49,55},{57,63},{64,6... | collective-permute-start | bytes 393224 | tf_op jit(solution)/shard_map/ppermute | solution.py:109
  69.3 1.7 %copy-start.12 = (f32[64,512]{1,0:T(8,128)}, f32[64,512]{1,0:T(8,128)S(1)}, u32[]{:S(2)}) copy-start(f32[64,512]{1,0:T(8,128)S(1)} %collective-permute-done.8.off_far) | copy-start | bytes 393220
  69.3 31.8 %collective-permute-start.17 = (f32[512,512]{1,0:T(8,128)S(1)}, f32[512,512]{1,0:T(8,128)}, u32[]{:S(2)}, u32[]{:S(2)}) collective-permute-start(f32[512,512]{1,0:T(8,128)S(1)} %fusion.3.two), channel_id=1, source_target_pairs={{39,37},{47,45},{55,53},{63,61},{103,101},{111,109},{119,117},{127... | collective-permute-start | bytes 3145736 | tf_op jit(solution)/shard_map/ppermute | solution.py:109
  70.9 0.7 copy-start.13
  71.6 9.3 %copy-start.3 = (f32[64,512]{1,0:T(8,128)S(1)}, f32[64,512]{1,0:T(8,128)}, u32[]{:S(2)}) copy-start(f32[64,512]{1,0:T(8,128)} %convolution_add_fusion.6.off_own) | copy-start | bytes 393220
  80.1 6.1 %copy-start.10 = (f32[64,512]{1,0:T(8,128)S(1)}, f32[64,512]{1,0:T(8,128)}, u32[]{:S(2)}) copy-start(f32[64,512]{1,0:T(8,128)} %get-tuple-element.16) | copy-start | bytes 393220
  80.1 6.1 %collective-permute-start.10 = (f32[64,512]{1,0:T(8,128)}, f32[64,512]{1,0:T(8,128)S(1)}, u32[]{:S(2)}, u32[]{:S(2)}) collective-permute-start(f32[64,512]{1,0:T(8,128)} %get-tuple-element.14), channel_id=1, source_target_pairs={{26,18},{63,55},{90,82},{127,119},{154,146},{191,183},{218,210},{2... | collective-permute-start | bytes 393224 | tf_op jit(solution)/shard_map/ppermute | solution.py:109
  81.6 8.3 %collective-permute-start.20 = (f32[64,512]{1,0:T(8,128)}, f32[64,512]{1,0:T(8,128)}, u32[]{:S(2)}, u32[]{:S(2)}) collective-permute-start(f32[64,512]{1,0:T(8,128)} %broadcast_select_fusion.5), channel_id=1, source_target_pairs={{2,4},{10,12},{18,20},{26,28},{39,37},{47,45},{55,53},{63,61},{66,... | collective-permute-start | bytes 393224 | tf_op jit(solution)/shard_map/ppermute | solution.py:109
  82.9 18.2 %collective-permute-start.16 = (f32[512,512]{1,0:T(8,128)}, f32[512,512]{1,0:T(8,128)}, u32[]{:S(2)}, u32[]{:S(2)}) collective-permute-start(f32[512,512]{1,0:T(8,128)} %get-tuple-element.17), channel_id=1, source_target_pairs={{2,0},{10,8},{18,16},{26,24},{39,33},{47,41},{55,49},{63,57},{66,6... | collective-permute-start | bytes 3145736 | tf_op jit(solution)/shard_map/ppermute | solution.py:109
  84.5 16.6 %collective-permute-start.18 = (f32[512,512]{1,0:T(8,128)}, f32[512,512]{1,0:T(8,128)}, u32[]{:S(2)}, u32[]{:S(2)}) collective-permute-start(f32[512,512]{1,0:T(8,128)} %get-tuple-element.18), channel_id=1, source_target_pairs={{39,35},{47,43},{55,51},{63,59},{103,99},{111,107},{119,115},{127,... | collective-permute-start | bytes 3145736 | tf_op jit(solution)/shard_map/ppermute | solution.py:109
  86.2 6.3 %copy-start.11 = (f32[64,512]{1,0:T(8,128)S(1)}, f32[64,512]{1,0:T(8,128)}, u32[]{:S(2)}) copy-start(f32[64,512]{1,0:T(8,128)} %get-tuple-element.16) | copy-start | bytes 393220
  88.6 2.6 %collective-permute-start.11 = (f32[64,512]{1,0:T(8,128)}, f32[64,512]{1,0:T(8,128)}, u32[]{:S(2)}, u32[]{:S(2)}) collective-permute-start(f32[64,512]{1,0:T(8,128)} %convolution_add_fusion.4), channel_id=1, source_target_pairs={{18,10},{55,47},{82,74},{119,111},{146,138},{183,175},{210,202},{2... | collective-permute-start | bytes 393224 | tf_op jit(solution)/shard_map/ppermute | solution.py:109
  89.9 5.1 %collective-permute-start.19 = (f32[64,512]{1,0:T(8,128)}, f32[64,512]{1,0:T(8,128)}, u32[]{:S(2)}, u32[]{:S(2)}) collective-permute-start(f32[64,512]{1,0:T(8,128)} %get-tuple-element.19), channel_id=1, source_target_pairs={{2,0},{10,8},{18,16},{26,24},{39,33},{47,41},{55,49},{63,57},{66,6... | collective-permute-start | bytes 393224 | tf_op jit(solution)/shard_map/ppermute | solution.py:109
  91.2 5.0 %collective-permute-start.21 = (f32[64,512]{1,0:T(8,128)}, f32[64,512]{1,0:T(8,128)}, u32[]{:S(2)}, u32[]{:S(2)}) collective-permute-start(f32[64,512]{1,0:T(8,128)} %get-tuple-element.20), channel_id=1, source_target_pairs={{39,35},{47,43},{55,51},{63,59},{103,99},{111,107},{119,115},{127,... | collective-permute-start | bytes 393224 | tf_op jit(solution)/shard_map/ppermute | solution.py:109
  94.9 2.6 %collective-permute-start.14 = (f32[64,512]{1,0:T(8,128)}, f32[64,512]{1,0:T(8,128)}, u32[]{:S(2)}, u32[]{:S(2)}) collective-permute-start(f32[64,512]{1,0:T(8,128)} %select_select_fusion.3), channel_id=1, source_target_pairs={{10,4},{18,12},{26,20},{47,37},{55,45},{63,53},{74,68},{82,76},{90... | collective-permute-start | bytes 393224 | tf_op jit(solution)/shard_map/ppermute | solution.py:109
  96.2 2.1 %collective-permute-start.15 = (f32[64,512]{1,0:T(8,128)}, f32[64,512]{1,0:T(8,128)}, u32[]{:S(2)}, u32[]{:S(2)}) collective-permute-start(f32[64,512]{1,0:T(8,128)} %select_select_fusion.3), channel_id=1, source_target_pairs={{10,2},{18,10},{26,18},{47,39},{55,47},{63,55},{74,66},{82,74},{90... | collective-permute-start | bytes 393224 | tf_op jit(solution)/shard_map/ppermute | solution.py:109
  97.5 2.5 %copy-start.9 = (f32[1,64,512]{2,1,0:T(8,128)S(1)}, f32[1,64,512]{2,1,0:T(8,128)}, u32[]{:S(2)}) copy-start(f32[1,64,512]{2,1,0:T(8,128)} %param.10) | copy-start | bytes 393220
  97.5 3.6 %copy-start.4 = (f32[512,512]{1,0:T(8,128)S(1)}, f32[512,512]{1,0:T(8,128)}, u32[]{:S(2)}) copy-start(f32[512,512]{1,0:T(8,128)} %get-tuple-element.18) | copy-start | bytes 3145732
  97.6 2.5 %collective-permute-start.12 = (f32[64,512]{1,0:T(8,128)}, f32[64,512]{1,0:T(8,128)S(1)}, u32[]{:S(2)}, u32[]{:S(2)}) collective-permute-start(f32[64,512]{1,0:T(8,128)} %select_select_fusion.3), channel_id=1, source_target_pairs={{10,6},{18,14},{26,22},{47,35},{55,43},{63,51},{74,70},{82,78},{90... | collective-permute-start | bytes 393224 | tf_op jit(solution)/shard_map/ppermute | solution.py:109
  98.4 1.7 %collective-permute-start.13 = (f32[64,512]{1,0:T(8,128)}, f32[64,512]{1,0:T(8,128)S(1)}, u32[]{:S(2)}, u32[]{:S(2)}) collective-permute-start(f32[64,512]{1,0:T(8,128)} %select_select_fusion.3), channel_id=1, source_target_pairs={{10,0},{18,8},{26,16},{47,33},{55,41},{63,49},{74,64},{82,72},{90,... | collective-permute-start | bytes 393224 | tf_op jit(solution)/shard_map/ppermute | solution.py:109
  103.7 0.9 copy-start.6
  103.7 1.0 copy-start.7
  105.1 40.8 %collective-permute-start.22 = (f32[64,512]{1,0:T(8,128)S(1)}, f32[64,512]{1,0:T(8,128)S(1)}, u32[]{:S(2)}, u32[]{:S(2)}) collective-permute-start(f32[64,512]{1,0:T(8,128)S(1)} %get-tuple-element.28), channel_id=1, source_target_pairs={{0,1},{2,3},{4,5},{6,7},{8,9},{10,11},{12,13},{14,15},{16,17},{18,... | collective-permute-start | bytes 393224 | tf_op jit(solution)/shard_map/ppermute | solution.py:109
